TPU v7x, 768 devices: a whole 4x8x12 slice. The times are simulated.
768 devices in a mesh: space: 192 (over z, y_lo, x), tm: 4 (over y_hi, core).
Axes of the slice: x: 4, y: 8 (y_hi: 2, y_lo: 4; y = y_hi * 4 + y_lo), z: 12, core: 2. Of those that a mesh axis runs over, the one named last changes fastest.
Arguments:
- eigvecs: float32 [4, 2, 3, 64, 192, 144], P('tm', None, None, None, 'space'), may hold values from -6 to 6
- gauge_links: float32 [3, 4, 2, 3, 3, 192, 144], P(None, 'tm', None, None, None, 'space'), may hold values from -4 to 4
- perambulators: bfloat16 [4, 4, 2, 4, 4, 64, 64], P('tm'), may hold values from -0.375 to 0.375
- momenta: int32 [32, 3], replicated, may hold values from -2 to 2, as said below
Outputs:
- smeared: bfloat16 [4, 2, 3, 64, 192, 144], P('tm', None, None, None, 'space')
- elementals: bfloat16 [32, 4, 2, 64, 64], P(None, 'tm')
- correlator: float32 [2, 32, 4, 4], P(None, None, 'tm')
Inputs may be any that keep to these rules, and one draw needn't show every extreme that they name: `momenta`: every row is a nonzero vector of integers.
All inputs are finite; a program needn't handle non-finite values.
Results may differ from a plain program's by a relative error of at most 0.0053.
Values may be sent and summed in bfloat16 or wider, within the bound.
No kernel may reach another device: no remote copies, remote signals or barrier semaphores. Data moves between devices by JAX's collectives and lax.ppermute only.
A program may use at most 32 MiB of HBM per device.

v0:
```python
import math

import jax
import jax.numpy as jnp
from jax import lax
from jax.sharding import PartitionSpec as P

NEV = 64
LX = 24
YB = 4


KAPPA = 0.25
op_block = 4


def shifted(value, axis, steps):
    count = lax.axis_size(axis)
    pairs = [(source, (source + steps) % count) for source in range(count)]
    return lax.ppermute(value, axis, pairs)


def padded(cells, sides, width):
    for axis, dim in sides:
        count = lax.axis_size(axis)
        head = lax.slice_in_dim(cells, 0, width, axis=dim)
        tail = lax.slice_in_dim(cells, cells.shape[dim] - width, cells.shape[dim], axis=dim)
        cells = jnp.concatenate(
            [
                lax.ppermute(tail, axis, [(i, (i + 1) % count) for i in range(count)]),
                cells,
                lax.ppermute(head, axis, [((i + 1) % count, i) for i in range(count)]),
            ],
            axis=dim,
        )
    return cells


def shift_row(lattice, stride):
    layout = lattice.shape
    planes = lattice.reshape(layout[:-1] + (layout[-1] // LX, LX))
    planes = jnp.roll(planes, -stride, axis=-1)
    return planes.reshape(layout)


def transport(one_link, vector, adjoint):
    link_re = one_link[..., 0, :, :, :, :]
    link_im = one_link[..., 1, :, :, :, :]
    vec_re = vector[..., 0, :, :, :, :]
    vec_im = vector[..., 1, :, :, :, :]
    out_re = 0.0
    out_im = 0.0
    for colour in range(3):
        if adjoint:
            factor_re = link_re[..., colour, :, None, :, :]
            factor_im = -link_im[..., colour, :, None, :, :]
        else:
            factor_re = link_re[..., :, colour, None, :, :]
            factor_im = link_im[..., :, colour, None, :, :]
        source_re = vec_re[..., colour : colour + 1, :, :, :]
        source_im = vec_im[..., colour : colour + 1, :, :, :]
        out_re = out_re + factor_re * source_re - factor_im * source_im
        out_im = out_im + factor_re * source_im + factor_im * source_re
    return jnp.stack([out_re, out_im], axis=-5)


def phases(momenta, z_index, y_start, site_count, z_total):
    site_index = jnp.arange(site_count, dtype=jnp.int32)
    x_coord = site_index % LX
    y_coord = y_start + site_index // LX
    z_coord = z_index + jnp.arange(1, dtype=jnp.int32)
    turn_x = momenta[:, 0, None] * x_coord[None] % LX
    turn_y = momenta[:, 1, None] * y_coord[None] % LX
    turn_z = momenta[:, 2, None] * z_coord[None] % z_total
    angles = (
        2.0
        * math.pi
        * (
            turn_x.astype(jnp.float32)[:, None, :] / LX
            + turn_y.astype(jnp.float32)[:, None, :] / LX
            + turn_z.astype(jnp.float32)[:, :, None] / z_total
        )
    )
    return (jnp.cos(angles), -jnp.sin(angles))


def pair_product(left, right):
    return jnp.einsum("tcazs,ptcbzs->ptab", left, right, preferred_element_type=jnp.float32)


def contract(smeared, cos_part, sin_part, norm_scale):
    smear_re = smeared[:, 0]
    smear_im = smeared[:, 1]
    wide_re = smear_re.astype(jnp.float32)
    wide_im = smear_im.astype(jnp.float32)
    cos_wide = cos_part[:, None, None, None]
    sin_wide = sin_part[:, None, None, None]
    phased_re = (wide_re[None] * cos_wide - wide_im[None] * sin_wide).astype(jnp.bfloat16)
    phased_im = (wide_re[None] * sin_wide + wide_im[None] * cos_wide).astype(jnp.bfloat16)
    elem_re = pair_product(smear_re, phased_re) + pair_product(smear_im, phased_im)
    elem_im = pair_product(smear_re, phased_im) - pair_product(smear_im, phased_re)
    return norm_scale * jnp.stack([elem_re, elem_im], axis=2)


def local(eigvecs, gauge_links, perambulators, momenta):
    spaces = lax.axis_size("space")
    z_total = spaces // YB
    site_count = eigvecs.shape[5]
    row_count = site_count // LX
    block_index = lax.axis_index("space")
    y_block = block_index % YB
    z_index = block_index // YB
    summed = (1.0 - 6.0 * KAPPA) * eigvecs
    link_x = gauge_links[0]
    forward = transport(link_x, shift_row(eigvecs, 1), False)
    behind = shift_row(transport(link_x, eigvecs, True), -1)
    summed = summed + KAPPA * (forward + behind)
    link_y = gauge_links[1]
    link_z = gauge_links[2]
    v_above, ylink_above = shifted((eigvecs, link_y[..., site_count - LX :]), "space", -YB)
    v_below, zlink_below = shifted((eigvecs, link_z), "space", YB)
    back_y = transport(link_y, eigvecs, True)
    back_above = transport(ylink_above, v_above[..., site_count - LX :], True)
    to_lower = jnp.where(y_block == 0, v_below[..., :LX], eigvecs[..., :LX])
    to_upper = jnp.where(y_block == YB - 1, back_above, back_y[..., site_count - LX :])
    payload = jnp.concatenate([to_lower, to_upper], axis=4)
    rim_rows = padded(payload, (("space", 4),), 1)
    row_below = rim_rows[:, :, :, :, 0:1]
    row_above = rim_rows[:, :, :, :, 3:4]
    forward = transport(link_y, jnp.concatenate([eigvecs[..., LX:], row_above], axis=5), False)
    behind = jnp.concatenate([row_below, back_y[..., : site_count - LX]], axis=5)
    summed = summed + KAPPA * (forward + behind)
    forward = transport(link_z, v_above, False)
    behind = transport(zlink_below, v_below, True)
    summed = summed + KAPPA * (forward + behind)
    smeared = summed.astype(jnp.bfloat16)
    op_count = momenta.shape[0]
    cos_all, sin_all = phases(momenta, z_index, y_block * row_count, site_count, z_total)
    norm_scale = 1.0 / math.sqrt(3.0 * z_total * LX * LX)
    group_count = op_count // op_block
    cos_group = cos_all.reshape((group_count, op_block) + cos_all.shape[1:])
    sin_group = sin_all.reshape((group_count, op_block) + sin_all.shape[1:])

    def per_group(phase_pair):
        return contract(smeared, phase_pair[0], phase_pair[1], norm_scale)

    partial_sums = lax.map(per_group, (cos_group, sin_group))
    partial_sums = partial_sums.reshape((op_count,) + partial_sums.shape[2:])
    raw_sums = lax.psum(partial_sums, "space")
    elementals = raw_sums.astype(jnp.bfloat16)
    pair_count = perambulators.shape[3] * perambulators.shape[4]
    item_count = op_count * pair_count
    slot_count = (item_count + spaces - 1) // spaces
    item_ids = block_index * slot_count + jnp.arange(slot_count, dtype=jnp.int32)
    is_valid = (item_ids < item_count).astype(jnp.float32)
    clipped = jnp.minimum(item_ids, item_count - 1)
    op_slots = clipped // pair_count
    pair_slots = clipped % pair_count
    owners = (op_slots[:, None] == jnp.arange(op_count, dtype=jnp.int32)[None]).astype(
        jnp.float32
    ) * is_valid[:, None]
    nearby = jnp.take(elementals, op_slots, axis=0)
    near_wide = nearby.astype(jnp.float32)
    near_re = near_wide[:, :, 0]
    near_im = near_wide[:, :, 1]
    blocks = perambulators.reshape(
        perambulators.shape[:3] + (pair_count,) + perambulators.shape[5:]
    )
    chosen = jnp.take(blocks, pair_slots, axis=3)
    high = lax.Precision.HIGHEST
    remote = jnp.take(lax.all_gather(elementals, "tm", axis=1, tiled=True), op_slots, axis=0)
    tau_re = chosen[:, :, 0]
    tau_im = chosen[:, :, 1]
    far_re = remote[:, :, 0]
    far_im = remote[:, :, 1]
    left_re = (
        jnp.einsum("tnjia,jnba->tnjib", tau_re, far_re, preferred_element_type=jnp.float32)
        + jnp.einsum("tnjia,jnba->tnjib", tau_im, far_im, preferred_element_type=jnp.float32)
    ).astype(jnp.bfloat16)
    left_im = (
        jnp.einsum("tnjia,jnba->tnjib", tau_im, far_re, preferred_element_type=jnp.float32)
        - jnp.einsum("tnjia,jnba->tnjib", tau_re, far_im, preferred_element_type=jnp.float32)
    ).astype(jnp.bfloat16)
    right_re = jnp.einsum(
        "tnjib,tnjkb->tnjik", left_re, tau_re, preferred_element_type=jnp.float32
    ) + jnp.einsum("tnjib,tnjkb->tnjik", left_im, tau_im, preferred_element_type=jnp.float32)
    right_im = jnp.einsum(
        "tnjib,tnjkb->tnjik", left_im, tau_re, preferred_element_type=jnp.float32
    ) - jnp.einsum("tnjib,tnjkb->tnjik", left_re, tau_im, preferred_element_type=jnp.float32)
    corr_re = jnp.einsum("jtab,tnjba->tnj", near_re, right_re, precision=high) - jnp.einsum(
        "jtab,tnjba->tnj", near_im, right_im, precision=high
    )
    corr_im = jnp.einsum("jtab,tnjba->tnj", near_re, right_im, precision=high) + jnp.einsum(
        "jtab,tnjba->tnj", near_im, right_re, precision=high
    )
    traces = jnp.stack([corr_re, corr_im]) / NEV
    contrib = jnp.einsum("rtnj,jp->rptn", traces, owners, precision=high)
    correlator = lax.psum(contrib, "space")
    return (smeared, elementals, correlator)


def solution(mesh):
    return jax.shard_map(
        local,
        mesh=mesh,
        in_specs=(
            P("tm", None, None, None, "space", None),
            P(None, "tm", None, None, None, "space", None),
            P("tm", None, None, None, None, None, None),
            P(),
        ),
        out_specs=(
            P("tm", None, None, None, "space", None),
            P(None, "tm", None, None, None),
            P(None, None, "tm", None),
        ),
        check_vma=False,
    )
```

profile of v0, /device:TPU:2, one launch (start us, length us, event | category | flops | bytes accessed | tf_op | source)
XLA Modules:
  0.0 1876.6 jit_solution(7922083069451363006)
XLA Ops:
  7.2 3.6 collective-permute-start
  10.9 16.1 collective-permute-start.3
  28.4 3.9 collective-permute-start.2
  32.3 1.9 collective-permute-start.5
  34.2 2.0 fusion.95
  36.2 1.2 copy.21
  43.7 1.3 copy.206
  45.1 1.3 copy.213
  46.3 1.3 copy.214
  47.6 1.3 copy.215
  48.9 1.3 copy.216
  50.1 1.3 copy.217
  51.4 1.3 copy.218
  55.0 1.4 slice_reduce_fusion.4
  56.4 1.2 fusion.87
  57.6 1.3 div.63
  59.5 1.3 mul.2642
  60.8 1.3 mul.2638
  62.9 1.7 sine_negate_fusion
  65.8 1.2 subtract_bitcast_fusion.3
  68.2 1.2 slice.429
  79.8 1.8 broadcast_select_fusion
  81.6 2.4 collective-permute-start.1
  84.0 1.5 fusion.94
  86.8 3.4 collective-permute-start.4
  90.2 1.3 slice_bitcast_fusion.9
  93.0 1.3 slice_bitcast_fusion.7
  95.2 1.6 copy.98
  96.8 1.6 copy.97
  98.4 1.6 copy.96
  100.0 1.6 copy.95
  101.5 1.6 copy.94
  103.1 1.6 copy.93
  104.7 2.1 subtract_bitcast_fusion.1
  106.8 2.3 subtract_bitcast_fusion
  109.1 1.8 fusion.44
  113.1 1.6 copy.82
  114.6 1.6 copy.81
  116.2 1.3 subtract_bitcast_fusion.2
  117.6 1.8 fusion.37
  120.1 21.6 %while.10 = (s32[]{:T(128)}, f32[8,4,1,2,64,64]{5,4,3,1,0,2:T(8,128)}, bf16[1,2,3,64,1,144]{5,3,2,4,1,0:T(8,128)(2,1)S(1)}, f32[8,4,1,144]{3,1,2,0:T(4,128)}, f32[8,4,1,144]{3,1,2,0:T(4,128)}, /*index=5*/s32[]{:T(128)}) while((s32[]{:T(128)}, f32[8,4,1,2,64,64]{5,4,3,1,0,2:T(8,128)}, bf16[1,2,3,64,1,144]{5,3,2,4,1,0:T(8,128)(2,1)S(1)}, ...), condition=%wide.region_1.2_spmd, body=%wide.region_0.1_spmd.sunk | while | flops 58546176 | bytes 3781717 | solution.py:147
  141.6 1103.2 %all-reduce.1 = bf16[32,1,2,64,64]{4,3,2,1,0:T(8,128)(2,1)} all-reduce(f32[32,1,2,64,64]{4,3,2,1,0:T(8,128)} %bitcast.409), channel_id=1, replica_groups=mesh['space'=192,'tm'=4] {'space'}, use_global_device_ids=true, to_apply=%region_2.3 | all-reduce | flops 262144 | bytes 1572864 | tf_op jit(solution)/shard_map/psum | solution.py:149
  1246.6 1.8 gather_fusion.2
  1249.1 66.7 %all-gather.2.cloned.1.call-done = bf16[32,4,2,64,64]{4,3,2,1,0:T(8,128)(2,1)} async-done(((bf16[32,1,2,64,64]{4,3,2,1,0:T(8,128)(2,1)}), bf16[32,4,2,64,64]{4,3,2,1,0:T(8,128)(2,1)}) %all-gather.2.cloned.1.call-update) | async-done | bytes 2097168 | tf_op jit(solution)/shard_map/all_gather | solution.py:171
  1315.8 2.8 gather_fusion
  1321.9 1.9 fusion.49
  1323.8 1.7 fusion.51
  1327.9 541.9 %psum.15 = f32[2,32,1,4]{1,3,0,2:T(4,128)} all-reduce(f32[2,32,1,4]{1,3,0,2:T(4,128)S(1)} %convolution_bitcast_fusion.4), channel_id=1, replica_groups=mesh['space'=192,'tm'=4] {'space'}, use_global_device_ids=true, to_apply=%region_3.4 | all-reduce | flops 256 | bytes 2048 | tf_op jit(solution)/shard_map/psum | solution.py:198
  (267 shorter events, 59.6 us)
Async XLA Ops:
  7.2 1237.7 %copy-start = (bf16[1,4,2,4,4,64,64]{6,5,4,3,2,1,0:T(8,128)(2,1)S(1)}, bf16[1,4,2,4,4,64,64]{6,5,4,3,2,1,0:T(8,128)(2,1)}, u32[]{:S(2)}) copy-start(bf16[1,4,2,4,4,64,64]{6,5,4,3,2,1,0:T(8,128)(2,1)} %param.8) | copy-start | bytes 3145732
  7.2 1308.6 %all-gather.2.cloned.1.call-start = ((), (), s32[]{:S(2)}) async-start(), calls=%async_computation | async-start | bytes 5242880 | tf_op jit(solution)/shard_map/all_gather | solution.py:171
  7.2 72.5 %collective-permute-start = (f32[1,2,3,64,1,144]{5,4,3,2,1,0:T(1,128)}, f32[1,2,3,64,1,144]{5,4,3,2,1,0:T(1,128)}, u32[]{:S(2)}, u32[]{:S(2)}) collective-permute-start(f32[1,2,3,64,1,144]{5,4,3,2,1,0:T(1,128)} %param.6), channel_id=1, source_target_pairs={{0,16},{4,20},{8,24},{12,28},{16,32},{20,36},{24,40},{28,44},{32,4... | collective-permute-start | bytes 663560 | tf_op jit(solution)/shard_map/ppermute | solution.py:20
  10.9 73.2 %collective-permute-start.3 = (f32[1,2,3,64,1,144]{5,4,3,2,1,0:T(1,128)}, f32[1,2,3,64,1,144]{5,4,3,2,1,0:T(1,128)}, u32[]{:S(2)}, u32[]{:S(2)}) collective-permute-start(f32[1,2,3,64,1,144]{5,4,3,2,1,0:T(1,128)} %param.6), channel_id=1, source_target_pairs={{0,752},{4,756},{8,760},{12,764},{16,0},{20,4},{24,8},{28,12},{32,... | collective-permute-start | bytes 663560 | tf_op jit(solution)/shard_map/ppermute | solution.py:20
  28.4 47.0 %collective-permute-start.2 = (f32[1,2,3,3,1,24]{5,4,3,2,1,0:T(1,128)}, f32[1,2,3,3,1,24]{5,4,3,2,1,0:T(1,128)}, u32[]{:S(2)}, u32[]{:S(2)}) collective-permute-start(f32[1,2,3,3,1,24]{5,4,3,2,1,0:T(1,128)} %slice.566), channel_id=1, source_target_pairs={{0,752},{4,756},{8,760},{12,764},{16,0},{20,4},{24,8},{28,12},{32,... | collective-permute-start | bytes 5192 | tf_op jit(solution)/shard_map/ppermute | solution.py:20
  32.3 43.9 %collective-permute-start.5 = (f32[1,2,3,3,1,144]{5,4,3,2,1,0:T(1,128)S(1)}, f32[1,2,3,3,1,144]{5,4,3,2,1,0:T(1,128)S(1)}, u32[]{:S(2)}, u32[]{:S(2)}) collective-permute-start(f32[1,2,3,3,1,144]{5,4,3,2,1,0:T(1,128)S(1)} %get-tuple-element.139), channel_id=1, source_target_pairs={{0,16},{4,20},{8,24},{12,28},{16,32},{20,36},{24,40},{28,44},{32,4... | collective-permute-start | bytes 31112 | tf_op jit(solution)/shard_map/ppermute | solution.py:20
  62.1 0.7 copy-start.18
  62.1 0.7 copy-start.19
  62.1 0.7 copy-start.20
  62.2 0.7 copy-start.33
  62.2 2.4 copy-start.13
  62.2 3.6 copy-start.11
  62.2 3.6 copy-start.12
  62.2 3.6 copy-start.14
  62.2 3.6 copy-start.15
  62.2 3.6 copy-start.16
  62.2 3.6 copy-start.17
  62.8 5.4 copy-start.1
  62.8 6.6 copy-start.23
  62.9 6.6 copy-start.26
  64.5 4.9 copy-start.22
  64.5 5.5 copy-start.25
  64.5 6.1 copy-start.21
  64.5 6.7 copy-start.24
  64.5 7.3 copy-start.30
  64.6 7.8 copy-start.32
  64.6 8.4 copy-start.28
  64.6 9.0 copy-start.31
  64.6 9.6 copy-start.27
  64.6 10.2 copy-start.29
  81.6 27.5 %collective-permute-start.1 = (f32[1,2,3,64,1,24]{5,4,3,2,1,0:T(1,128)}, f32[1,2,3,64,1,24]{5,4,3,2,1,0:T(1,128)}, u32[]{:S(2)}, u32[]{:S(2)}) collective-permute-start(f32[1,2,3,64,1,24]{5,4,3,2,1,0:T(1,128)} %broadcast_select_fusion), channel_id=1, source_target_pairs={{4,0},{8,4},{12,8},{16,12},{20,16},{24,20},{28,24},{32,28},{36,32}... | collective-permute-start | bytes 110600 | tf_op jit(solution)/shard_map/ppermute | solution.py:32
  86.8 30.8 %collective-permute-start.4 = (f32[1,2,3,64,1,24]{3,5,2,1,4,0:T(8,128)}, f32[1,2,3,64,1,24]{3,5,2,1,4,0:T(8,128)}, u32[]{:S(2)}, u32[]{:S(2)}) collective-permute-start(f32[1,2,3,64,1,24]{3,5,2,1,4,0:T(8,128)} %maximum_select_fusion), channel_id=1, source_target_pairs={{0,4},{4,8},{8,12},{12,16},{16,20},{20,24},{24,28},{28,32},{32,36}... | collective-permute-start | bytes 110600 | tf_op jit(solution)/shard_map/ppermute | solution.py:30
  93.0 16.1 copy-start.5
  106.8 9.4 copy-start.7
  106.8 9.4 copy-start.8
  106.8 9.4 copy-start.9
  106.8 9.4 copy-start.10
  106.8 10.8 copy-start.4
  119.4 0.7 copy-start.2
  1244.8 0.9 copy-start.3
  1321.7 4.8 copy-start.6
Sparse Core Ops, SparseCore 0:
  1245.0 70.7 all-gather.1
where the time goes:
time: 1880 us
  blocking collectives  1650 us (88%)
  local copies, waits for them, and re-layouts  80.9 us (4%)
  waiting for transfers between devices  66.7 us (4%)
  starting transfers between devices  31.4 us (2%)
  other arithmetic  21.1 us (1%)
    psum x1, blocking collectives, local(): raw_sums = lax.psum(partial_sums, 'space')  1100 us
    psum x1, blocking collectives, local(): correlator = lax.psum(contrib, 'space')  542 us
    all_gather x1, waiting for transfers between devices, local(): lax.all_gather(elementals, 'tm', axis=1, tiled=True)  66.7 us
  transfers between devices with their start and end apart: 7, of which 1 were waited for; matrix products, arithmetic and copies ran while one was open for 4% of the time, Pallas kernels for 0%

commit v1 on v0

v1 whole, which is shorter than its diff:
```python
import math

import jax
import jax.numpy as jnp
from jax import lax
from jax.experimental import pallas as pl
from jax.experimental.pallas import tpu as pltpu
from jax.sharding import Mesh, PartitionSpec as P

NEV = 64
LX = 24
NZ = 48
SITES = 144
ROW = LX
KAPPA = 0.25
F32 = jnp.float32
BF16 = jnp.bfloat16
NT_DIMS = (((1,), (1,)), ((), ()))

USE_PALLAS = True


def roll(x, shift, axis):
    shift = shift % x.shape[axis]
    if USE_PALLAS:
        return pltpu.roll(x, shift, axis)
    return jnp.roll(x, shift, axis)


def half_sign(shape, low):
    lane = lax.broadcasted_iota(jnp.int32, shape, len(shape) - 1)
    return jnp.where(lane < 64, low, -low).astype(F32)


def turned(x):
    return roll(x, 64, 1) * half_sign(x.shape, -1.0)


def link(cols, mu, part, row, col, lo, hi):
    index = ((mu * 2 + part) * 3 + row) * 3 + col
    return cols[lo:hi, index : index + 1]


def carry(cols, mu, values, adjoint, lo, hi):
    spun = [turned(v) for v in values]
    out = []
    for i in range(3):
        total = None
        for j in range(3):
            if adjoint:
                term = link(cols, mu, 0, j, i, lo, hi) * values[j] - link(cols, mu, 1, j, i, lo, hi) * spun[j]
            else:
                term = link(cols, mu, 0, i, j, lo, hi) * values[j] + link(cols, mu, 1, i, j, lo, hi) * spun[j]
            total = term if total is None else total + term
        out.append(total)
    return out


def kernel_prepare(v_ref, g_ref, vt_ref, bz_ref, yf_ref, yb_ref, cols_ref):
    cols = g_ref[...].T
    cols_ref[...] = cols
    values = []
    for c in range(3):
        both = jnp.concatenate([v_ref[0, c], v_ref[1, c]], axis=0)
        values.append(both.T)
    for c in range(3):
        vt_ref[c] = values[c]
        yf_ref[c] = values[c][:ROW]
    back = carry(cols, 2, values, True, 0, SITES)
    edge = carry(cols, 1, [v[SITES - ROW :] for v in values], True, SITES - ROW, SITES)
    for c in range(3):
        bz_ref[c] = back[c]
        yb_ref[c] = edge[c]


def kernel_inner(vt_ref, cols_ref, acc_ref):
    cols = cols_ref[...]
    values = [vt_ref[c] for c in range(3)]
    x_coord = lax.broadcasted_iota(jnp.int32, (SITES, 128), 0) % LX
    ahead = [jnp.where(x_coord == LX - 1, roll(v, LX - 1, 0), roll(v, -1, 0)) for v in values]
    fwd = carry(cols, 0, ahead, False, 0, SITES)
    back = carry(cols, 0, values, True, 0, SITES)
    back = [jnp.where(x_coord == 0, roll(b, -(LX - 1), 0), roll(b, 1, 0)) for b in back]
    up = carry(cols, 1, [v[ROW:] for v in values], False, 0, SITES - ROW)
    down = carry(cols, 1, [v[: SITES - ROW] for v in values], True, 0, SITES - ROW)
    zero = jnp.zeros((ROW, 128), F32)
    for c in range(3):
        inner_y = jnp.concatenate([up[c], zero], axis=0) + jnp.concatenate([zero, down[c]], axis=0)
        acc_ref[c] = (1.0 - 6.0 * KAPPA) * values[c] + KAPPA * (fwd[c] + back[c]) + KAPPA * inner_y


def kernel_smear(acc_ref, cols_ref, above_ref, bz_ref, ya_ref, yb_ref, send_ref, out_ref):
    cols = cols_ref[...]
    fwd = carry(cols, 2, [above_ref[c] for c in range(3)], False, 0, SITES)
    edge = carry(cols, 1, [ya_ref[c] for c in range(3)], False, SITES - ROW, SITES)
    middle = jnp.zeros((SITES - 2 * ROW, 128), F32)
    for c in range(3):
        rims = jnp.concatenate([yb_ref[c], middle, edge[c]], axis=0)
        total = acc_ref[c] + KAPPA * rims + KAPPA * (fwd[c] + bz_ref[c])
        rounded = total.astype(BF16)
        for k in range(4):
            send_ref[k, c] = rounded
        flat = rounded.astype(F32).T
        out_ref[0, c] = flat[:64].astype(BF16)
        out_ref[1, c] = flat[64:].astype(BF16)


def kernel_contract(s_ref, ph_ref, out_ref, wide_ref, spun_ref, *, scale):
    rows = 4 * 3 * SITES
    lhs = []
    for k in range(4):
        for c in range(3):
            at = (k * 3 + c) * SITES
            wide = s_ref[k, c].astype(F32)
            wide_ref[at : at + SITES] = wide
            spun_ref[at : at + SITES] = turned(wide)
            lhs.append(wide.T.astype(BF16))
    lhs = jnp.concatenate(lhs, axis=1)
    phase = ph_ref[...].T
    sign = half_sign((64, 128), 1.0)
    for yl in range(4):
        pair = []
        for pp in range(2):
            p = yl * 2 + pp
            parts = []
            for k in range(4):
                cos = jnp.broadcast_to(phase[k * SITES : (k + 1) * SITES, p : p + 1], (SITES, 128))
                sin = jnp.broadcast_to(phase[k * SITES : (k + 1) * SITES, 8 + p : 9 + p], (SITES, 128))
                for c in range(3):
                    at = (k * 3 + c) * SITES
                    parts.append((wide_ref[at : at + SITES] * cos + spun_ref[at : at + SITES] * sin).astype(BF16))
            pair.append(jnp.concatenate(parts, axis=0))
        both = jnp.concatenate(pair, axis=1)
        prod = jnp.dot(lhs, both, preferred_element_type=F32)
        for pp in range(2):
            block = prod[:, pp * 128 : (pp + 1) * 128]
            result = (block[:64] + roll(block[64:], 64, 1) * sign) * scale
            out_ref[pp * 2, yl] = result[:32]
            out_ref[pp * 2 + 1, yl] = result[32:]


def kernel_correlate(tm_ref, e_ref, b1_ref, b2_ref, out_ref):
    own = tm_ref[0]
    flip = []
    for pp in range(2):
        phi = jnp.concatenate([e_ref[2 * pp, own], e_ref[2 * pp + 1, own]], axis=0)
        for k in range(16):
            out_ref[k, pp * 64 : (pp + 1) * 64] = phi
        tall = phi.astype(F32).T
        flip.append(jnp.concatenate([tall[:64], tall[64:]], axis=1))
    sign = half_sign((64, 128), 1.0)
    row = lax.broadcasted_iota(jnp.int32, (16, 128), 0)
    lane = lax.broadcasted_iota(jnp.int32, (16, 128), 1)
    tile = jnp.zeros((16, 128), F32)
    for t0 in range(4):
        weights = []
        for pp in range(2):
            far = jnp.concatenate([e_ref[2 * pp, t0], e_ref[2 * pp + 1, t0]], axis=0)
            weights.append(far)
            weights.append(turned(far.astype(F32)).astype(BF16))
        weights = jnp.concatenate(weights, axis=0)
        left = lax.dot_general(b1_ref[t0], weights, NT_DIMS, preferred_element_type=F32).astype(BF16)
        tall = []
        for pp in range(2):
            tall.append(
                jnp.concatenate([left[q * 64 : (q + 1) * 64, pp * 128 : (pp + 1) * 128] for q in range(16)], axis=1)
            )
        tall = jnp.concatenate(tall, axis=0)
        right = lax.dot_general(tall, b2_ref[t0], NT_DIMS, preferred_element_type=F32)
        for pp in range(2):
            block = right[pp * 64 : (pp + 1) * 64]
            real = jnp.sum(flip[pp] * block * sign) * (1.0 / NEV)
            imag = jnp.sum(flip[pp] * roll(block, 64, 1)) * (1.0 / NEV)
            here = row == pp * 4 + t0
            tile = jnp.where(here & (lane % 2 == 0), real, tile)
            tile = jnp.where(here & (lane % 2 == 1), imag, tile)
    high = tile.astype(BF16).astype(F32)
    middle = (tile - high).astype(BF16).astype(F32)
    low = tile - high - middle
    packed = jnp.where(lane < 2, high, jnp.where(lane < 4, middle, low)).astype(BF16)
    for k in range(16):
        out_ref[k, 128:144] = packed


def kernel_unpack(r_ref, e_ref):
    for s in range(16):
        for pp in range(2):
            both = r_ref[s, pp * 64 : (pp + 1) * 64]
            e_ref[2 * s + pp, 0] = both[:, :64]
            e_ref[2 * s + pp, 1] = both[:, 64:]


def shape(dims, dtype):
    return jax.ShapeDtypeStruct(dims, dtype)


def run(kernel, outs, args, name, scratch=(), scalar=False):
    in_specs = None
    if scalar:
        in_specs = [pl.BlockSpec(memory_space=pltpu.SMEM)] + [pl.BlockSpec(memory_space=pltpu.VMEM)] * (len(args) - 1)
    else:
        in_specs = [pl.BlockSpec(memory_space=pltpu.VMEM)] * len(args)
    return pl.pallas_call(
        kernel,
        out_shape=outs,
        in_specs=in_specs,
        out_specs=jax.tree.map(lambda _: pl.BlockSpec(memory_space=pltpu.VMEM), outs),
        scratch_shapes=list(scratch),
        name=name,
        compiler_params=pltpu.CompilerParams(vmem_limit_bytes=48 << 20),
    )(*args)


def phases(momenta, z_index):
    site = jnp.arange(4 * SITES, dtype=jnp.int32)
    turn_x = momenta[:, 0, None] * (site % LX)[None] % LX
    turn_y = momenta[:, 1, None] * (site // LX)[None] % LX
    turn_z = momenta[:, 2, None] * z_index % NZ
    angles = (
        2.0
        * math.pi
        * (turn_x.astype(F32) / LX + turn_y.astype(F32) / LX + turn_z.astype(F32) / NZ)
    )
    return jnp.concatenate([jnp.cos(angles), -jnp.sin(angles)], axis=0)


def swap(value, axes):
    return lax.all_to_all(value, axes, split_axis=0, concat_axis=0, tiled=True)


def spread(value, axes, count):
    return swap(jnp.broadcast_to(value[None], (count,) + value.shape), axes)


def local(eigvecs, gauge_links, perambulators, momenta):
    planes = ("zh", "zl", "yl")
    up = [(i, (i + 1) % NZ) for i in range(NZ)]
    down = [((i + 1) % NZ, i) for i in range(NZ)]
    ring_up = [(i, (i + 1) % 4) for i in range(4)]
    ring_down = [((i + 1) % 4, i) for i in range(4)]
    z_index = lax.axis_index(planes)
    x_index = lax.axis_index("x")
    tm_index = lax.axis_index(("yh", "c"))

    field = eigvecs.reshape(2, 3, NEV, SITES)
    links = gauge_links.reshape(54, SITES)
    site_shape = shape((3, SITES, 128), F32)
    row_shape = shape((3, ROW, 128), F32)
    values, back_z, first_row, last_row, cols = run(
        kernel_prepare,
        (site_shape, site_shape, row_shape, row_shape, shape((SITES, 54), F32)),
        (field, links),
        "prepare",
    )
    above = lax.ppermute(values, planes, down)
    below = lax.ppermute(back_z, planes, up)
    row_above = lax.ppermute(first_row, "x", ring_down)
    row_below = lax.ppermute(last_row, "x", ring_up)

    inner = run(kernel_inner, site_shape, (values, cols), "inner")
    mine = lax.dynamic_index_in_dim(momenta.reshape(4, 4, 2, 3), x_index, 1, keepdims=False).reshape(8, 3)
    phase = phases(mine, z_index)
    blocks = perambulators.reshape(4, 2, 16, NEV, NEV)
    tau_re = blocks[:, 0]
    tau_im = blocks[:, 1]
    straight = jnp.concatenate([tau_re, tau_im], axis=-1)
    crossed = jnp.concatenate([-tau_im, tau_re], axis=-1)
    first_factor = straight.reshape(4, 16 * NEV, 128)
    second_factor = jnp.concatenate(
        [
            jnp.swapaxes(straight, 1, 2).reshape(4, NEV, 16 * 128),
            jnp.swapaxes(crossed, 1, 2).reshape(4, NEV, 16 * 128),
        ],
        axis=1,
    )

    send, smeared = run(
        kernel_smear,
        (shape((4, 3, SITES, 128), BF16), shape((2, 3, NEV, SITES), BF16)),
        (inner, cols, above, below, row_above, row_below),
        "smear",
    )
    shared = swap(send, "x")
    scale = 1.0 / math.sqrt(3.0 * NZ * LX * LX)

    def contract(*refs):
        kernel_contract(*refs, scale=scale)

    partial = run(
        contract,
        shape((4, 4, 32, 128), F32),
        (shared, phase),
        "contract",
        scratch=[pltpu.VMEM((12 * SITES, 128), F32), pltpu.VMEM((12 * SITES, 128), F32)],
    )
    pieces = swap(partial.reshape(16, 32, 128), ("zl", "yl"))
    part = jnp.sum(pieces, axis=0)
    part = jnp.sum(spread(part, "zh", 3), axis=0)
    near = spread(part.astype(BF16), ("zl", "yh", "c"), 16).reshape(4, 4, 32, 128)
    payload = run(
        kernel_correlate,
        shape((16, 144, 128), BF16),
        (tm_index.astype(jnp.int32).reshape(1), near, first_factor, second_factor),
        "correlate",
        scalar=True,
    )
    everything = swap(payload, ("yl", "x"))
    elementals = run(kernel_unpack, shape((32, 2, NEV, NEV), BF16), (everything,), "unpack")
    terms = everything[:, 128:136, :6].astype(F32).reshape(16, 2, 4, 3, 2)
    correlator = (terms[..., 0, :] + terms[..., 1, :]) + terms[..., 2, :]
    correlator = jnp.moveaxis(correlator.reshape(32, 4, 2), 2, 0)
    return (
        smeared.reshape(1, 2, 3, NEV, 1, SITES),
        elementals.reshape(32, 1, 2, NEV, NEV),
        correlator.reshape(2, 32, 1, 4),
    )


def solution(mesh):
    fine = Mesh(mesh.devices.reshape(3, 4, 4, 4, 2, 2), ("zh", "zl", "yl", "x", "yh", "c"))
    space = ("zh", "zl", "yl", "x")
    times = ("yh", "c")
    return jax.shard_map(
        local,
        mesh=fine,
        in_specs=(
            P(times, None, None, None, space, None),
            P(None, times, None, None, None, space, None),
            P(times, None, None, None, None, None, None),
            P(),
        ),
        out_specs=(
            P(times, None, None, None, space, None),
            P(None, times, None, None, None),
            P(None, None, times, None),
        ),
        check_vma=False,
    )
```

time: 1880 us -> 127 us (0.07)
  the two profiles are of different devices: /device:TPU:2 before, /device:TPU:1 now
where the time goes in v1:
time: 127 us; the launch traced here: 126 us
  starting transfers between devices  54.9 us (43%)
  waiting for transfers between devices  19.6 us (15%)
  blocking collectives  19.5 us (15%)
  local copies, waits for them, and re-layouts  13.5 us (11%)
  Pallas kernels  10.4 us (8%)
  other arithmetic  7.17 us (6%)
    all_to_all x4, starting transfers between devices, swap(): return lax.all_to_all(value, axes, split_axis=0, concat_axis=0, tiled=True)  28.6 us
    all_to_all x1, blocking collectives, swap(): return lax.all_to_all(value, axes, split_axis=0, concat_axis=0, tiled=True)  19.5 us
    all_to_all x4, waiting for transfers between devices, swap(): return lax.all_to_all(value, axes, split_axis=0, concat_axis=0, tiled=True)  18.3 us
    ppermute x1, starting transfers between devices, local(): above = lax.ppermute(values, planes, down)  16.1 us
    pallas_call x6, Pallas kernels, run(): pl.pallas_call(kernel, out_shape=outs, in_specs=in_specs, out_specs=jax.t...  10.4 us
    ppermute x1, starting transfers between devices, local(): row_above = lax.ppermute(first_row, 'x', ring_down)  5.2 us
    transpose x1, other arithmetic, local(): jnp.swapaxes(straight, 1, 2).reshape(4, NEV, 16 * 128)  4.35 us
    ppermute x1, starting transfers between devices, local(): below = lax.ppermute(back_z, planes, up)  3.2 us
  transfers between devices with their start and end apart: 8, of which 5 were waited for; matrix products, arithmetic and copies ran while one was open for 12% of the time, Pallas kernels for 1%

profile of v1, /device:TPU:1, one launch (start us, length us, event | category | flops | bytes accessed | tf_op | source)
XLA Modules:
  0.0 125.9 jit_solution(4070319345935681770)
XLA Ops:
  0.6 1.0 reduce
  1.6 1.0 copy.56
  2.7 0.8 prepare.1
  3.4 5.2 %collective-permute-start.2 = (f32[3,24,128]{2,1,0:T(8,128)S(1)}, f32[3,24,128]{2,1,0:T(8,128)S(1)}, u32[]{:S(2)}, u32[]{:S(2)}) collective-permute-start(f32[3,24,128]{2,1,0:T(8,128)S(1)} %get-tuple-element.13), channel_id=1, source_target_pairs={{4,0},{8,4},{12,8},{0,12},{5,1},{9,5},{13,9},{1,13},{6,2},{10,6},{... | collective-permute-start | bytes 110600 | tf_op jit(solution)/shard_map/ppermute | solution.py:257
  8.6 1.9 %collective-permute-start.3 = (f32[3,24,128]{2,1,0:T(8,128)S(1)}, f32[3,24,128]{2,1,0:T(8,128)S(1)}, u32[]{:S(2)}, u32[]{:S(2)}) collective-permute-start(f32[3,24,128]{2,1,0:T(8,128)S(1)} %get-tuple-element.14), channel_id=1, source_target_pairs={{0,4},{4,8},{8,12},{12,0},{1,5},{5,9},{9,13},{13,1},{2,6},{6,10},{... | collective-permute-start | bytes 110600 | tf_op jit(solution)/shard_map/ppermute | solution.py:258
  10.6 3.2 %collective-permute-start.1 = (f32[3,144,128]{2,1,0:T(8,128)S(1)}, f32[3,144,128]{2,1,0:T(8,128)S(1)}, u32[]{:S(2)}, u32[]{:S(2)}) collective-permute-start(f32[3,144,128]{2,1,0:T(8,128)S(1)} %get-tuple-element.12), channel_id=1, source_target_pairs={{0,16},{16,32},{32,48},{48,64},{64,80},{80,96},{96,112},{112,128},... | collective-permute-start | bytes 663560 | tf_op jit(solution)/shard_map/ppermute | solution.py:256
  13.8 16.1 %collective-permute-start = (f32[3,144,128]{2,1,0:T(8,128)S(1)}, f32[3,144,128]{2,1,0:T(8,128)S(1)}, u32[]{:S(2)}, u32[]{:S(2)}) collective-permute-start(f32[3,144,128]{2,1,0:T(8,128)S(1)} %get-tuple-element.10.vt_ref), channel_id=1, source_target_pairs={{16,0},{32,16},{48,32},{64,48},{80,64},{96,80},{112,96},{128,112},... | collective-permute-start | bytes 663560 | tf_op jit(solution)/shard_map/ppermute | solution.py:255
  29.9 0.8 reshape.91
  30.7 0.1 copy.35
  30.8 0.2 fusion.16
  31.0 0.2 slice_reduce_fusion.1
  31.2 1.1 inner.1.acc_ref
  32.3 0.0 collective-permute-done.2.ya_ref
  32.3 0.0 collective-permute-done.3.yb_ref
  32.3 0.5 collective-permute-done.1.bz_ref
  32.8 0.9 collective-permute-done.above_ref
  33.7 1.4 %smear.1 = (bf16[4,3,144,128]{3,2,1,0:T(8,128)(2,1)}, bf16[2,3,64,144]{3,2,1,0:T(8,128)(2,1)}) custom-call(f32[3,144,128]{2,1,0:T(8,128)S(1)} %inner.1.acc_ref, f32[144,54]{1,0:T(8,128)S(1)} %get-tuple-element.11.cols_ref, f32[3,144,128]{2,1,0:T(8,128)S(1)} %collective-permute-done.above_ref, f32[3,144,128]{2,1,0:T(8,128)S(1)} %collective-permute-done.1.bz_ref, ...), custom_call_target="tpu_custom_call" | custom-call | tf_op jit(solution)/shard_map/smear/pallas_call | solution.py:203
  35.1 3.6 %all-to-all-start = ((bf16[4,3,144,128]{3,2,1,0:T(8,128)(2,1)}), bf16[4,3,144,128]{3,2,1,0:T(8,128)(2,1)S(1)}, u32[]{:S(2)}, u32[]{:S(2)}) async-start(bf16[4,3,144,128]{3,2,1,0:T(8,128)(2,1)} %get-tuple-element.16), calls=%async_computation | async-start | bytes 884736 | tf_op jit(solution)/shard_map/all_to_all | solution.py:228
  38.7 0.2 fusion.12
  38.9 6.3 %all-to-all-done.refs_0_ = bf16[4,3,144,128]{3,2,1,0:T(8,128)(2,1)S(1)} async-done(((bf16[4,3,144,128]{3,2,1,0:T(8,128)(2,1)}), bf16[4,3,144,128]{3,2,1,0:T(8,128)(2,1)S(1)}, u32[]{:S(2)}, u32[]{:S(2)}) %all-to-all-start) | async-done | bytes 442400 | tf_op jit(solution)/shard_map/all_to_all | solution.py:228
  45.2 4.1 %contract.1 = f32[4,4,32,128]{3,2,1,0:T(8,128)} custom-call(bf16[4,3,144,128]{3,2,1,0:T(8,128)(2,1)S(1)} %all-to-all-done.refs_0_, f32[16,576]{1,0:T(8,128)S(1)} %pad_maximum_fusion.2.refs_1_), custom_call_target="tpu_custom_call" | custom-call | tf_op jit(solution)/shard_map/contract/pallas_call | solution.py:203
  49.4 3.5 %all-to-all-start.1 = ((f32[16,32,128]{2,1,0:T(8,128)}), f32[16,32,128]{2,1,0:T(8,128)S(1)}, u32[]{:S(2)}, u32[]{:S(2)}) async-start(f32[16,32,128]{2,1,0:T(8,128)} %bitcast.4), calls=%async_computation.1 | async-start | bytes 524288 | tf_op jit(solution)/shard_map/all_to_all | solution.py:228
  52.9 1.8 %fusion.22 = (bf16[4,1,16,64,64]{4,3,2,1,0:T(8,128)(2,1)S(1)}, bf16[4,1,16,64,64]{4,3,2,1,0:T(8,128)(2,1)S(1)}) fusion(bf16[4,2,16,64,64]{4,3,2,1,0:T(8,128)(2,1)} %bitcast.46), kind=kLoop, calls=%fused_computation.48 | loop fusion | bytes 2097152 | tf_op jit(solution)/shard_map/slice | solution.py:264
  54.7 0.7 fusion.21
  55.4 2.7 %copy_bitcast_fusion = (bf16[4,16,64,64]{3,1,2,0:T(8,128)(2,1)}, bf16[4,16,64,64]{3,1,2,0:T(8,128)(2,1)}) fusion(bf16[4,1,16,64,64]{4,3,2,1,0:T(8,128)(2,1)S(1)} %get-tuple-element.32, bf16[4,1,16,64,64]{4,3,2,1,0:T(8,128)(2,1)S(1)} %get-tuple-element.31), kind=kLoop, calls=%fused_computation.4 | loop fusion | bytes 2097152 | tf_op jit(solution)/shard_map/squeeze | solution.py:265
  58.2 3.0 %all-to-all-done.1 = f32[16,32,128]{2,1,0:T(8,128)S(1)} async-done(((f32[16,32,128]{2,1,0:T(8,128)}), f32[16,32,128]{2,1,0:T(8,128)S(1)}, u32[]{:S(2)}, u32[]{:S(2)}) %all-to-all-start.1) | async-done | bytes 262176 | tf_op jit(solution)/shard_map/all_to_all | solution.py:228
  61.2 0.6 broadcast_in_dim.4
  61.8 9.8 %all-to-all-start.2 = ((f32[3,32,128]{2,1,0:T(8,128)}), f32[3,32,128]{2,1,0:T(8,128)S(1)}, u32[]{:S(2)}, u32[]{:S(2)}) async-start(f32[3,32,128]{2,1,0:T(8,128)} %broadcast_in_dim.4), calls=%async_computation.2 | async-start | bytes 98304 | tf_op jit(solution)/shard_map/all_to_all | solution.py:228
  71.6 4.3 %maximum_bitcast_fusion = (bf16[4,64,16,128]{3,2,1,0:T(8,128)(2,1)}, bf16[4,64,16,128]{3,2,1,0:T(8,128)(2,1)}) fusion(bf16[4,16,64,64]{3,1,2,0:T(8,128)(2,1)} %get-tuple-element.39, bf16[4,16,64,64]{3,1,2,0:T(8,128)(2,1)} %get-tuple-element.40, bf16[4,16,64,64]{3,1,2,0:T(8,128)(2,1)S(1)} %fusion.21), kind=kLoop, calls=%fused_computation.2 | loop fusion | flops 4194304 | bytes 3670016 | tf_op jit(solution)/shard_map/transpose | solution.py:271
  75.9 0.0 copy-start
  75.9 2.4 %reshape.96 = bf16[4,64,2048]{2,1,0:T(8,128)(2,1)} reshape(bf16[4,64,16,128]{3,2,1,0:T(8,128)(2,1)} %get-tuple-element.33) | data formatting | bytes 2097152 | tf_op jit(solution)/shard_map/reshape | solution.py:271
  78.3 0.0 copy-done
  78.3 1.3 reshape.97
  79.5 0.0 all-to-all-done.2
  79.6 0.7 broadcast_in_dim.5
  80.2 11.6 %all-to-all-start.3 = ((bf16[16,32,128]{2,1,0:T(8,128)(2,1)}), bf16[16,32,128]{2,1,0:T(8,128)(2,1)S(1)}, u32[]{:S(2)}, u32[]{:S(2)}) async-start(bf16[16,32,128]{2,1,0:T(8,128)(2,1)} %broadcast_in_dim.5), calls=%async_computation.3 | async-start | bytes 262144 | tf_op jit(solution)/shard_map/all_to_all | solution.py:228
  91.8 0.0 copy-start.2
  91.8 0.6 pad_maximum_fusion.1.b1_ref
  92.4 0.6 copy-done.1
  93.1 0.3 copy-done.2
  93.4 0.1 pad_maximum_fusion.b2_ref
  93.5 9.0 %all-to-all-done.3 = bf16[16,32,128]{2,1,0:T(8,128)(2,1)S(1)} async-done(((bf16[16,32,128]{2,1,0:T(8,128)(2,1)}), bf16[16,32,128]{2,1,0:T(8,128)(2,1)S(1)}, u32[]{:S(2)}, u32[]{:S(2)}) %all-to-all-start.3) | async-done | bytes 131104 | tf_op jit(solution)/shard_map/all_to_all | solution.py:228
  102.5 1.7 %correlate.1 = bf16[16,144,128]{2,1,0:T(8,128)(2,1)S(1)} custom-call(s32[1]{0:T(128)} %bitcast.2.tm_ref, bf16[4,4,32,128]{3,2,1,0:T(8,128)(2,1)S(1)} %bitcast.43, bf16[4,1024,128]{2,1,0:T(8,128)(2,1)S(1)} %pad_maximum_fusion.1.b1_ref, bf16[4,128,2048]{2,1,0:T(8,128)(2,1)S(1)} %pad_maximum_fusion.b2_ref), custom_call_target="tpu_custom_call" | custom-call | tf_op jit(solution)/shard_map/correlate/pallas_call | solution.py:203
  104.2 19.5 %all_to_all.25.r_ref = bf16[16,144,128]{2,1,0:T(8,128)(2,1)S(1)} all-to-all(bf16[16,144,128]{2,1,0:T(8,128)(2,1)S(1)} %correlate.1), channel_id=1, replica_groups=mesh['zh'=3,'zl'=4,'yl'=4,'x'=4,'yh'=2,'c'=2] {'yl','x'}, dimensions={0} | all-to-all | bytes 1179648 | tf_op jit(solution)/shard_map/all_to_all | solution.py:228
  123.7 0.1 copy.40
  123.8 0.1 copy.41
  123.9 0.7 copy.44
  124.6 1.3 %unpack.1 = bf16[32,2,64,64]{3,2,1,0:T(8,128)(2,1)} custom-call(bf16[16,144,128]{2,1,0:T(8,128)(2,1)S(1)} %all_to_all.25.r_ref), custom_call_target="tpu_custom_call" | custom-call | tf_op jit(solution)/shard_map/unpack/pallas_call | solution.py:203
  (9 shorter events, 0.1 us)
Async XLA Ops:
  3.4 28.8 %collective-permute-start.2 = (f32[3,24,128]{2,1,0:T(8,128)S(1)}, f32[3,24,128]{2,1,0:T(8,128)S(1)}, u32[]{:S(2)}, u32[]{:S(2)}) collective-permute-start(f32[3,24,128]{2,1,0:T(8,128)S(1)} %get-tuple-element.13), channel_id=1, source_target_pairs={{4,0},{8,4},{12,8},{0,12},{5,1},{9,5},{13,9},{1,13},{6,2},{10,6},{... | collective-permute-start | bytes 110600 | tf_op jit(solution)/shard_map/ppermute | solution.py:257
  8.6 23.6 %collective-permute-start.3 = (f32[3,24,128]{2,1,0:T(8,128)S(1)}, f32[3,24,128]{2,1,0:T(8,128)S(1)}, u32[]{:S(2)}, u32[]{:S(2)}) collective-permute-start(f32[3,24,128]{2,1,0:T(8,128)S(1)} %get-tuple-element.14), channel_id=1, source_target_pairs={{0,4},{4,8},{8,12},{12,0},{1,5},{5,9},{9,13},{13,1},{2,6},{6,10},{... | collective-permute-start | bytes 110600 | tf_op jit(solution)/shard_map/ppermute | solution.py:258
  10.6 22.2 %collective-permute-start.1 = (f32[3,144,128]{2,1,0:T(8,128)S(1)}, f32[3,144,128]{2,1,0:T(8,128)S(1)}, u32[]{:S(2)}, u32[]{:S(2)}) collective-permute-start(f32[3,144,128]{2,1,0:T(8,128)S(1)} %get-tuple-element.12), channel_id=1, source_target_pairs={{0,16},{16,32},{32,48},{48,64},{64,80},{80,96},{96,112},{112,128},... | collective-permute-start | bytes 663560 | tf_op jit(solution)/shard_map/ppermute | solution.py:256
  13.8 19.9 %collective-permute-start = (f32[3,144,128]{2,1,0:T(8,128)S(1)}, f32[3,144,128]{2,1,0:T(8,128)S(1)}, u32[]{:S(2)}, u32[]{:S(2)}) collective-permute-start(f32[3,144,128]{2,1,0:T(8,128)S(1)} %get-tuple-element.10.vt_ref), channel_id=1, source_target_pairs={{16,0},{32,16},{48,32},{64,48},{80,64},{96,80},{112,96},{128,112},... | collective-permute-start | bytes 663560 | tf_op jit(solution)/shard_map/ppermute | solution.py:255
  35.1 10.1 %all-to-all-start = ((bf16[4,3,144,128]{3,2,1,0:T(8,128)(2,1)}), bf16[4,3,144,128]{3,2,1,0:T(8,128)(2,1)S(1)}, u32[]{:S(2)}, u32[]{:S(2)}) async-start(bf16[4,3,144,128]{3,2,1,0:T(8,128)(2,1)} %get-tuple-element.16), calls=%async_computation | async-start | bytes 884736 | tf_op jit(solution)/shard_map/all_to_all | solution.py:228
  49.4 11.8 %all-to-all-start.1 = ((f32[16,32,128]{2,1,0:T(8,128)}), f32[16,32,128]{2,1,0:T(8,128)S(1)}, u32[]{:S(2)}, u32[]{:S(2)}) async-start(f32[16,32,128]{2,1,0:T(8,128)} %bitcast.4), calls=%async_computation.1 | async-start | bytes 524288 | tf_op jit(solution)/shard_map/all_to_all | solution.py:228
  61.8 17.8 %all-to-all-start.2 = ((f32[3,32,128]{2,1,0:T(8,128)}), f32[3,32,128]{2,1,0:T(8,128)S(1)}, u32[]{:S(2)}, u32[]{:S(2)}) async-start(f32[3,32,128]{2,1,0:T(8,128)} %broadcast_in_dim.4), calls=%async_computation.2 | async-start | bytes 98304 | tf_op jit(solution)/shard_map/all_to_all | solution.py:228
  75.9 2.4 %copy-start = (bf16[4,64,16,128]{3,2,1,0:T(8,128)(2,1)S(1)}, bf16[4,64,16,128]{3,2,1,0:T(8,128)(2,1)}, u32[]{:S(2)}) copy-start(bf16[4,64,16,128]{3,2,1,0:T(8,128)(2,1)} %get-tuple-element.34) | copy-start | bytes 3145732
  80.2 22.3 %all-to-all-start.3 = ((bf16[16,32,128]{2,1,0:T(8,128)(2,1)}), bf16[16,32,128]{2,1,0:T(8,128)(2,1)S(1)}, u32[]{:S(2)}, u32[]{:S(2)}) async-start(bf16[16,32,128]{2,1,0:T(8,128)(2,1)} %broadcast_in_dim.5), calls=%async_computation.3 | async-start | bytes 262144 | tf_op jit(solution)/shard_map/all_to_all | solution.py:228
  91.8 1.2 copy-start.1
  91.8 1.5 %copy-start.2 = (bf16[4,64,2048]{2,1,0:T(8,128)(2,1)S(1)}, bf16[4,64,2048]{2,1,0:T(8,128)(2,1)}, u32[]{:S(2)}) copy-start(bf16[4,64,2048]{2,1,0:T(8,128)(2,1)} %reshape.97) | copy-start | bytes 3145732

commit v2 on v1

--- a/solution.py
+++ b/solution.py
@@ -6,6 +6,7 @@
 from jax.experimental import pallas as pl
 from jax.experimental.pallas import tpu as pltpu
 from jax.sharding import Mesh, PartitionSpec as P
+
 
 NEV = 64
 LX = 24
@@ -56,21 +57,23 @@
     return out
 
 
-def kernel_prepare(v_ref, g_ref, vt_ref, bz_ref, yf_ref, yb_ref, cols_ref):
-    cols = g_ref[...].T
+def kernel_prepare(odd_ref, v_ref, g_ref, vt_ref, za_ref, zb_ref, xa_ref, xb_ref, cols_ref):
+    cols = g_ref[:, 0, :].T
     cols_ref[...] = cols
     values = []
     for c in range(3):
-        both = jnp.concatenate([v_ref[0, c], v_ref[1, c]], axis=0)
+        both = jnp.concatenate([v_ref[c * 64 : (c + 1) * 64, 0, :], v_ref[192 + c * 64 : 256 + c * 64, 0, :]], axis=0)
         values.append(both.T)
+    back = carry(cols, 2, values, True, 0, SITES)
+    edge = carry(cols, 1, [v[SITES - ROW :] for v in values], True, SITES - ROW, SITES)
+    plane_odd = odd_ref[0] == 1
+    block_odd = odd_ref[1] == 1
     for c in range(3):
         vt_ref[c] = values[c]
-        yf_ref[c] = values[c][:ROW]
-    back = carry(cols, 2, values, True, 0, SITES)
-    edge = carry(cols, 1, [v[SITES - ROW :] for v in values], True, SITES - ROW, SITES)
-    for c in range(3):
-        bz_ref[c] = back[c]
-        yb_ref[c] = edge[c]
+        za_ref[c] = jnp.where(plane_odd, values[c], back[c])
+        zb_ref[c] = jnp.where(plane_odd, back[c], values[c])
+        xa_ref[c] = jnp.where(block_odd, values[c][:ROW], edge[c])
+        xb_ref[c] = jnp.where(block_odd, edge[c], values[c][:ROW])
 
 
 def kernel_inner(vt_ref, cols_ref, acc_ref):
@@ -89,14 +92,18 @@
         acc_ref[c] = (1.0 - 6.0 * KAPPA) * values[c] + KAPPA * (fwd[c] + back[c]) + KAPPA * inner_y
 
 
-def kernel_smear(acc_ref, cols_ref, above_ref, bz_ref, ya_ref, yb_ref, send_ref, out_ref):
+def kernel_smear(odd_ref, acc_ref, cols_ref, za_ref, zb_ref, xa_ref, xb_ref, send_ref, out_ref):
     cols = cols_ref[...]
-    fwd = carry(cols, 2, [above_ref[c] for c in range(3)], False, 0, SITES)
-    edge = carry(cols, 1, [ya_ref[c] for c in range(3)], False, SITES - ROW, SITES)
+    plane_odd = odd_ref[0] == 1
+    block_odd = odd_ref[1] == 1
+    fwd = carry(cols, 2, [jnp.where(plane_odd, zb_ref[c], za_ref[c]) for c in range(3)], False, 0, SITES)
+    edge = carry(cols, 1, [jnp.where(block_odd, xb_ref[c], xa_ref[c]) for c in range(3)], False, SITES - ROW, SITES)
     middle = jnp.zeros((SITES - 2 * ROW, 128), F32)
     for c in range(3):
-        rims = jnp.concatenate([yb_ref[c], middle, edge[c]], axis=0)
-        total = acc_ref[c] + KAPPA * rims + KAPPA * (fwd[c] + bz_ref[c])
+        below = jnp.where(plane_odd, za_ref[c], zb_ref[c])
+        row_below = jnp.where(block_odd, xa_ref[c], xb_ref[c])
+        rims = jnp.concatenate([row_below, middle, edge[c]], axis=0)
+        total = acc_ref[c] + KAPPA * rims + KAPPA * (fwd[c] + below)
         rounded = total.astype(BF16)
         for k in range(4):
             send_ref[k, c] = rounded
@@ -106,7 +113,6 @@
 
 
 def kernel_contract(s_ref, ph_ref, out_ref, wide_ref, spun_ref, *, scale):
-    rows = 4 * 3 * SITES
     lhs = []
     for k in range(4):
         for c in range(3):
@@ -139,7 +145,17 @@
             out_ref[pp * 2 + 1, yl] = result[32:]
 
 
-def kernel_correlate(tm_ref, e_ref, b1_ref, b2_ref, out_ref):
+def kernel_factors(p_ref, out_ref):
+    for t0 in range(4):
+        for q in range(16):
+            real = p_ref[t0, 0, q].astype(F32)
+            imag = p_ref[t0, 1, q].astype(F32)
+            at = q * 128
+            out_ref[t0, :64, at : at + 128] = jnp.concatenate([real, imag], axis=1).astype(BF16)
+            out_ref[t0, 64:, at : at + 128] = jnp.concatenate([-imag, real], axis=1).astype(BF16)
+
+
+def kernel_correlate(tm_ref, e_ref, b_ref, out_ref):
     own = tm_ref[0]
     flip = []
     for pp in range(2):
@@ -159,14 +175,15 @@
             weights.append(far)
             weights.append(turned(far.astype(F32)).astype(BF16))
         weights = jnp.concatenate(weights, axis=0)
-        left = lax.dot_general(b1_ref[t0], weights, NT_DIMS, preferred_element_type=F32).astype(BF16)
+        first = jnp.concatenate([b_ref[t0, :64, q * 128 : (q + 1) * 128] for q in range(16)], axis=0)
+        left = lax.dot_general(first, weights, NT_DIMS, preferred_element_type=F32).astype(BF16)
         tall = []
         for pp in range(2):
             tall.append(
                 jnp.concatenate([left[q * 64 : (q + 1) * 64, pp * 128 : (pp + 1) * 128] for q in range(16)], axis=1)
             )
         tall = jnp.concatenate(tall, axis=0)
-        right = lax.dot_general(tall, b2_ref[t0], NT_DIMS, preferred_element_type=F32)
+        right = lax.dot_general(tall, b_ref[t0], NT_DIMS, preferred_element_type=F32)
         for pp in range(2):
             block = right[pp * 64 : (pp + 1) * 64]
             real = jnp.sum(flip[pp] * block * sign) * (1.0 / NEV)
@@ -194,7 +211,7 @@
     return jax.ShapeDtypeStruct(dims, dtype)
 
 
-def run(kernel, outs, args, name, scratch=(), scalar=False):
+def run(kernel, outs, args, scratch=(), scalar=False):
     in_specs = None
     if scalar:
         in_specs = [pl.BlockSpec(memory_space=pltpu.SMEM)] + [pl.BlockSpec(memory_space=pltpu.VMEM)] * (len(args) - 1)
@@ -206,7 +223,6 @@
         in_specs=in_specs,
         out_specs=jax.tree.map(lambda _: pl.BlockSpec(memory_space=pltpu.VMEM), outs),
         scratch_shapes=list(scratch),
-        name=name,
         compiler_params=pltpu.CompilerParams(vmem_limit_bytes=48 << 20),
     )(*args)
 
@@ -234,51 +250,41 @@
 
 def local(eigvecs, gauge_links, perambulators, momenta):
     planes = ("zh", "zl", "yl")
-    up = [(i, (i + 1) % NZ) for i in range(NZ)]
-    down = [((i + 1) % NZ, i) for i in range(NZ)]
-    ring_up = [(i, (i + 1) % 4) for i in range(4)]
-    ring_down = [((i + 1) % 4, i) for i in range(4)]
+    pairs_a = [(i, i ^ 1) for i in range(NZ)]
+    pairs_b = [(i, ((i + 1) ^ 1) - 1) for i in range(NZ)]
+    pairs_b = [(i, j % NZ) for i, j in pairs_b]
+    ring_a = [(i, i ^ 1) for i in range(4)]
+    ring_b = [(i, (((i + 1) ^ 1) - 1) % 4) for i in range(4)]
     z_index = lax.axis_index(planes)
     x_index = lax.axis_index("x")
     tm_index = lax.axis_index(("yh", "c"))
-
-    field = eigvecs.reshape(2, 3, NEV, SITES)
-    links = gauge_links.reshape(54, SITES)
+    odd = jnp.stack([lax.axis_index("yl") % 2, x_index % 2]).astype(jnp.int32)
+
+    field = eigvecs.reshape(6 * NEV, 1, SITES)
+    links = gauge_links.reshape(54, 1, SITES)
     site_shape = shape((3, SITES, 128), F32)
     row_shape = shape((3, ROW, 128), F32)
-    values, back_z, first_row, last_row, cols = run(
+    values, send_za, send_zb, send_xa, send_xb, cols = run(
         kernel_prepare,
-        (site_shape, site_shape, row_shape, row_shape, shape((SITES, 54), F32)),
-        (field, links),
-        "prepare",
-    )
-    above = lax.ppermute(values, planes, down)
-    below = lax.ppermute(back_z, planes, up)
-    row_above = lax.ppermute(first_row, "x", ring_down)
-    row_below = lax.ppermute(last_row, "x", ring_up)
-
-    inner = run(kernel_inner, site_shape, (values, cols), "inner")
+        (site_shape, site_shape, site_shape, row_shape, row_shape, shape((SITES, 54), F32)),
+        (odd, field, links),
+        scalar=True,
+    )
+    recv_za = lax.ppermute(send_za, planes, pairs_a)
+    recv_zb = lax.ppermute(send_zb, planes, pairs_b)
+    recv_xa = lax.ppermute(send_xa, "x", ring_a)
+    recv_xb = lax.ppermute(send_xb, "x", ring_b)
+
+    inner = run(kernel_inner, site_shape, (values, cols))
     mine = lax.dynamic_index_in_dim(momenta.reshape(4, 4, 2, 3), x_index, 1, keepdims=False).reshape(8, 3)
     phase = phases(mine, z_index)
-    blocks = perambulators.reshape(4, 2, 16, NEV, NEV)
-    tau_re = blocks[:, 0]
-    tau_im = blocks[:, 1]
-    straight = jnp.concatenate([tau_re, tau_im], axis=-1)
-    crossed = jnp.concatenate([-tau_im, tau_re], axis=-1)
-    first_factor = straight.reshape(4, 16 * NEV, 128)
-    second_factor = jnp.concatenate(
-        [
-            jnp.swapaxes(straight, 1, 2).reshape(4, NEV, 16 * 128),
-            jnp.swapaxes(crossed, 1, 2).reshape(4, NEV, 16 * 128),
-        ],
-        axis=1,
-    )
+    factors = run(kernel_factors, shape((4, 128, 16 * 128), BF16), (perambulators.reshape(4, 2, 16, NEV, NEV),))
 
     send, smeared = run(
         kernel_smear,
         (shape((4, 3, SITES, 128), BF16), shape((2, 3, NEV, SITES), BF16)),
-        (inner, cols, above, below, row_above, row_below),
-        "smear",
+        (odd, inner, cols, recv_za, recv_zb, recv_xa, recv_xb),
+        scalar=True,
     )
     shared = swap(send, "x")
     scale = 1.0 / math.sqrt(3.0 * NZ * LX * LX)
@@ -290,7 +296,6 @@
         contract,
         shape((4, 4, 32, 128), F32),
         (shared, phase),
-        "contract",
         scratch=[pltpu.VMEM((12 * SITES, 128), F32), pltpu.VMEM((12 * SITES, 128), F32)],
     )
     pieces = swap(partial.reshape(16, 32, 128), ("zl", "yl"))
@@ -300,12 +305,11 @@
     payload = run(
         kernel_correlate,
         shape((16, 144, 128), BF16),
-        (tm_index.astype(jnp.int32).reshape(1), near, first_factor, second_factor),
-        "correlate",
+        (tm_index.astype(jnp.int32).reshape(1), near, factors),
         scalar=True,
     )
     everything = swap(payload, ("yl", "x"))
-    elementals = run(kernel_unpack, shape((32, 2, NEV, NEV), BF16), (everything,), "unpack")
+    elementals = run(kernel_unpack, shape((32, 2, NEV, NEV), BF16), (everything,))
     terms = everything[:, 128:136, :6].astype(F32).reshape(16, 2, 4, 3, 2)
     correlator = (terms[..., 0, :] + terms[..., 1, :]) + terms[..., 2, :]
     correlator = jnp.moveaxis(correlator.reshape(32, 4, 2), 2, 0)
@@ -320,6 +324,7 @@
     fine = Mesh(mesh.devices.reshape(3, 4, 4, 4, 2, 2), ("zh", "zl", "yl", "x", "yh", "c"))
     space = ("zh", "zl", "yl", "x")
     times = ("yh", "c")
+
     return jax.shard_map(
         local,
         mesh=fine,

time: 127 us -> 125 us (0.984)
  blocking collectives: 19.5 us -> 44.9 us
  starting transfers between devices: 54.9 us -> 43.8 us
  local copies, waits for them, and re-layouts: 13.5 us -> 6.06 us
  other arithmetic: 7.17 us -> 0.52 us
  waiting for transfers between devices: 19.6 us -> 16.3 us
  Pallas kernels: 10.4 us -> 11.7 us
    all_to_all x1 -> x3, blocking collectives: 19.5 us -> 44.9 us  [swap(): return lax.all_to_all(value, axes, split_axis=0, concat_axis=0, tiled=True)]
    all_to_all x4 -> x2, starting transfers between devices: 28.6 us -> 16.8 us  [swap(): return lax.all_to_all(value, axes, split_axis=0, concat_axis=0, tiled=True)]
    transpose x1 -> x0, other arithmetic: 4.35 us -> none  [local(): jnp.swapaxes(straight, 1, 2).reshape(4, NEV, 16 * 128)]
    all_to_all x4 -> x2, waiting for transfers between devices: 18.3 us -> 14.5 us  [swap(): return lax.all_to_all(value, axes, split_axis=0, concat_axis=0, tiled=True)]
    reshape x3 -> x0, local copies, waits for them, and re-layouts: 3.66 us -> none  [the longest x1 2.38 us: local(): jnp.swapaxes(straight, 1, 2).reshape(4, NEV, 16 * 128)]
    squeeze x1 -> x0, local copies, waits for them, and re-layouts: 2.75 us -> none  [local(): tau_im = blocks[:, 1]]
    slice x1 -> x0, local copies, waits for them, and re-layouts: 1.82 us -> none  [local(): tau_re = blocks[:, 0]]
    unnamed x8 -> x7, local copies, waits for them, and re-layouts: 2.65 us -> 4.07 us
  transfers between devices with their start and end apart: 8 -> 6, of which waited for: 5 -> 3; matrix products, arithmetic and copies ran while one was open for 12% -> 1% of each run, Pallas kernels for 1% -> 2%
where the time goes in v2:
time: 125 us; the launch traced here: 124 us
  blocking collectives  44.9 us (36%)
  starting transfers between devices  43.8 us (35%)
  waiting for transfers between devices  16.3 us (13%)
  Pallas kernels  11.7 us (9%)
  local copies, waits for them, and re-layouts  6.06 us (5%)
    all_to_all x3, blocking collectives, swap(): return lax.all_to_all(value, axes, split_axis=0, concat_axis=0, tiled=True)  44.9 us
    all_to_all x2, starting transfers between devices, swap(): return lax.all_to_all(value, axes, split_axis=0, concat_axis=0, tiled=True)  16.8 us
    ppermute x1, starting transfers between devices, local(): recv_zb = lax.ppermute(send_zb, planes, pairs_b)  16.2 us
    all_to_all x2, waiting for transfers between devices, swap(): return lax.all_to_all(value, axes, split_axis=0, concat_axis=0, tiled=True)  14.5 us
    pallas_call x7, Pallas kernels, run(): pl.pallas_call(kernel, out_shape=outs, in_specs=in_specs, out_specs=jax.t...  11.7 us
    unnamed x7, local copies, waits for them, and re-layouts  4.07 us
    ppermute x1, starting transfers between devices, local(): recv_xa = lax.ppermute(send_xa, 'x', ring_a)  3.94 us
    ppermute x1, starting transfers between devices, local(): recv_xb = lax.ppermute(send_xb, 'x', ring_b)  3.72 us
  transfers between devices with their start and end apart: 6, of which 3 were waited for; matrix products, arithmetic and copies ran while one was open for 1% of the time, Pallas kernels for 2%

profile of v2, /device:TPU:1, one launch (start us, length us, event | category | flops | bytes accessed | tf_op | source)
XLA Modules:
  0.0 124.2 jit_solution(11016329132982996243)
XLA Ops:
  0.7 0.1 pad_add_fusion.odd_ref
  0.7 0.0 copy-start.1
  0.7 1.0 copy-done.1
  1.7 0.0 copy-start.2
  1.7 0.8 copy-done.2
  2.5 1.3 %shard_map.67 = (f32[3,144,128]{2,1,0:T(8,128)S(1)}, f32[3,144,128]{2,1,0:T(8,128)S(1)}, f32[3,144,128]{2,1,0:T(8,128)S(1)}, f32[3,24,128]{2,1,0:T(8,128)S(1)}, ...) custom-call(s32[2]{0:T(128)S(1)} %pad_add_fusion.odd_ref, f32[384,1,144]{2,1,0:T(1,128)S(1)} %bitcast.26, ...), custom_call_target="tpu_custom_call" | custom-call | tf_op jit(solution)/shard_map/pallas_call | solution.py:220
  3.9 3.9 %collective-permute-start.2 = (f32[3,24,128]{2,1,0:T(8,128)S(1)}, f32[3,24,128]{2,1,0:T(8,128)S(1)}, u32[]{:S(2)}, u32[]{:S(2)}) collective-permute-start(f32[3,24,128]{2,1,0:T(8,128)S(1)} %get-tuple-element.15), channel_id=1, source_target_pairs={{0,4},{4,0},{8,12},{12,8},{1,5},{5,1},{9,13},{13,9},{2,6},{6,2},{1... | collective-permute-start | bytes 110600 | tf_op jit(solution)/shard_map/ppermute | solution.py:275
  7.8 3.7 %collective-permute-start.3 = (f32[3,24,128]{2,1,0:T(8,128)S(1)}, f32[3,24,128]{2,1,0:T(8,128)S(1)}, u32[]{:S(2)}, u32[]{:S(2)}) collective-permute-start(f32[3,24,128]{2,1,0:T(8,128)S(1)} %get-tuple-element.16), channel_id=1, source_target_pairs={{0,12},{4,8},{8,4},{12,0},{1,13},{5,9},{9,5},{13,1},{2,14},{6,10},... | collective-permute-start | bytes 110600 | tf_op jit(solution)/shard_map/ppermute | solution.py:276
  11.5 3.2 %collective-permute-start = (f32[3,144,128]{2,1,0:T(8,128)S(1)}, f32[3,144,128]{2,1,0:T(8,128)S(1)}, u32[]{:S(2)}, u32[]{:S(2)}) collective-permute-start(f32[3,144,128]{2,1,0:T(8,128)S(1)} %get-tuple-element.13), channel_id=1, source_target_pairs={{0,16},{16,0},{32,48},{48,32},{64,80},{80,64},{96,112},{112,96},{1... | collective-permute-start | bytes 663560 | tf_op jit(solution)/shard_map/ppermute | solution.py:273
  14.7 16.2 %collective-permute-start.1 = (f32[3,144,128]{2,1,0:T(8,128)S(1)}, f32[3,144,128]{2,1,0:T(8,128)S(1)}, u32[]{:S(2)}, u32[]{:S(2)}) collective-permute-start(f32[3,144,128]{2,1,0:T(8,128)S(1)} %get-tuple-element.14), channel_id=1, source_target_pairs={{0,752},{16,32},{32,16},{48,64},{64,48},{80,96},{96,80},{112,128},... | collective-permute-start | bytes 663560 | tf_op jit(solution)/shard_map/ppermute | solution.py:274
  31.0 0.8 reshape.80
  31.8 0.1 copy.23
  31.9 0.2 fusion.16
  32.1 0.2 slice_reduce_fusion.1
  32.3 1.1 shard_map.68.acc_ref
  33.4 0.0 collective-permute-done.2.xa_ref
  33.4 0.0 collective-permute-done.3.xb_ref
  33.4 0.0 collective-permute-done.za_ref
  33.4 1.8 %collective-permute-done.1.zb_ref = f32[3,144,128]{2,1,0:T(8,128)S(1)} collective-permute-done((f32[3,144,128]{2,1,0:T(8,128)S(1)}, f32[3,144,128]{2,1,0:T(8,128)S(1)}, u32[]{:S(2)}, u32[]{:S(2)}) %collective-permute-start.1) | collective-permute-done | bytes 221216 | tf_op jit(solution)/shard_map/ppermute | solution.py:274
  35.2 2.0 %shard_map.69 = (bf16[4,3,144,128]{3,2,1,0:T(8,128)(2,1)}, bf16[2,3,64,144]{3,2,1,0:T(8,128)(2,1)}) custom-call(s32[2]{0:T(128)S(1)} %pad_add_fusion.odd_ref, f32[3,144,128]{2,1,0:T(8,128)S(1)} %shard_map.68.acc_ref, f32[144,54]{1,0:T(8,128)S(1)} %get-tuple-element.12.cols_ref, f32[3,144,128]{2,1,0:T(8,128)S(1)} %collective-permute-done.za_ref, ...), custom_call_target="tpu_custom_call" | custom-call | tf_op jit(solution)/shard_map/pallas_call | solution.py:220
  37.3 3.5 %all-to-all-start = ((bf16[4,3,144,128]{3,2,1,0:T(8,128)(2,1)}), bf16[4,3,144,128]{3,2,1,0:T(8,128)(2,1)S(1)}, u32[]{:S(2)}, u32[]{:S(2)}) async-start(bf16[4,3,144,128]{3,2,1,0:T(8,128)(2,1)} %get-tuple-element.18), calls=%async_computation | async-start | bytes 884736 | tf_op jit(solution)/shard_map/all_to_all | solution.py:244
  40.7 0.2 fusion.12
  40.9 6.3 %all-to-all-done.refs_0_ = bf16[4,3,144,128]{3,2,1,0:T(8,128)(2,1)S(1)} async-done(((bf16[4,3,144,128]{3,2,1,0:T(8,128)(2,1)}), bf16[4,3,144,128]{3,2,1,0:T(8,128)(2,1)S(1)}, u32[]{:S(2)}, u32[]{:S(2)}) %all-to-all-start) | async-done | bytes 442400 | tf_op jit(solution)/shard_map/all_to_all | solution.py:244
  47.2 3.4 %shard_map.70 = f32[4,4,32,128]{3,2,1,0:T(8,128)S(1)} custom-call(bf16[4,3,144,128]{3,2,1,0:T(8,128)(2,1)S(1)} %all-to-all-done.refs_0_, f32[16,576]{1,0:T(8,128)S(1)} %pad_maximum_fusion.refs_1_), custom_call_target="tpu_custom_call" | custom-call | tf_op jit(solution)/shard_map/pallas_call | solution.py:220
  50.6 11.1 %all_to_all.25 = f32[16,32,128]{2,1,0:T(8,128)S(1)} all-to-all(f32[16,32,128]{2,1,0:T(8,128)S(1)} %bitcast.24), channel_id=1, replica_groups=mesh['zh'=3,'zl'=4,'yl'=4,'x'=4,'yh'=2,'c'=2] {'zl','yl'}, dimensions={0} | all-to-all | bytes 524288 | tf_op jit(solution)/shard_map/all_to_all | solution.py:244
  61.7 14.4 %all_to_all.26 = f32[3,32,128]{2,1,0:T(8,128)S(1)} all-to-all(f32[3,32,128]{2,1,0:T(8,128)S(1)} %broadcast_in_dim.4), channel_id=1, replica_groups=mesh['zh'=3,'zl'=4,'yl'=4,'x'=4,'yh'=2,'c'=2] {'zh'}, dimensions={0} | all-to-all | bytes 98304 | tf_op jit(solution)/shard_map/all_to_all | solution.py:244
  76.2 0.7 broadcast_in_dim.5
  76.8 13.3 %all-to-all-start.3 = ((bf16[16,32,128]{2,1,0:T(8,128)(2,1)}), bf16[16,32,128]{2,1,0:T(8,128)(2,1)S(1)}, u32[]{:S(2)}, u32[]{:S(2)}) async-start(bf16[16,32,128]{2,1,0:T(8,128)(2,1)} %broadcast_in_dim.5), calls=%async_computation.3 | async-start | bytes 262144 | tf_op jit(solution)/shard_map/all_to_all | solution.py:244
  90.1 0.0 copy-start
  90.1 1.6 %copy-done = bf16[1,4,2,4,4,64,64]{6,5,4,3,2,1,0:T(8,128)(2,1)S(1)} copy-done((bf16[1,4,2,4,4,64,64]{6,5,4,3,2,1,0:T(8,128)(2,1)S(1)}, bf16[1,4,2,4,4,64,64]{6,5,4,3,2,1,0:T(8,128)(2,1)}, u32[]{:S(2)}) %copy-start) | copy-done | bytes 1048600
  91.7 0.8 shard_map.71.b_ref
  92.6 8.2 %all-to-all-done.3 = bf16[16,32,128]{2,1,0:T(8,128)(2,1)S(1)} async-done(((bf16[16,32,128]{2,1,0:T(8,128)(2,1)}), bf16[16,32,128]{2,1,0:T(8,128)(2,1)S(1)}, u32[]{:S(2)}, u32[]{:S(2)}) %all-to-all-start.3) | async-done | bytes 131104 | tf_op jit(solution)/shard_map/all_to_all | solution.py:244
  100.8 1.7 %shard_map.72 = bf16[16,144,128]{2,1,0:T(8,128)(2,1)S(1)} custom-call(s32[1]{0:T(128)} %bitcast.6.tm_ref, bf16[4,4,32,128]{3,2,1,0:T(8,128)(2,1)S(1)} %bitcast.25, bf16[4,128,2048]{2,1,0:T(8,128)(2,1)S(1)} %shard_map.71.b_ref), custom_call_target="tpu_custom_call" | custom-call | tf_op jit(solution)/shard_map/pallas_call | solution.py:220
  102.5 19.4 %all_to_all.27.r_ref = bf16[16,144,128]{2,1,0:T(8,128)(2,1)S(1)} all-to-all(bf16[16,144,128]{2,1,0:T(8,128)(2,1)S(1)} %shard_map.72), channel_id=1, replica_groups=mesh['zh'=3,'zl'=4,'yl'=4,'x'=4,'yh'=2,'c'=2] {'yl','x'}, dimensions={0} | all-to-all | bytes 1179648 | tf_op jit(solution)/shard_map/all_to_all | solution.py:244
  121.9 0.1 copy.24
  122.1 0.1 copy.25
  122.2 0.7 copy.28
  122.9 1.3 %shard_map.73 = bf16[32,2,64,64]{3,2,1,0:T(8,128)(2,1)} custom-call(bf16[16,144,128]{2,1,0:T(8,128)(2,1)S(1)} %all_to_all.27.r_ref), custom_call_target="tpu_custom_call" | custom-call | tf_op jit(solution)/shard_map/pallas_call | solution.py:220
  (8 shorter events, 0.1 us)
Async XLA Ops:
  0.7 1.0 copy-start.1
  1.7 0.8 copy-start.2
  3.9 29.5 %collective-permute-start.2 = (f32[3,24,128]{2,1,0:T(8,128)S(1)}, f32[3,24,128]{2,1,0:T(8,128)S(1)}, u32[]{:S(2)}, u32[]{:S(2)}) collective-permute-start(f32[3,24,128]{2,1,0:T(8,128)S(1)} %get-tuple-element.15), channel_id=1, source_target_pairs={{0,4},{4,0},{8,12},{12,8},{1,5},{5,1},{9,13},{13,9},{2,6},{6,2},{1... | collective-permute-start | bytes 110600 | tf_op jit(solution)/shard_map/ppermute | solution.py:275
  7.8 25.6 %collective-permute-start.3 = (f32[3,24,128]{2,1,0:T(8,128)S(1)}, f32[3,24,128]{2,1,0:T(8,128)S(1)}, u32[]{:S(2)}, u32[]{:S(2)}) collective-permute-start(f32[3,24,128]{2,1,0:T(8,128)S(1)} %get-tuple-element.16), channel_id=1, source_target_pairs={{0,12},{4,8},{8,4},{12,0},{1,13},{5,9},{9,5},{13,1},{2,14},{6,10},... | collective-permute-start | bytes 110600 | tf_op jit(solution)/shard_map/ppermute | solution.py:276
  11.5 21.9 %collective-permute-start = (f32[3,144,128]{2,1,0:T(8,128)S(1)}, f32[3,144,128]{2,1,0:T(8,128)S(1)}, u32[]{:S(2)}, u32[]{:S(2)}) collective-permute-start(f32[3,144,128]{2,1,0:T(8,128)S(1)} %get-tuple-element.13), channel_id=1, source_target_pairs={{0,16},{16,0},{32,48},{48,32},{64,80},{80,64},{96,112},{112,96},{1... | collective-permute-start | bytes 663560 | tf_op jit(solution)/shard_map/ppermute | solution.py:273
  14.7 20.5 %collective-permute-start.1 = (f32[3,144,128]{2,1,0:T(8,128)S(1)}, f32[3,144,128]{2,1,0:T(8,128)S(1)}, u32[]{:S(2)}, u32[]{:S(2)}) collective-permute-start(f32[3,144,128]{2,1,0:T(8,128)S(1)} %get-tuple-element.14), channel_id=1, source_target_pairs={{0,752},{16,32},{32,16},{48,64},{64,48},{80,96},{96,80},{112,128},... | collective-permute-start | bytes 663560 | tf_op jit(solution)/shard_map/ppermute | solution.py:274
  37.3 9.9 %all-to-all-start = ((bf16[4,3,144,128]{3,2,1,0:T(8,128)(2,1)}), bf16[4,3,144,128]{3,2,1,0:T(8,128)(2,1)S(1)}, u32[]{:S(2)}, u32[]{:S(2)}) async-start(bf16[4,3,144,128]{3,2,1,0:T(8,128)(2,1)} %get-tuple-element.18), calls=%async_computation | async-start | bytes 884736 | tf_op jit(solution)/shard_map/all_to_all | solution.py:244
  76.8 24.0 %all-to-all-start.3 = ((bf16[16,32,128]{2,1,0:T(8,128)(2,1)}), bf16[16,32,128]{2,1,0:T(8,128)(2,1)S(1)}, u32[]{:S(2)}, u32[]{:S(2)}) async-start(bf16[16,32,128]{2,1,0:T(8,128)(2,1)} %broadcast_in_dim.5), calls=%async_computation.3 | async-start | bytes 262144 | tf_op jit(solution)/shard_map/all_to_all | solution.py:244
  90.1 1.6 %copy-start = (bf16[1,4,2,4,4,64,64]{6,5,4,3,2,1,0:T(8,128)(2,1)S(1)}, bf16[1,4,2,4,4,64,64]{6,5,4,3,2,1,0:T(8,128)(2,1)}, u32[]{:S(2)}) copy-start(bf16[1,4,2,4,4,64,64]{6,5,4,3,2,1,0:T(8,128)(2,1)} %param.6) | copy-start | bytes 3145732

commit v3 on v2

--- a/solution.py
+++ b/solution.py
@@ -57,9 +57,15 @@
     return out
 
 
-def kernel_prepare(odd_ref, v_ref, g_ref, vt_ref, za_ref, zb_ref, xa_ref, xb_ref, cols_ref):
+def kernel_prepare(odd_ref, v_hbm, g_hbm, vt_ref, za_ref, zb_ref, xa_ref, xb_ref, cols_ref, v_ref, g_ref, sem):
+    copy_g = pltpu.make_async_copy(g_hbm, g_ref, sem.at[0])
+    copy_v = pltpu.make_async_copy(v_hbm, v_ref, sem.at[1])
+    copy_g.start()
+    copy_v.start()
+    copy_g.wait()
     cols = g_ref[:, 0, :].T
     cols_ref[...] = cols
+    copy_v.wait()
     values = []
     for c in range(3):
         both = jnp.concatenate([v_ref[c * 64 : (c + 1) * 64, 0, :], v_ref[192 + c * 64 : 256 + c * 64, 0, :]], axis=0)
@@ -92,7 +98,7 @@
         acc_ref[c] = (1.0 - 6.0 * KAPPA) * values[c] + KAPPA * (fwd[c] + back[c]) + KAPPA * inner_y
 
 
-def kernel_smear(odd_ref, acc_ref, cols_ref, za_ref, zb_ref, xa_ref, xb_ref, send_ref, out_ref):
+def kernel_smear(odd_ref, acc_ref, cols_ref, za_ref, zb_ref, xa_ref, xb_ref, send_ref):
     cols = cols_ref[...]
     plane_odd = odd_ref[0] == 1
     block_odd = odd_ref[1] == 1
@@ -107,7 +113,11 @@
         rounded = total.astype(BF16)
         for k in range(4):
             send_ref[k, c] = rounded
-        flat = rounded.astype(F32).T
+
+
+def kernel_output(s_ref, out_ref):
+    for c in range(3):
+        flat = s_ref[0, c].astype(F32).T
         out_ref[0, c] = flat[:64].astype(BF16)
         out_ref[1, c] = flat[64:].astype(BF16)
 
@@ -188,18 +198,22 @@
             block = right[pp * 64 : (pp + 1) * 64]
             real = jnp.sum(flip[pp] * block * sign) * (1.0 / NEV)
             imag = jnp.sum(flip[pp] * roll(block, 64, 1)) * (1.0 / NEV)
-            here = row == pp * 4 + t0
-            tile = jnp.where(here & (lane % 2 == 0), real, tile)
-            tile = jnp.where(here & (lane % 2 == 1), imag, tile)
+            tile = jnp.where((row == pp) & (lane % 8 == t0), real, tile)
+            tile = jnp.where((row == pp) & (lane % 8 == 4 + t0), imag, tile)
     high = tile.astype(BF16).astype(F32)
     middle = (tile - high).astype(BF16).astype(F32)
     low = tile - high - middle
-    packed = jnp.where(lane < 2, high, jnp.where(lane < 4, middle, low)).astype(BF16)
+    packed = jnp.where(lane < 8, high, jnp.where(lane < 16, middle, low)).astype(BF16)
     for k in range(16):
         out_ref[k, 128:144] = packed
 
 
-def kernel_unpack(r_ref, e_ref):
+def kernel_unpack(r_ref, e_ref, c_ref):
+    rows = jnp.concatenate([r_ref[s, 128:144].astype(F32)[:2] for s in range(16)], axis=0)
+    total = (rows + roll(rows, -8, 1)) + roll(rows, -16, 1)
+    tall = total.T
+    c_ref[0] = tall[:4]
+    c_ref[1] = tall[4:8]
     for s in range(16):
         for pp in range(2):
             both = r_ref[s, pp * 64 : (pp + 1) * 64]
@@ -211,9 +225,11 @@
     return jax.ShapeDtypeStruct(dims, dtype)
 
 
-def run(kernel, outs, args, scratch=(), scalar=False):
+def run(kernel, outs, args, scratch=(), scalar=False, raw=False):
     in_specs = None
-    if scalar:
+    if raw:
+        in_specs = [pl.BlockSpec(memory_space=pltpu.SMEM)] + [pl.BlockSpec(memory_space=pltpu.HBM)] * (len(args) - 1)
+    elif scalar:
         in_specs = [pl.BlockSpec(memory_space=pltpu.SMEM)] + [pl.BlockSpec(memory_space=pltpu.VMEM)] * (len(args) - 1)
     else:
         in_specs = [pl.BlockSpec(memory_space=pltpu.VMEM)] * len(args)
@@ -268,7 +284,12 @@
         kernel_prepare,
         (site_shape, site_shape, site_shape, row_shape, row_shape, shape((SITES, 54), F32)),
         (odd, field, links),
-        scalar=True,
+        scratch=[
+            pltpu.VMEM((6 * NEV, 1, SITES), F32),
+            pltpu.VMEM((54, 1, SITES), F32),
+            pltpu.SemaphoreType.DMA((2,)),
+        ],
+        raw=True,
     )
     recv_za = lax.ppermute(send_za, planes, pairs_a)
     recv_zb = lax.ppermute(send_zb, planes, pairs_b)
@@ -276,17 +297,19 @@
     recv_xb = lax.ppermute(send_xb, "x", ring_b)
 
     inner = run(kernel_inner, site_shape, (values, cols))
+    send = run(
+        kernel_smear,
+        shape((4, 3, SITES, 128), BF16),
+        (odd, inner, cols, recv_za, recv_zb, recv_xa, recv_xb),
+        scalar=True,
+    )
+    send, momenta, perambulators = lax.optimization_barrier((send, momenta, perambulators))
+    shared = swap(send, "x")
+    smeared = run(kernel_output, shape((2, 3, NEV, SITES), BF16), (send,))
     mine = lax.dynamic_index_in_dim(momenta.reshape(4, 4, 2, 3), x_index, 1, keepdims=False).reshape(8, 3)
     phase = phases(mine, z_index)
     factors = run(kernel_factors, shape((4, 128, 16 * 128), BF16), (perambulators.reshape(4, 2, 16, NEV, NEV),))
 
-    send, smeared = run(
-        kernel_smear,
-        (shape((4, 3, SITES, 128), BF16), shape((2, 3, NEV, SITES), BF16)),
-        (odd, inner, cols, recv_za, recv_zb, recv_xa, recv_xb),
-        scalar=True,
-    )
-    shared = swap(send, "x")
     scale = 1.0 / math.sqrt(3.0 * NZ * LX * LX)
 
     def contract(*refs):
@@ -309,14 +332,11 @@
         scalar=True,
     )
     everything = swap(payload, ("yl", "x"))
-    elementals = run(kernel_unpack, shape((32, 2, NEV, NEV), BF16), (everything,))
-    terms = everything[:, 128:136, :6].astype(F32).reshape(16, 2, 4, 3, 2)
-    correlator = (terms[..., 0, :] + terms[..., 1, :]) + terms[..., 2, :]
-    correlator = jnp.moveaxis(correlator.reshape(32, 4, 2), 2, 0)
+    elementals, correlator = run(kernel_unpack, (shape((32, 2, NEV, NEV), BF16), shape((2, 4, 32), F32)), (everything,))
     return (
         smeared.reshape(1, 2, 3, NEV, 1, SITES),
         elementals.reshape(32, 1, 2, NEV, NEV),
-        correlator.reshape(2, 32, 1, 4),
+        jnp.swapaxes(correlator, 1, 2).reshape(2, 32, 1, 4),
     )
 
 

time: 125 us -> 120 us (0.960)
  the two profiles are of different devices: /device:TPU:1 before, /device:TPU:8 now
where the time goes in v3:
time: 120 us; the launch traced here: 119 us
  waiting for transfers between devices  34.3 us (29%)
  blocking collectives  33.1 us (28%)
  starting transfers between devices  31.1 us (26%)
  Pallas kernels  14.7 us (12%)
  local copies, waits for them, and re-layouts  4.47 us (4%)
    all_to_all x2, blocking collectives, swap(): return lax.all_to_all(value, axes, split_axis=0, concat_axis=0, tiled=True)  33.1 us
    all_to_all x3, waiting for transfers between devices, swap(): return lax.all_to_all(value, axes, split_axis=0, concat_axis=0, tiled=True)  30.3 us
    pallas_call x8, Pallas kernels, run(): pl.pallas_call(kernel, out_shape=outs, in_specs=in_specs, out_specs=jax.t...  14.7 us
    all_to_all x3, starting transfers between devices, swap(): return lax.all_to_all(value, axes, split_axis=0, concat_axis=0, tiled=True)  14 us
    ppermute x1, starting transfers between devices, local(): recv_za = lax.ppermute(send_za, planes, pairs_a)  11.3 us
    unnamed x8, local copies, waits for them, and re-layouts  3.4 us
    ppermute x1, waiting for transfers between devices, local(): recv_xb = lax.ppermute(send_xb, 'x', ring_b)  3.14 us
  transfers between devices with their start and end apart: 7, of which 5 were waited for; matrix products, arithmetic and copies ran while one was open for 1% of the time, Pallas kernels for 3%

profile of v3, /device:TPU:8, one launch (start us, length us, event | category | flops | bytes accessed | tf_op | source)
XLA Modules:
  0.0 119.0 jit_solution(10323332396496313026)
XLA Ops:
  0.6 0.0 copy-start.3
  0.7 0.1 pad_add_fusion.odd_ref
  0.7 0.0 copy-start.1
  0.7 1.0 copy-done.1
  1.7 0.0 copy-start.2
  1.7 0.8 copy-done.2
  2.5 1.7 %shard_map.67 = (f32[3,144,128]{2,1,0:T(8,128)S(1)}, f32[3,144,128]{2,1,0:T(8,128)S(1)}, f32[3,144,128]{2,1,0:T(8,128)S(1)}, f32[3,24,128]{2,1,0:T(8,128)S(1)}, ...) custom-call(s32[2]{0:T(128)S(1)} %pad_add_fusion.odd_ref, f32[384,1,144]{2,1,0:T(1,128)S(1)} %bitcast.25, ...), custom_call_target="tpu_custom_call" | custom-call | tf_op jit(solution)/shard_map/pallas_call | solution.py:236
  4.3 11.3 %collective-permute-start = (f32[3,144,128]{2,1,0:T(8,128)S(1)}, f32[3,144,128]{2,1,0:T(8,128)S(1)}, u32[]{:S(2)}, u32[]{:S(2)}) collective-permute-start(f32[3,144,128]{2,1,0:T(8,128)S(1)} %get-tuple-element.16), channel_id=1, source_target_pairs={{0,16},{16,0},{32,48},{48,32},{64,80},{80,64},{96,112},{112,96},{1... | collective-permute-start | bytes 663560 | tf_op jit(solution)/shard_map/ppermute | solution.py:294
  15.6 1.9 %collective-permute-start.1 = (f32[3,144,128]{2,1,0:T(8,128)S(1)}, f32[3,144,128]{2,1,0:T(8,128)S(1)}, u32[]{:S(2)}, u32[]{:S(2)}) collective-permute-start(f32[3,144,128]{2,1,0:T(8,128)S(1)} %get-tuple-element.17), channel_id=1, source_target_pairs={{0,752},{16,32},{32,16},{48,64},{64,48},{80,96},{96,80},{112,128},... | collective-permute-start | bytes 663560 | tf_op jit(solution)/shard_map/ppermute | solution.py:295
  17.5 1.9 %collective-permute-start.2 = (f32[3,24,128]{2,1,0:T(8,128)S(1)}, f32[3,24,128]{2,1,0:T(8,128)S(1)}, u32[]{:S(2)}, u32[]{:S(2)}) collective-permute-start(f32[3,24,128]{2,1,0:T(8,128)S(1)} %get-tuple-element.18), channel_id=1, source_target_pairs={{0,4},{4,0},{8,12},{12,8},{1,5},{5,1},{9,13},{13,9},{2,6},{6,2},{1... | collective-permute-start | bytes 110600 | tf_op jit(solution)/shard_map/ppermute | solution.py:296
  19.5 1.9 %collective-permute-start.3 = (f32[3,24,128]{2,1,0:T(8,128)S(1)}, f32[3,24,128]{2,1,0:T(8,128)S(1)}, u32[]{:S(2)}, u32[]{:S(2)}) collective-permute-start(f32[3,24,128]{2,1,0:T(8,128)S(1)} %get-tuple-element.19), channel_id=1, source_target_pairs={{0,12},{4,8},{8,4},{12,0},{1,13},{5,9},{9,5},{13,1},{2,14},{6,10},... | collective-permute-start | bytes 110600 | tf_op jit(solution)/shard_map/ppermute | solution.py:297
  21.4 1.1 shard_map.68.acc_ref
  22.5 0.9 collective-permute-done.2.xa_ref
  23.4 3.1 %collective-permute-done.3.xb_ref = f32[3,24,128]{2,1,0:T(8,128)S(1)} collective-permute-done((f32[3,24,128]{2,1,0:T(8,128)S(1)}, f32[3,24,128]{2,1,0:T(8,128)S(1)}, u32[]{:S(2)}, u32[]{:S(2)}) %collective-permute-start.3) | collective-permute-done | bytes 36896 | tf_op jit(solution)/shard_map/ppermute | solution.py:297
  26.5 0.0 collective-permute-done.za_ref
  26.5 0.0 collective-permute-done.1.zb_ref
  26.5 1.9 %shard_map.69.s_ref = bf16[4,3,144,128]{3,2,1,0:T(8,128)(2,1)} custom-call(s32[2]{0:T(128)S(1)} %pad_add_fusion.odd_ref, f32[3,144,128]{2,1,0:T(8,128)S(1)} %shard_map.68.acc_ref, f32[144,54]{1,0:T(8,128)S(1)} %get-tuple-element.15.cols_ref, f32[3,144,128]{2,1,0:T(8,128)S(1)} %collective-permute-done.za_ref, ...), custom_call_target="tpu_custom_call" | custom-call | tf_op jit(solution)/shard_map/pallas_call | solution.py:236
  28.5 3.5 %all-to-all-start = ((bf16[4,3,144,128]{3,2,1,0:T(8,128)(2,1)}), bf16[4,3,144,128]{3,2,1,0:T(8,128)(2,1)S(1)}, u32[]{:S(2)}, u32[]{:S(2)}) async-start(bf16[4,3,144,128]{3,2,1,0:T(8,128)(2,1)} %shard_map.69.s_ref), calls=%async_computation | async-start | bytes 884736 | tf_op jit(solution)/shard_map/all_to_all | solution.py:260
  32.0 0.0 copy-done.3
  32.0 0.1 reshape.68
  32.1 0.1 copy.15
  32.2 0.2 slice_reduce_fusion.1
  32.4 0.2 fusion.16
  32.6 0.2 fusion.12
  32.8 6.8 %all-to-all-done.refs_0_ = bf16[4,3,144,128]{3,2,1,0:T(8,128)(2,1)S(1)} async-done(((bf16[4,3,144,128]{3,2,1,0:T(8,128)(2,1)}), bf16[4,3,144,128]{3,2,1,0:T(8,128)(2,1)S(1)}, u32[]{:S(2)}, u32[]{:S(2)}) %all-to-all-start) | async-done | bytes 442400 | tf_op jit(solution)/shard_map/all_to_all | solution.py:260
  39.6 3.4 %shard_map.71 = f32[4,4,32,128]{3,2,1,0:T(8,128)S(1)} custom-call(bf16[4,3,144,128]{3,2,1,0:T(8,128)(2,1)S(1)} %all-to-all-done.refs_0_, f32[16,576]{1,0:T(8,128)S(1)} %pad_maximum_fusion.refs_1_), custom_call_target="tpu_custom_call" | custom-call | tf_op jit(solution)/shard_map/pallas_call | solution.py:236
  43.0 20.1 %all_to_all.25 = f32[16,32,128]{2,1,0:T(8,128)S(1)} all-to-all(f32[16,32,128]{2,1,0:T(8,128)S(1)} %bitcast.23), channel_id=1, replica_groups=mesh['zh'=3,'zl'=4,'yl'=4,'x'=4,'yh'=2,'c'=2] {'zl','yl'}, dimensions={0} | all-to-all | bytes 524288 | tf_op jit(solution)/shard_map/all_to_all | solution.py:260
  63.1 13.0 %all_to_all.26 = f32[3,32,128]{2,1,0:T(8,128)S(1)} all-to-all(f32[3,32,128]{2,1,0:T(8,128)S(1)} %broadcast_in_dim.4), channel_id=1, replica_groups=mesh['zh'=3,'zl'=4,'yl'=4,'x'=4,'yh'=2,'c'=2] {'zh'}, dimensions={0} | all-to-all | bytes 98304 | tf_op jit(solution)/shard_map/all_to_all | solution.py:260
  76.1 0.7 broadcast_in_dim.5
  76.8 5.6 %all-to-all-start.3 = ((bf16[16,32,128]{2,1,0:T(8,128)(2,1)}), bf16[16,32,128]{2,1,0:T(8,128)(2,1)S(1)}, u32[]{:S(2)}, u32[]{:S(2)}) async-start(bf16[16,32,128]{2,1,0:T(8,128)(2,1)} %broadcast_in_dim.5), calls=%async_computation.3 | async-start | bytes 262144 | tf_op jit(solution)/shard_map/all_to_all | solution.py:260
  82.4 0.0 copy-start
  82.4 1.6 %copy-done = bf16[1,4,2,4,4,64,64]{6,5,4,3,2,1,0:T(8,128)(2,1)S(1)} copy-done((bf16[1,4,2,4,4,64,64]{6,5,4,3,2,1,0:T(8,128)(2,1)S(1)}, bf16[1,4,2,4,4,64,64]{6,5,4,3,2,1,0:T(8,128)(2,1)}, u32[]{:S(2)}) %copy-start) | copy-done | bytes 1048600
  84.0 0.8 shard_map.72.b_ref
  84.8 9.4 %all-to-all-done.3 = bf16[16,32,128]{2,1,0:T(8,128)(2,1)S(1)} async-done(((bf16[16,32,128]{2,1,0:T(8,128)(2,1)}), bf16[16,32,128]{2,1,0:T(8,128)(2,1)S(1)}, u32[]{:S(2)}, u32[]{:S(2)}) %all-to-all-start.3) | async-done | bytes 131104 | tf_op jit(solution)/shard_map/all_to_all | solution.py:260
  94.2 2.5 %shard_map.73 = bf16[16,144,128]{2,1,0:T(8,128)(2,1)} custom-call(s32[1]{0:T(128)} %bitcast.6.tm_ref, bf16[4,4,32,128]{3,2,1,0:T(8,128)(2,1)S(1)} %bitcast.24, bf16[4,128,2048]{2,1,0:T(8,128)(2,1)S(1)} %shard_map.72.b_ref), custom_call_target="tpu_custom_call" | custom-call | tf_op jit(solution)/shard_map/pallas_call | solution.py:236
  96.7 5.0 %all-to-all-start.4 = ((bf16[16,144,128]{2,1,0:T(8,128)(2,1)}), bf16[16,144,128]{2,1,0:T(8,128)(2,1)S(1)}, u32[]{:S(2)}, u32[]{:S(2)}) async-start(bf16[16,144,128]{2,1,0:T(8,128)(2,1)} %shard_map.73), calls=%async_computation.4 | async-start | bytes 1179648 | tf_op jit(solution)/shard_map/all_to_all | solution.py:260
  101.7 1.8 %shard_map.70 = bf16[2,3,64,144]{3,2,1,0:T(8,128)(2,1)} custom-call(bf16[4,3,144,128]{3,2,1,0:T(8,128)(2,1)} %shard_map.69.s_ref), custom_call_target="tpu_custom_call" | custom-call | tf_op jit(solution)/shard_map/pallas_call | solution.py:236
  103.5 14.1 %all-to-all-done.4.r_ref = bf16[16,144,128]{2,1,0:T(8,128)(2,1)S(1)} async-done(((bf16[16,144,128]{2,1,0:T(8,128)(2,1)}), bf16[16,144,128]{2,1,0:T(8,128)(2,1)S(1)}, u32[]{:S(2)}, u32[]{:S(2)}) %all-to-all-start.4) | async-done | bytes 589856 | tf_op jit(solution)/shard_map/all_to_all | solution.py:260
  117.6 1.4 %shard_map.74 = (bf16[32,2,64,64]{3,2,1,0:T(8,128)(2,1)}, f32[2,4,32]{2,1,0:T(4,128)}) custom-call(bf16[16,144,128]{2,1,0:T(8,128)(2,1)S(1)} %all-to-all-done.4.r_ref), custom_call_target="tpu_custom_call" | custom-call | tf_op jit(solution)/shard_map/pallas_call | solution.py:236
  (6 shorter events, 0.1 us)
Async XLA Ops:
  0.6 31.3 %copy-start.3 = (s32[32,3]{0,1:T(4,128)S(1)}, s32[32,3]{0,1:T(4,128)}, u32[]{:S(2)}) copy-start(s32[32,3]{0,1:T(4,128)} %param.7) | copy-start | bytes 1156
  0.7 1.0 copy-start.1
  1.7 0.8 copy-start.2
  4.3 22.3 %collective-permute-start = (f32[3,144,128]{2,1,0:T(8,128)S(1)}, f32[3,144,128]{2,1,0:T(8,128)S(1)}, u32[]{:S(2)}, u32[]{:S(2)}) collective-permute-start(f32[3,144,128]{2,1,0:T(8,128)S(1)} %get-tuple-element.16), channel_id=1, source_target_pairs={{0,16},{16,0},{32,48},{48,32},{64,80},{80,64},{96,112},{112,96},{1... | collective-permute-start | bytes 663560 | tf_op jit(solution)/shard_map/ppermute | solution.py:294
  15.6 10.9 %collective-permute-start.1 = (f32[3,144,128]{2,1,0:T(8,128)S(1)}, f32[3,144,128]{2,1,0:T(8,128)S(1)}, u32[]{:S(2)}, u32[]{:S(2)}) collective-permute-start(f32[3,144,128]{2,1,0:T(8,128)S(1)} %get-tuple-element.17), channel_id=1, source_target_pairs={{0,752},{16,32},{32,16},{48,64},{64,48},{80,96},{96,80},{112,128},... | collective-permute-start | bytes 663560 | tf_op jit(solution)/shard_map/ppermute | solution.py:295
  17.5 5.9 %collective-permute-start.2 = (f32[3,24,128]{2,1,0:T(8,128)S(1)}, f32[3,24,128]{2,1,0:T(8,128)S(1)}, u32[]{:S(2)}, u32[]{:S(2)}) collective-permute-start(f32[3,24,128]{2,1,0:T(8,128)S(1)} %get-tuple-element.18), channel_id=1, source_target_pairs={{0,4},{4,0},{8,12},{12,8},{1,5},{5,1},{9,13},{13,9},{2,6},{6,2},{1... | collective-permute-start | bytes 110600 | tf_op jit(solution)/shard_map/ppermute | solution.py:296
  19.5 7.1 %collective-permute-start.3 = (f32[3,24,128]{2,1,0:T(8,128)S(1)}, f32[3,24,128]{2,1,0:T(8,128)S(1)}, u32[]{:S(2)}, u32[]{:S(2)}) collective-permute-start(f32[3,24,128]{2,1,0:T(8,128)S(1)} %get-tuple-element.19), channel_id=1, source_target_pairs={{0,12},{4,8},{8,4},{12,0},{1,13},{5,9},{9,5},{13,1},{2,14},{6,10},... | collective-permute-start | bytes 110600 | tf_op jit(solution)/shard_map/ppermute | solution.py:297
  28.5 11.1 %all-to-all-start = ((bf16[4,3,144,128]{3,2,1,0:T(8,128)(2,1)}), bf16[4,3,144,128]{3,2,1,0:T(8,128)(2,1)S(1)}, u32[]{:S(2)}, u32[]{:S(2)}) async-start(bf16[4,3,144,128]{3,2,1,0:T(8,128)(2,1)} %shard_map.69.s_ref), calls=%async_computation | async-start | bytes 884736 | tf_op jit(solution)/shard_map/all_to_all | solution.py:260
  76.8 17.5 %all-to-all-start.3 = ((bf16[16,32,128]{2,1,0:T(8,128)(2,1)}), bf16[16,32,128]{2,1,0:T(8,128)(2,1)S(1)}, u32[]{:S(2)}, u32[]{:S(2)}) async-start(bf16[16,32,128]{2,1,0:T(8,128)(2,1)} %broadcast_in_dim.5), calls=%async_computation.3 | async-start | bytes 262144 | tf_op jit(solution)/shard_map/all_to_all | solution.py:260
  82.4 1.6 %copy-start = (bf16[1,4,2,4,4,64,64]{6,5,4,3,2,1,0:T(8,128)(2,1)S(1)}, bf16[1,4,2,4,4,64,64]{6,5,4,3,2,1,0:T(8,128)(2,1)}, u32[]{:S(2)}) copy-start(bf16[1,4,2,4,4,64,64]{6,5,4,3,2,1,0:T(8,128)(2,1)} %param.6) | copy-start | bytes 3145732
  96.7 20.9 %all-to-all-start.4 = ((bf16[16,144,128]{2,1,0:T(8,128)(2,1)}), bf16[16,144,128]{2,1,0:T(8,128)(2,1)S(1)}, u32[]{:S(2)}, u32[]{:S(2)}) async-start(bf16[16,144,128]{2,1,0:T(8,128)(2,1)} %shard_map.73), calls=%async_computation.4 | async-start | bytes 1179648 | tf_op jit(solution)/shard_map/all_to_all | solution.py:260

commit v4 on v3

--- a/solution.py
+++ b/solution.py
@@ -122,32 +122,44 @@
         out_ref[1, c] = flat[64:].astype(BF16)
 
 
-def kernel_contract(s_ref, ph_ref, out_ref, wide_ref, spun_ref, *, scale):
-    lhs = []
+def kernel_contract(s_ref, ph_ref, out_ref, wide_ref, spun_ref, lhs_ref, rhs_ref, wave_ref, *, scale):
+    phase = ph_ref[...]
+    high = phase.astype(BF16)
+    rest = phase - high.astype(F32)
+    middle = rest.astype(BF16)
+    low = (rest - middle.astype(F32)).astype(BF16)
+    split = jnp.concatenate([high.astype(F32), middle.astype(F32), low.astype(F32)], axis=0).T.astype(BF16)
+    row = lax.broadcasted_iota(jnp.int32, (48, 256), 0) % 16
+    lane = lax.broadcasted_iota(jnp.int32, (48, 256), 1) // 128
+
+    def spread_phase(p):
+        ones = jnp.where(row == p + 8 * lane, 1.0, 0.0).astype(BF16)
+        wave_ref[p] = jnp.dot(split, ones, preferred_element_type=F32)
+
+    spread_phase(0)
     for k in range(4):
         for c in range(3):
             at = (k * 3 + c) * SITES
             wide = s_ref[k, c].astype(F32)
             wide_ref[at : at + SITES] = wide
             spun_ref[at : at + SITES] = turned(wide)
-            lhs.append(wide.T.astype(BF16))
-    lhs = jnp.concatenate(lhs, axis=1)
-    phase = ph_ref[...].T
+            lhs_ref[:, at : at + SITES] = wide.T.astype(BF16)
     sign = half_sign((64, 128), 1.0)
     for yl in range(4):
-        pair = []
         for pp in range(2):
             p = yl * 2 + pp
-            parts = []
+            if p < 7:
+                spread_phase(p + 1)
             for k in range(4):
-                cos = jnp.broadcast_to(phase[k * SITES : (k + 1) * SITES, p : p + 1], (SITES, 128))
-                sin = jnp.broadcast_to(phase[k * SITES : (k + 1) * SITES, 8 + p : 9 + p], (SITES, 128))
-                for c in range(3):
-                    at = (k * 3 + c) * SITES
-                    parts.append((wide_ref[at : at + SITES] * cos + spun_ref[at : at + SITES] * sin).astype(BF16))
-            pair.append(jnp.concatenate(parts, axis=0))
-        both = jnp.concatenate(pair, axis=1)
-        prod = jnp.dot(lhs, both, preferred_element_type=F32)
+                for r in range(0, SITES, 16):
+                    site = k * SITES + r
+                    cos = wave_ref[p, site : site + 16, :128]
+                    sin = wave_ref[p, site : site + 16, 128:]
+                    for c in range(3):
+                        at = (k * 3 + c) * SITES + r
+                        value = wide_ref[at : at + 16] * cos + spun_ref[at : at + 16] * sin
+                        rhs_ref[yl, at : at + 16, pp * 128 : (pp + 1) * 128] = value.astype(BF16)
+        prod = jnp.dot(lhs_ref[...], rhs_ref[yl], preferred_element_type=F32)
         for pp in range(2):
             block = prod[:, pp * 128 : (pp + 1) * 128]
             result = (block[:64] + roll(block[64:], 64, 1) * sign) * scale
@@ -283,7 +295,11 @@
     values, send_za, send_zb, send_xa, send_xb, cols = run(
         kernel_prepare,
         (site_shape, site_shape, site_shape, row_shape, row_shape, shape((SITES, 54), F32)),
-        (odd, field, links),
+        (
+            odd,
+            pltpu.with_memory_space_constraint(field, pltpu.HBM),
+            pltpu.with_memory_space_constraint(links, pltpu.HBM),
+        ),
         scratch=[
             pltpu.VMEM((6 * NEV, 1, SITES), F32),
             pltpu.VMEM((54, 1, SITES), F32),
@@ -319,7 +335,13 @@
         contract,
         shape((4, 4, 32, 128), F32),
         (shared, phase),
-        scratch=[pltpu.VMEM((12 * SITES, 128), F32), pltpu.VMEM((12 * SITES, 128), F32)],
+        scratch=[
+            pltpu.VMEM((12 * SITES, 128), F32),
+            pltpu.VMEM((12 * SITES, 128), F32),
+            pltpu.VMEM((128, 12 * SITES), BF16),
+            pltpu.VMEM((4, 12 * SITES, 256), BF16),
+            pltpu.VMEM((8, 4 * SITES, 256), F32),
+        ],
     )
     pieces = swap(partial.reshape(16, 32, 128), ("zl", "yl"))
     part = jnp.sum(pieces, axis=0)

time: 120 us -> 117 us (0.975)
  local copies, waits for them, and re-layouts: 4.47 us -> 2.66 us
    unnamed x8 -> x4, local copies, waits for them, and re-layouts: 3.4 us -> 1.59 us
where the time goes in v4:
time: 117 us
  waiting for transfers between devices  34.3 us (29%)
  blocking collectives  33.1 us (28%)
  starting transfers between devices  31.1 us (27%)
  Pallas kernels  14.2 us (12%)
  local copies, waits for them, and re-layouts  2.66 us (2%)
    all_to_all x2, blocking collectives, swap(): return lax.all_to_all(value, axes, split_axis=0, concat_axis=0, tiled=True)  33.1 us
    all_to_all x3, waiting for transfers between devices, swap(): return lax.all_to_all(value, axes, split_axis=0, concat_axis=0, tiled=True)  30.3 us
    pallas_call x8, Pallas kernels, run(): pl.pallas_call(kernel, out_shape=outs, in_specs=in_specs, out_specs=jax.t...  14.2 us
    all_to_all x3, starting transfers between devices, swap(): return lax.all_to_all(value, axes, split_axis=0, concat_axis=0, tiled=True)  14 us
    ppermute x1, starting transfers between devices, local(): recv_za = lax.ppermute(send_za, planes, pairs_a)  11.3 us
    ppermute x1, waiting for transfers between devices, local(): recv_xb = lax.ppermute(send_xb, 'x', ring_b)  3.14 us
  transfers between devices with their start and end apart: 7, of which 5 were waited for; matrix products, arithmetic and copies ran while one was open for 1% of the time, Pallas kernels for 3%

profile of v4, /device:TPU:8, one launch (start us, length us, event | category | flops | bytes accessed | tf_op | source)
XLA Modules:
  0.0 116.7 jit_solution(14485151924255356073)
XLA Ops:
  0.6 0.0 copy-start.1
  0.7 0.1 pad_add_fusion.odd_ref
  0.7 2.4 %shard_map.67 = (f32[3,144,128]{2,1,0:T(8,128)S(1)}, f32[3,144,128]{2,1,0:T(8,128)S(1)}, f32[3,144,128]{2,1,0:T(8,128)S(1)}, f32[3,24,128]{2,1,0:T(8,128)S(1)}, ...) custom-call(s32[2]{0:T(128)S(1)} %pad_add_fusion.odd_ref, f32[384,1,144]{2,1,0:T(1,128)} %bitcast.25, f32[54,1,144]{2,1,0:T(1,128)} %bitcast.29), custom_call_target="tpu_custom_call" | custom-call | tf_op jit(solution)/shard_map/pallas_call | solution.py:248
  3.1 11.3 %collective-permute-start = (f32[3,144,128]{2,1,0:T(8,128)S(1)}, f32[3,144,128]{2,1,0:T(8,128)S(1)}, u32[]{:S(2)}, u32[]{:S(2)}) collective-permute-start(f32[3,144,128]{2,1,0:T(8,128)S(1)} %get-tuple-element.16), channel_id=1, source_target_pairs={{0,16},{16,0},{32,48},{48,32},{64,80},{80,64},{96,112},{112,96},{1... | collective-permute-start | bytes 663560 | tf_op jit(solution)/shard_map/ppermute | solution.py:310
  14.5 1.9 %collective-permute-start.1 = (f32[3,144,128]{2,1,0:T(8,128)S(1)}, f32[3,144,128]{2,1,0:T(8,128)S(1)}, u32[]{:S(2)}, u32[]{:S(2)}) collective-permute-start(f32[3,144,128]{2,1,0:T(8,128)S(1)} %get-tuple-element.17), channel_id=1, source_target_pairs={{0,752},{16,32},{32,16},{48,64},{64,48},{80,96},{96,80},{112,128},... | collective-permute-start | bytes 663560 | tf_op jit(solution)/shard_map/ppermute | solution.py:311
  16.4 1.9 %collective-permute-start.2 = (f32[3,24,128]{2,1,0:T(8,128)S(1)}, f32[3,24,128]{2,1,0:T(8,128)S(1)}, u32[]{:S(2)}, u32[]{:S(2)}) collective-permute-start(f32[3,24,128]{2,1,0:T(8,128)S(1)} %get-tuple-element.18), channel_id=1, source_target_pairs={{0,4},{4,0},{8,12},{12,8},{1,5},{5,1},{9,13},{13,9},{2,6},{6,2},{1... | collective-permute-start | bytes 110600 | tf_op jit(solution)/shard_map/ppermute | solution.py:312
  18.3 1.9 %collective-permute-start.3 = (f32[3,24,128]{2,1,0:T(8,128)S(1)}, f32[3,24,128]{2,1,0:T(8,128)S(1)}, u32[]{:S(2)}, u32[]{:S(2)}) collective-permute-start(f32[3,24,128]{2,1,0:T(8,128)S(1)} %get-tuple-element.19), channel_id=1, source_target_pairs={{0,12},{4,8},{8,4},{12,0},{1,13},{5,9},{9,5},{13,1},{2,14},{6,10},... | collective-permute-start | bytes 110600 | tf_op jit(solution)/shard_map/ppermute | solution.py:313
  20.3 1.1 shard_map.68.acc_ref
  21.4 0.9 collective-permute-done.2.xa_ref
  22.2 3.1 %collective-permute-done.3.xb_ref = f32[3,24,128]{2,1,0:T(8,128)S(1)} collective-permute-done((f32[3,24,128]{2,1,0:T(8,128)S(1)}, f32[3,24,128]{2,1,0:T(8,128)S(1)}, u32[]{:S(2)}, u32[]{:S(2)}) %collective-permute-start.3) | collective-permute-done | bytes 36896 | tf_op jit(solution)/shard_map/ppermute | solution.py:313
  25.4 0.0 collective-permute-done.za_ref
  25.4 0.0 collective-permute-done.1.zb_ref
  25.4 1.9 %shard_map.69.s_ref = bf16[4,3,144,128]{3,2,1,0:T(8,128)(2,1)} custom-call(s32[2]{0:T(128)S(1)} %pad_add_fusion.odd_ref, f32[3,144,128]{2,1,0:T(8,128)S(1)} %shard_map.68.acc_ref, f32[144,54]{1,0:T(8,128)S(1)} %get-tuple-element.15.cols_ref, f32[3,144,128]{2,1,0:T(8,128)S(1)} %collective-permute-done.za_ref, ...), custom_call_target="tpu_custom_call" | custom-call | tf_op jit(solution)/shard_map/pallas_call | solution.py:248
  27.3 3.5 %all-to-all-start = ((bf16[4,3,144,128]{3,2,1,0:T(8,128)(2,1)}), bf16[4,3,144,128]{3,2,1,0:T(8,128)(2,1)S(1)}, u32[]{:S(2)}, u32[]{:S(2)}) async-start(bf16[4,3,144,128]{3,2,1,0:T(8,128)(2,1)} %shard_map.69.s_ref), calls=%async_computation | async-start | bytes 884736 | tf_op jit(solution)/shard_map/all_to_all | solution.py:272
  30.8 0.0 copy-done.1
  30.8 0.1 reshape.68
  30.9 0.1 copy.15
  31.0 0.2 slice_reduce_fusion.1
  31.2 0.2 fusion.16
  31.4 0.2 fusion.12
  31.6 6.8 %all-to-all-done.refs_0_ = bf16[4,3,144,128]{3,2,1,0:T(8,128)(2,1)S(1)} async-done(((bf16[4,3,144,128]{3,2,1,0:T(8,128)(2,1)}), bf16[4,3,144,128]{3,2,1,0:T(8,128)(2,1)S(1)}, u32[]{:S(2)}, u32[]{:S(2)}) %all-to-all-start) | async-done | bytes 442400 | tf_op jit(solution)/shard_map/all_to_all | solution.py:272
  38.4 2.3 %shard_map.71 = f32[4,4,32,128]{3,2,1,0:T(8,128)S(1)} custom-call(bf16[4,3,144,128]{3,2,1,0:T(8,128)(2,1)S(1)} %all-to-all-done.refs_0_, f32[16,576]{1,0:T(8,128)S(1)} %pad_maximum_fusion.refs_1_), custom_call_target="tpu_custom_call" | custom-call | tf_op jit(solution)/shard_map/pallas_call | solution.py:248
  40.7 20.1 %all_to_all.25 = f32[16,32,128]{2,1,0:T(8,128)S(1)} all-to-all(f32[16,32,128]{2,1,0:T(8,128)S(1)} %bitcast.23), channel_id=1, replica_groups=mesh['zh'=3,'zl'=4,'yl'=4,'x'=4,'yh'=2,'c'=2] {'zl','yl'}, dimensions={0} | all-to-all | bytes 524288 | tf_op jit(solution)/shard_map/all_to_all | solution.py:272
  60.8 13.0 %all_to_all.26 = f32[3,32,128]{2,1,0:T(8,128)S(1)} all-to-all(f32[3,32,128]{2,1,0:T(8,128)S(1)} %broadcast_in_dim.4), channel_id=1, replica_groups=mesh['zh'=3,'zl'=4,'yl'=4,'x'=4,'yh'=2,'c'=2] {'zh'}, dimensions={0} | all-to-all | bytes 98304 | tf_op jit(solution)/shard_map/all_to_all | solution.py:272
  73.8 0.7 broadcast_in_dim.5
  74.5 5.6 %all-to-all-start.3 = ((bf16[16,32,128]{2,1,0:T(8,128)(2,1)}), bf16[16,32,128]{2,1,0:T(8,128)(2,1)S(1)}, u32[]{:S(2)}, u32[]{:S(2)}) async-start(bf16[16,32,128]{2,1,0:T(8,128)(2,1)} %broadcast_in_dim.5), calls=%async_computation.3 | async-start | bytes 262144 | tf_op jit(solution)/shard_map/all_to_all | solution.py:272
  80.0 0.0 copy-start
  80.1 1.6 %copy-done = bf16[1,4,2,4,4,64,64]{6,5,4,3,2,1,0:T(8,128)(2,1)S(1)} copy-done((bf16[1,4,2,4,4,64,64]{6,5,4,3,2,1,0:T(8,128)(2,1)S(1)}, bf16[1,4,2,4,4,64,64]{6,5,4,3,2,1,0:T(8,128)(2,1)}, u32[]{:S(2)}) %copy-start) | copy-done | bytes 1048600
  81.6 0.8 shard_map.72.b_ref
  82.5 9.4 %all-to-all-done.3 = bf16[16,32,128]{2,1,0:T(8,128)(2,1)S(1)} async-done(((bf16[16,32,128]{2,1,0:T(8,128)(2,1)}), bf16[16,32,128]{2,1,0:T(8,128)(2,1)S(1)}, u32[]{:S(2)}, u32[]{:S(2)}) %all-to-all-start.3) | async-done | bytes 131104 | tf_op jit(solution)/shard_map/all_to_all | solution.py:272
  91.9 2.5 %shard_map.73 = bf16[16,144,128]{2,1,0:T(8,128)(2,1)} custom-call(s32[1]{0:T(128)} %bitcast.6.tm_ref, bf16[4,4,32,128]{3,2,1,0:T(8,128)(2,1)S(1)} %bitcast.24, bf16[4,128,2048]{2,1,0:T(8,128)(2,1)S(1)} %shard_map.72.b_ref), custom_call_target="tpu_custom_call" | custom-call | tf_op jit(solution)/shard_map/pallas_call | solution.py:248
  94.4 5.0 %all-to-all-start.4 = ((bf16[16,144,128]{2,1,0:T(8,128)(2,1)}), bf16[16,144,128]{2,1,0:T(8,128)(2,1)S(1)}, u32[]{:S(2)}, u32[]{:S(2)}) async-start(bf16[16,144,128]{2,1,0:T(8,128)(2,1)} %shard_map.73), calls=%async_computation.4 | async-start | bytes 1179648 | tf_op jit(solution)/shard_map/all_to_all | solution.py:272
  99.4 1.8 %shard_map.70 = bf16[2,3,64,144]{3,2,1,0:T(8,128)(2,1)} custom-call(bf16[4,3,144,128]{3,2,1,0:T(8,128)(2,1)} %shard_map.69.s_ref), custom_call_target="tpu_custom_call" | custom-call | tf_op jit(solution)/shard_map/pallas_call | solution.py:248
  101.2 14.1 %all-to-all-done.4.r_ref = bf16[16,144,128]{2,1,0:T(8,128)(2,1)S(1)} async-done(((bf16[16,144,128]{2,1,0:T(8,128)(2,1)}), bf16[16,144,128]{2,1,0:T(8,128)(2,1)S(1)}, u32[]{:S(2)}, u32[]{:S(2)}) %all-to-all-start.4) | async-done | bytes 589856 | tf_op jit(solution)/shard_map/all_to_all | solution.py:272
  115.3 1.4 %shard_map.74 = (bf16[32,2,64,64]{3,2,1,0:T(8,128)(2,1)}, f32[2,4,32]{2,1,0:T(4,128)}) custom-call(bf16[16,144,128]{2,1,0:T(8,128)(2,1)S(1)} %all-to-all-done.4.r_ref), custom_call_target="tpu_custom_call" | custom-call | tf_op jit(solution)/shard_map/pallas_call | solution.py:248
  (6 shorter events, 0.1 us)
Async XLA Ops:
  0.6 30.2 %copy-start.1 = (s32[32,3]{0,1:T(4,128)S(1)}, s32[32,3]{0,1:T(4,128)}, u32[]{:S(2)}) copy-start(s32[32,3]{0,1:T(4,128)} %param.7) | copy-start | bytes 1156
  3.1 22.3 %collective-permute-start = (f32[3,144,128]{2,1,0:T(8,128)S(1)}, f32[3,144,128]{2,1,0:T(8,128)S(1)}, u32[]{:S(2)}, u32[]{:S(2)}) collective-permute-start(f32[3,144,128]{2,1,0:T(8,128)S(1)} %get-tuple-element.16), channel_id=1, source_target_pairs={{0,16},{16,0},{32,48},{48,32},{64,80},{80,64},{96,112},{112,96},{1... | collective-permute-start | bytes 663560 | tf_op jit(solution)/shard_map/ppermute | solution.py:310
  14.5 10.9 %collective-permute-start.1 = (f32[3,144,128]{2,1,0:T(8,128)S(1)}, f32[3,144,128]{2,1,0:T(8,128)S(1)}, u32[]{:S(2)}, u32[]{:S(2)}) collective-permute-start(f32[3,144,128]{2,1,0:T(8,128)S(1)} %get-tuple-element.17), channel_id=1, source_target_pairs={{0,752},{16,32},{32,16},{48,64},{64,48},{80,96},{96,80},{112,128},... | collective-permute-start | bytes 663560 | tf_op jit(solution)/shard_map/ppermute | solution.py:311
  16.4 5.9 %collective-permute-start.2 = (f32[3,24,128]{2,1,0:T(8,128)S(1)}, f32[3,24,128]{2,1,0:T(8,128)S(1)}, u32[]{:S(2)}, u32[]{:S(2)}) collective-permute-start(f32[3,24,128]{2,1,0:T(8,128)S(1)} %get-tuple-element.18), channel_id=1, source_target_pairs={{0,4},{4,0},{8,12},{12,8},{1,5},{5,1},{9,13},{13,9},{2,6},{6,2},{1... | collective-permute-start | bytes 110600 | tf_op jit(solution)/shard_map/ppermute | solution.py:312
  18.3 7.1 %collective-permute-start.3 = (f32[3,24,128]{2,1,0:T(8,128)S(1)}, f32[3,24,128]{2,1,0:T(8,128)S(1)}, u32[]{:S(2)}, u32[]{:S(2)}) collective-permute-start(f32[3,24,128]{2,1,0:T(8,128)S(1)} %get-tuple-element.19), channel_id=1, source_target_pairs={{0,12},{4,8},{8,4},{12,0},{1,13},{5,9},{9,5},{13,1},{2,14},{6,10},... | collective-permute-start | bytes 110600 | tf_op jit(solution)/shard_map/ppermute | solution.py:313
  27.3 11.1 %all-to-all-start = ((bf16[4,3,144,128]{3,2,1,0:T(8,128)(2,1)}), bf16[4,3,144,128]{3,2,1,0:T(8,128)(2,1)S(1)}, u32[]{:S(2)}, u32[]{:S(2)}) async-start(bf16[4,3,144,128]{3,2,1,0:T(8,128)(2,1)} %shard_map.69.s_ref), calls=%async_computation | async-start | bytes 884736 | tf_op jit(solution)/shard_map/all_to_all | solution.py:272
  74.5 17.5 %all-to-all-start.3 = ((bf16[16,32,128]{2,1,0:T(8,128)(2,1)}), bf16[16,32,128]{2,1,0:T(8,128)(2,1)S(1)}, u32[]{:S(2)}, u32[]{:S(2)}) async-start(bf16[16,32,128]{2,1,0:T(8,128)(2,1)} %broadcast_in_dim.5), calls=%async_computation.3 | async-start | bytes 262144 | tf_op jit(solution)/shard_map/all_to_all | solution.py:272
  80.0 1.6 %copy-start = (bf16[1,4,2,4,4,64,64]{6,5,4,3,2,1,0:T(8,128)(2,1)S(1)}, bf16[1,4,2,4,4,64,64]{6,5,4,3,2,1,0:T(8,128)(2,1)}, u32[]{:S(2)}) copy-start(bf16[1,4,2,4,4,64,64]{6,5,4,3,2,1,0:T(8,128)(2,1)} %param.6) | copy-start | bytes 3145732
  94.4 20.9 %all-to-all-start.4 = ((bf16[16,144,128]{2,1,0:T(8,128)(2,1)}), bf16[16,144,128]{2,1,0:T(8,128)(2,1)S(1)}, u32[]{:S(2)}, u32[]{:S(2)}) async-start(bf16[16,144,128]{2,1,0:T(8,128)(2,1)} %shard_map.73), calls=%async_computation.4 | async-start | bytes 1179648 | tf_op jit(solution)/shard_map/all_to_all | solution.py:272

commit v5 on v4

--- a/solution.py
+++ b/solution.py
@@ -319,13 +319,10 @@
         (odd, inner, cols, recv_za, recv_zb, recv_xa, recv_xb),
         scalar=True,
     )
-    send, momenta, perambulators = lax.optimization_barrier((send, momenta, perambulators))
-    shared = swap(send, "x")
-    smeared = run(kernel_output, shape((2, 3, NEV, SITES), BF16), (send,))
     mine = lax.dynamic_index_in_dim(momenta.reshape(4, 4, 2, 3), x_index, 1, keepdims=False).reshape(8, 3)
     phase = phases(mine, z_index)
-    factors = run(kernel_factors, shape((4, 128, 16 * 128), BF16), (perambulators.reshape(4, 2, 16, NEV, NEV),))
-
+    send, phase = lax.optimization_barrier((send, phase))
+    shared = swap(send, "x")
     scale = 1.0 / math.sqrt(3.0 * NZ * LX * LX)
 
     def contract(*refs):
@@ -346,13 +343,18 @@
     pieces = swap(partial.reshape(16, 32, 128), ("zl", "yl"))
     part = jnp.sum(pieces, axis=0)
     part = jnp.sum(spread(part, "zh", 3), axis=0)
-    near = spread(part.astype(BF16), ("zl", "yh", "c"), 16).reshape(4, 4, 32, 128)
+    part, perambulators, send = lax.optimization_barrier((part.astype(BF16), perambulators, send))
+    near = spread(part, ("zl", "yh", "c"), 16).reshape(4, 4, 32, 128)
+    factors = run(kernel_factors, shape((4, 128, 16 * 128), BF16), (perambulators.reshape(4, 2, 16, NEV, NEV),))
+
+    smeared = run(kernel_output, shape((2, 3, NEV, SITES), BF16), (send,))
     payload = run(
         kernel_correlate,
         shape((16, 144, 128), BF16),
         (tm_index.astype(jnp.int32).reshape(1), near, factors),
         scalar=True,
     )
+    payload, smeared = lax.optimization_barrier((payload, smeared))
     everything = swap(payload, ("yl", "x"))
     elementals, correlator = run(kernel_unpack, (shape((32, 2, NEV, NEV), BF16), shape((2, 4, 32), F32)), (everything,))
     return (

time: 117 us -> 120 us (1.026)
  the two profiles are of different devices: /device:TPU:8 before, /device:TPU:1 now
where the time goes in v5:
time: 120 us; the launch traced here: 119 us
  blocking collectives  54.2 us (45%)
  starting transfers between devices  40 us (33%)
  Pallas kernels  11.5 us (10%)
  waiting for transfers between devices  9.09 us (8%)
  local copies, waits for them, and re-layouts  3.34 us (3%)
    all_to_all x4, blocking collectives, swap(): return lax.all_to_all(value, axes, split_axis=0, concat_axis=0, tiled=True)  54.2 us
    ppermute x1, starting transfers between devices, local(): recv_zb = lax.ppermute(send_zb, planes, pairs_b)  16.2 us
    all_to_all x1, starting transfers between devices, swap(): return lax.all_to_all(value, axes, split_axis=0, concat_axis=0, tiled=True)  12.9 us
    pallas_call x8, Pallas kernels, run(): pl.pallas_call(kernel, out_shape=outs, in_specs=in_specs, out_specs=jax.t...  11.5 us
    all_to_all x1, waiting for transfers between devices, swap(): return lax.all_to_all(value, axes, split_axis=0, concat_axis=0, tiled=True)  7.43 us
    ppermute x1, starting transfers between devices, local(): recv_xa = lax.ppermute(send_xa, 'x', ring_a)  3.94 us
    ppermute x1, starting transfers between devices, local(): recv_xb = lax.ppermute(send_xb, 'x', ring_b)  3.72 us
    ppermute x1, starting transfers between devices, local(): recv_za = lax.ppermute(send_za, planes, pairs_a)  3.2 us
  transfers between devices with their start and end apart: 5, of which 2 were waited for; matrix products, arithmetic and copies ran while one was open for 1% of the time, Pallas kernels for 2%

profile of v5, /device:TPU:1, one launch (start us, length us, event | category | flops | bytes accessed | tf_op | source)
XLA Modules:
  0.0 119.4 jit_solution(10506839054552362485)
XLA Ops:
  0.7 0.1 pad_add_fusion.odd_ref
  0.7 2.3 %shard_map.67 = (f32[3,144,128]{2,1,0:T(8,128)S(1)}, f32[3,144,128]{2,1,0:T(8,128)S(1)}, f32[3,144,128]{2,1,0:T(8,128)S(1)}, f32[3,24,128]{2,1,0:T(8,128)S(1)}, ...) custom-call(s32[2]{0:T(128)S(1)} %pad_add_fusion.odd_ref, f32[384,1,144]{2,1,0:T(1,128)} %bitcast.25, f32[54,1,144]{2,1,0:T(1,128)} %bitcast.29), custom_call_target="tpu_custom_call" | custom-call | tf_op jit(solution)/shard_map/pallas_call | solution.py:248
  3.1 3.9 %collective-permute-start.2 = (f32[3,24,128]{2,1,0:T(8,128)S(1)}, f32[3,24,128]{2,1,0:T(8,128)S(1)}, u32[]{:S(2)}, u32[]{:S(2)}) collective-permute-start(f32[3,24,128]{2,1,0:T(8,128)S(1)} %get-tuple-element.22), channel_id=1, source_target_pairs={{0,4},{4,0},{8,12},{12,8},{1,5},{5,1},{9,13},{13,9},{2,6},{6,2},{1... | collective-permute-start | bytes 110600 | tf_op jit(solution)/shard_map/ppermute | solution.py:312
  7.0 3.7 %collective-permute-start.3 = (f32[3,24,128]{2,1,0:T(8,128)S(1)}, f32[3,24,128]{2,1,0:T(8,128)S(1)}, u32[]{:S(2)}, u32[]{:S(2)}) collective-permute-start(f32[3,24,128]{2,1,0:T(8,128)S(1)} %get-tuple-element.23), channel_id=1, source_target_pairs={{0,12},{4,8},{8,4},{12,0},{1,13},{5,9},{9,5},{13,1},{2,14},{6,10},... | collective-permute-start | bytes 110600 | tf_op jit(solution)/shard_map/ppermute | solution.py:313
  10.7 3.2 %collective-permute-start = (f32[3,144,128]{2,1,0:T(8,128)S(1)}, f32[3,144,128]{2,1,0:T(8,128)S(1)}, u32[]{:S(2)}, u32[]{:S(2)}) collective-permute-start(f32[3,144,128]{2,1,0:T(8,128)S(1)} %get-tuple-element.20), channel_id=1, source_target_pairs={{0,16},{16,0},{32,48},{48,32},{64,80},{80,64},{96,112},{112,96},{1... | collective-permute-start | bytes 663560 | tf_op jit(solution)/shard_map/ppermute | solution.py:310
  14.0 16.2 %collective-permute-start.1 = (f32[3,144,128]{2,1,0:T(8,128)S(1)}, f32[3,144,128]{2,1,0:T(8,128)S(1)}, u32[]{:S(2)}, u32[]{:S(2)}) collective-permute-start(f32[3,144,128]{2,1,0:T(8,128)S(1)} %get-tuple-element.21), channel_id=1, source_target_pairs={{0,752},{16,32},{32,16},{48,64},{64,48},{80,96},{96,80},{112,128},... | collective-permute-start | bytes 663560 | tf_op jit(solution)/shard_map/ppermute | solution.py:311
  30.2 0.8 reshape.65
  31.0 0.1 copy.15
  31.1 0.2 slice_reduce_fusion.1
  31.3 0.2 fusion.16
  31.5 0.2 fusion.12
  31.7 1.1 shard_map.68.acc_ref
  32.8 0.0 collective-permute-done.2.xa_ref
  32.8 0.0 collective-permute-done.3.xb_ref
  32.8 0.0 collective-permute-done.za_ref
  32.8 1.7 %collective-permute-done.1.zb_ref = f32[3,144,128]{2,1,0:T(8,128)S(1)} collective-permute-done((f32[3,144,128]{2,1,0:T(8,128)S(1)}, f32[3,144,128]{2,1,0:T(8,128)S(1)}, u32[]{:S(2)}, u32[]{:S(2)}) %collective-permute-start.1) | collective-permute-done | bytes 221216 | tf_op jit(solution)/shard_map/ppermute | solution.py:311
  34.4 1.2 shard_map.69.s_ref
  35.6 8.9 %all_to_all.25.refs_0_ = bf16[4,3,144,128]{3,2,1,0:T(8,128)(2,1)S(1)} all-to-all(bf16[4,3,144,128]{3,2,1,0:T(8,128)(2,1)S(1)} %shard_map.69.s_ref), channel_id=1, replica_groups=mesh['zh'=3,'zl'=4,'yl'=4,'x'=4,'yh'=2,'c'=2] {'x'}, dimensions={0} | all-to-all | bytes 884736 | tf_op jit(solution)/shard_map/all_to_all | solution.py:272
  44.5 2.3 %shard_map.70 = f32[4,4,32,128]{3,2,1,0:T(8,128)S(1)} custom-call(bf16[4,3,144,128]{3,2,1,0:T(8,128)(2,1)S(1)} %all_to_all.25.refs_0_, f32[16,576]{1,0:T(8,128)S(1)} %pad_maximum_fusion.refs_1_), custom_call_target="tpu_custom_call" | custom-call | tf_op jit(solution)/shard_map/pallas_call | solution.py:248
  46.8 11.1 %all_to_all.26 = f32[16,32,128]{2,1,0:T(8,128)S(1)} all-to-all(f32[16,32,128]{2,1,0:T(8,128)S(1)} %bitcast.23), channel_id=1, replica_groups=mesh['zh'=3,'zl'=4,'yl'=4,'x'=4,'yh'=2,'c'=2] {'zl','yl'}, dimensions={0} | all-to-all | bytes 524288 | tf_op jit(solution)/shard_map/all_to_all | solution.py:272
  57.9 14.8 %all_to_all.27 = f32[3,32,128]{2,1,0:T(8,128)S(1)} all-to-all(f32[3,32,128]{2,1,0:T(8,128)S(1)} %broadcast_in_dim.4), channel_id=1, replica_groups=mesh['zh'=3,'zl'=4,'yl'=4,'x'=4,'yh'=2,'c'=2] {'zh'}, dimensions={0} | all-to-all | bytes 98304 | tf_op jit(solution)/shard_map/all_to_all | solution.py:272
  72.7 0.7 broadcast_in_dim.5
  73.4 12.9 %all-to-all-start.3 = ((bf16[16,32,128]{2,1,0:T(8,128)(2,1)}), bf16[16,32,128]{2,1,0:T(8,128)(2,1)S(1)}, u32[]{:S(2)}, u32[]{:S(2)}) async-start(bf16[16,32,128]{2,1,0:T(8,128)(2,1)} %broadcast_in_dim.5), calls=%async_computation.3 | async-start | bytes 262144 | tf_op jit(solution)/shard_map/all_to_all | solution.py:272
  86.3 0.8 shard_map.73
  87.1 0.0 copy-start
  87.1 1.6 %copy-done = bf16[1,4,2,4,4,64,64]{6,5,4,3,2,1,0:T(8,128)(2,1)S(1)} copy-done((bf16[1,4,2,4,4,64,64]{6,5,4,3,2,1,0:T(8,128)(2,1)S(1)}, bf16[1,4,2,4,4,64,64]{6,5,4,3,2,1,0:T(8,128)(2,1)}, u32[]{:S(2)}) %copy-start) | copy-done | bytes 1048600
  88.7 0.8 shard_map.71.b_ref
  89.5 7.4 %all-to-all-done.3 = bf16[16,32,128]{2,1,0:T(8,128)(2,1)S(1)} async-done(((bf16[16,32,128]{2,1,0:T(8,128)(2,1)}), bf16[16,32,128]{2,1,0:T(8,128)(2,1)S(1)}, u32[]{:S(2)}, u32[]{:S(2)}) %all-to-all-start.3) | async-done | bytes 131104 | tf_op jit(solution)/shard_map/all_to_all | solution.py:272
  97.0 1.7 %shard_map.72 = bf16[16,144,128]{2,1,0:T(8,128)(2,1)S(1)} custom-call(s32[1]{0:T(128)} %bitcast.tm_ref, bf16[4,4,32,128]{3,2,1,0:T(8,128)(2,1)S(1)} %bitcast.24, bf16[4,128,2048]{2,1,0:T(8,128)(2,1)S(1)} %shard_map.71.b_ref), custom_call_target="tpu_custom_call" | custom-call | tf_op jit(solution)/shard_map/pallas_call | solution.py:248
  98.6 19.4 %all_to_all.28.r_ref = bf16[16,144,128]{2,1,0:T(8,128)(2,1)S(1)} all-to-all(bf16[16,144,128]{2,1,0:T(8,128)(2,1)S(1)} %shard_map.72), channel_id=1, replica_groups=mesh['zh'=3,'zl'=4,'yl'=4,'x'=4,'yh'=2,'c'=2] {'yl','x'}, dimensions={0} | all-to-all | bytes 1179648 | tf_op jit(solution)/shard_map/all_to_all | solution.py:272
  118.1 1.4 %shard_map.74 = (bf16[32,2,64,64]{3,2,1,0:T(8,128)(2,1)}, f32[2,4,32]{2,1,0:T(4,128)}) custom-call(bf16[16,144,128]{2,1,0:T(8,128)(2,1)S(1)} %all_to_all.28.r_ref), custom_call_target="tpu_custom_call" | custom-call | tf_op jit(solution)/shard_map/pallas_call | solution.py:248
  (6 shorter events, 0.1 us)
Async XLA Ops:
  3.1 29.7 %collective-permute-start.2 = (f32[3,24,128]{2,1,0:T(8,128)S(1)}, f32[3,24,128]{2,1,0:T(8,128)S(1)}, u32[]{:S(2)}, u32[]{:S(2)}) collective-permute-start(f32[3,24,128]{2,1,0:T(8,128)S(1)} %get-tuple-element.22), channel_id=1, source_target_pairs={{0,4},{4,0},{8,12},{12,8},{1,5},{5,1},{9,13},{13,9},{2,6},{6,2},{1... | collective-permute-start | bytes 110600 | tf_op jit(solution)/shard_map/ppermute | solution.py:312
  7.0 25.8 %collective-permute-start.3 = (f32[3,24,128]{2,1,0:T(8,128)S(1)}, f32[3,24,128]{2,1,0:T(8,128)S(1)}, u32[]{:S(2)}, u32[]{:S(2)}) collective-permute-start(f32[3,24,128]{2,1,0:T(8,128)S(1)} %get-tuple-element.23), channel_id=1, source_target_pairs={{0,12},{4,8},{8,4},{12,0},{1,13},{5,9},{9,5},{13,1},{2,14},{6,10},... | collective-permute-start | bytes 110600 | tf_op jit(solution)/shard_map/ppermute | solution.py:313
  10.7 22.1 %collective-permute-start = (f32[3,144,128]{2,1,0:T(8,128)S(1)}, f32[3,144,128]{2,1,0:T(8,128)S(1)}, u32[]{:S(2)}, u32[]{:S(2)}) collective-permute-start(f32[3,144,128]{2,1,0:T(8,128)S(1)} %get-tuple-element.20), channel_id=1, source_target_pairs={{0,16},{16,0},{32,48},{48,32},{64,80},{80,64},{96,112},{112,96},{1... | collective-permute-start | bytes 663560 | tf_op jit(solution)/shard_map/ppermute | solution.py:310
  14.0 20.5 %collective-permute-start.1 = (f32[3,144,128]{2,1,0:T(8,128)S(1)}, f32[3,144,128]{2,1,0:T(8,128)S(1)}, u32[]{:S(2)}, u32[]{:S(2)}) collective-permute-start(f32[3,144,128]{2,1,0:T(8,128)S(1)} %get-tuple-element.21), channel_id=1, source_target_pairs={{0,752},{16,32},{32,16},{48,64},{64,48},{80,96},{96,80},{112,128},... | collective-permute-start | bytes 663560 | tf_op jit(solution)/shard_map/ppermute | solution.py:311
  73.4 23.6 %all-to-all-start.3 = ((bf16[16,32,128]{2,1,0:T(8,128)(2,1)}), bf16[16,32,128]{2,1,0:T(8,128)(2,1)S(1)}, u32[]{:S(2)}, u32[]{:S(2)}) async-start(bf16[16,32,128]{2,1,0:T(8,128)(2,1)} %broadcast_in_dim.5), calls=%async_computation.3 | async-start | bytes 262144 | tf_op jit(solution)/shard_map/all_to_all | solution.py:272
  87.1 1.6 %copy-start = (bf16[1,4,2,4,4,64,64]{6,5,4,3,2,1,0:T(8,128)(2,1)S(1)}, bf16[1,4,2,4,4,64,64]{6,5,4,3,2,1,0:T(8,128)(2,1)}, u32[]{:S(2)}) copy-start(bf16[1,4,2,4,4,64,64]{6,5,4,3,2,1,0:T(8,128)(2,1)} %param.6) | copy-start | bytes 3145732

commit v6 on v5

--- a/solution.py
+++ b/solution.py
@@ -145,9 +145,9 @@
             spun_ref[at : at + SITES] = turned(wide)
             lhs_ref[:, at : at + SITES] = wide.T.astype(BF16)
     sign = half_sign((64, 128), 1.0)
-    for yl in range(4):
-        for pp in range(2):
-            p = yl * 2 + pp
+    for pair in range(4):
+        for pp in range(2):
+            p = pair * 2 + pp
             if p < 7:
                 spread_phase(p + 1)
             for k in range(4):
@@ -158,13 +158,13 @@
                     for c in range(3):
                         at = (k * 3 + c) * SITES + r
                         value = wide_ref[at : at + 16] * cos + spun_ref[at : at + 16] * sin
-                        rhs_ref[yl, at : at + 16, pp * 128 : (pp + 1) * 128] = value.astype(BF16)
-        prod = jnp.dot(lhs_ref[...], rhs_ref[yl], preferred_element_type=F32)
+                        rhs_ref[pair, at : at + 16, pp * 128 : (pp + 1) * 128] = value.astype(BF16)
+        prod = jnp.dot(lhs_ref[...], rhs_ref[pair], preferred_element_type=F32)
         for pp in range(2):
             block = prod[:, pp * 128 : (pp + 1) * 128]
             result = (block[:64] + roll(block[64:], 64, 1) * sign) * scale
-            out_ref[pp * 2, yl] = result[:32]
-            out_ref[pp * 2 + 1, yl] = result[32:]
+            out_ref[pair, pp * 2] = result[:32]
+            out_ref[pair, pp * 2 + 1] = result[32:]
 
 
 def kernel_factors(p_ref, out_ref):
@@ -344,7 +344,7 @@
     part = jnp.sum(pieces, axis=0)
     part = jnp.sum(spread(part, "zh", 3), axis=0)
     part, perambulators, send = lax.optimization_barrier((part.astype(BF16), perambulators, send))
-    near = spread(part, ("zl", "yh", "c"), 16).reshape(4, 4, 32, 128)
+    near = spread(part, ("yl", "yh", "c"), 16).reshape(4, 4, 32, 128)
     factors = run(kernel_factors, shape((4, 128, 16 * 128), BF16), (perambulators.reshape(4, 2, 16, NEV, NEV),))
 
     smeared = run(kernel_output, shape((2, 3, NEV, SITES), BF16), (send,))
@@ -355,7 +355,7 @@
         scalar=True,
     )
     payload, smeared = lax.optimization_barrier((payload, smeared))
-    everything = swap(payload, ("yl", "x"))
+    everything = swap(payload, ("zl", "x"))
     elementals, correlator = run(kernel_unpack, (shape((32, 2, NEV, NEV), BF16), shape((2, 4, 32), F32)), (everything,))
     return (
         smeared.reshape(1, 2, 3, NEV, 1, SITES),

time: 120 us -> 118 us (0.983)
  waiting for transfers between devices: 9.09 us -> 7.44 us
    all_to_all x1, waiting for transfers between devices: 7.43 us -> 5.79 us  [swap(): return lax.all_to_all(value, axes, split_axis=0, concat_axis=0, tiled=True)]
where the time goes in v6:
time: 118 us
  blocking collectives  55.2 us (47%)
  starting transfers between devices  38.9 us (33%)
  Pallas kernels  11.5 us (10%)
  waiting for transfers between devices  7.44 us (6%)
  local copies, waits for them, and re-layouts  3.34 us (3%)
    all_to_all x4, blocking collectives, swap(): return lax.all_to_all(value, axes, split_axis=0, concat_axis=0, tiled=True)  55.2 us
    ppermute x1, starting transfers between devices, local(): recv_zb = lax.ppermute(send_zb, planes, pairs_b)  16.2 us
    all_to_all x1, starting transfers between devices, swap(): return lax.all_to_all(value, axes, split_axis=0, concat_axis=0, tiled=True)  11.8 us
    pallas_call x8, Pallas kernels, run(): pl.pallas_call(kernel, out_shape=outs, in_specs=in_specs, out_specs=jax.t...  11.5 us
    all_to_all x1, waiting for transfers between devices, swap(): return lax.all_to_all(value, axes, split_axis=0, concat_axis=0, tiled=True)  5.79 us
    ppermute x1, starting transfers between devices, local(): recv_xa = lax.ppermute(send_xa, 'x', ring_a)  3.94 us
    ppermute x1, starting transfers between devices, local(): recv_xb = lax.ppermute(send_xb, 'x', ring_b)  3.72 us
    ppermute x1, starting transfers between devices, local(): recv_za = lax.ppermute(send_za, planes, pairs_a)  3.2 us
  transfers between devices with their start and end apart: 5, of which 2 were waited for; matrix products, arithmetic and copies ran while one was open for 1% of the time, Pallas kernels for 2%

profile of v6, /device:TPU:1, one launch (start us, length us, event | category | flops | bytes accessed | tf_op | source)
XLA Modules:
  0.0 117.8 jit_solution(12751360600818899483)
XLA Ops:
  0.7 0.1 pad_add_fusion.odd_ref
  0.7 2.3 %shard_map.67 = (f32[3,144,128]{2,1,0:T(8,128)S(1)}, f32[3,144,128]{2,1,0:T(8,128)S(1)}, f32[3,144,128]{2,1,0:T(8,128)S(1)}, f32[3,24,128]{2,1,0:T(8,128)S(1)}, ...) custom-call(s32[2]{0:T(128)S(1)} %pad_add_fusion.odd_ref, f32[384,1,144]{2,1,0:T(1,128)} %bitcast.25, f32[54,1,144]{2,1,0:T(1,128)} %bitcast.29), custom_call_target="tpu_custom_call" | custom-call | tf_op jit(solution)/shard_map/pallas_call | solution.py:248
  3.1 3.9 %collective-permute-start.2 = (f32[3,24,128]{2,1,0:T(8,128)S(1)}, f32[3,24,128]{2,1,0:T(8,128)S(1)}, u32[]{:S(2)}, u32[]{:S(2)}) collective-permute-start(f32[3,24,128]{2,1,0:T(8,128)S(1)} %get-tuple-element.22), channel_id=1, source_target_pairs={{0,4},{4,0},{8,12},{12,8},{1,5},{5,1},{9,13},{13,9},{2,6},{6,2},{1... | collective-permute-start | bytes 110600 | tf_op jit(solution)/shard_map/ppermute | solution.py:312
  7.0 3.7 %collective-permute-start.3 = (f32[3,24,128]{2,1,0:T(8,128)S(1)}, f32[3,24,128]{2,1,0:T(8,128)S(1)}, u32[]{:S(2)}, u32[]{:S(2)}) collective-permute-start(f32[3,24,128]{2,1,0:T(8,128)S(1)} %get-tuple-element.23), channel_id=1, source_target_pairs={{0,12},{4,8},{8,4},{12,0},{1,13},{5,9},{9,5},{13,1},{2,14},{6,10},... | collective-permute-start | bytes 110600 | tf_op jit(solution)/shard_map/ppermute | solution.py:313
  10.7 3.2 %collective-permute-start = (f32[3,144,128]{2,1,0:T(8,128)S(1)}, f32[3,144,128]{2,1,0:T(8,128)S(1)}, u32[]{:S(2)}, u32[]{:S(2)}) collective-permute-start(f32[3,144,128]{2,1,0:T(8,128)S(1)} %get-tuple-element.20), channel_id=1, source_target_pairs={{0,16},{16,0},{32,48},{48,32},{64,80},{80,64},{96,112},{112,96},{1... | collective-permute-start | bytes 663560 | tf_op jit(solution)/shard_map/ppermute | solution.py:310
  14.0 16.2 %collective-permute-start.1 = (f32[3,144,128]{2,1,0:T(8,128)S(1)}, f32[3,144,128]{2,1,0:T(8,128)S(1)}, u32[]{:S(2)}, u32[]{:S(2)}) collective-permute-start(f32[3,144,128]{2,1,0:T(8,128)S(1)} %get-tuple-element.21), channel_id=1, source_target_pairs={{0,752},{16,32},{32,16},{48,64},{64,48},{80,96},{96,80},{112,128},... | collective-permute-start | bytes 663560 | tf_op jit(solution)/shard_map/ppermute | solution.py:311
  30.2 0.8 reshape.65
  31.0 0.1 copy.15
  31.1 0.2 slice_reduce_fusion.1
  31.3 0.2 fusion.16
  31.5 0.2 fusion.12
  31.7 1.1 shard_map.68.acc_ref
  32.8 0.0 collective-permute-done.2.xa_ref
  32.8 0.0 collective-permute-done.3.xb_ref
  32.8 0.0 collective-permute-done.za_ref
  32.8 1.7 %collective-permute-done.1.zb_ref = f32[3,144,128]{2,1,0:T(8,128)S(1)} collective-permute-done((f32[3,144,128]{2,1,0:T(8,128)S(1)}, f32[3,144,128]{2,1,0:T(8,128)S(1)}, u32[]{:S(2)}, u32[]{:S(2)}) %collective-permute-start.1) | collective-permute-done | bytes 221216 | tf_op jit(solution)/shard_map/ppermute | solution.py:311
  34.4 1.2 shard_map.69.s_ref
  35.6 8.9 %all_to_all.25.refs_0_ = bf16[4,3,144,128]{3,2,1,0:T(8,128)(2,1)S(1)} all-to-all(bf16[4,3,144,128]{3,2,1,0:T(8,128)(2,1)S(1)} %shard_map.69.s_ref), channel_id=1, replica_groups=mesh['zh'=3,'zl'=4,'yl'=4,'x'=4,'yh'=2,'c'=2] {'x'}, dimensions={0} | all-to-all | bytes 884736 | tf_op jit(solution)/shard_map/all_to_all | solution.py:272
  44.5 2.3 %shard_map.70 = f32[4,4,32,128]{3,2,1,0:T(8,128)S(1)} custom-call(bf16[4,3,144,128]{3,2,1,0:T(8,128)(2,1)S(1)} %all_to_all.25.refs_0_, f32[16,576]{1,0:T(8,128)S(1)} %pad_maximum_fusion.refs_1_), custom_call_target="tpu_custom_call" | custom-call | tf_op jit(solution)/shard_map/pallas_call | solution.py:248
  46.8 11.1 %all_to_all.26 = f32[16,32,128]{2,1,0:T(8,128)S(1)} all-to-all(f32[16,32,128]{2,1,0:T(8,128)S(1)} %bitcast.23), channel_id=1, replica_groups=mesh['zh'=3,'zl'=4,'yl'=4,'x'=4,'yh'=2,'c'=2] {'zl','yl'}, dimensions={0} | all-to-all | bytes 524288 | tf_op jit(solution)/shard_map/all_to_all | solution.py:272
  57.9 14.8 %all_to_all.27 = f32[3,32,128]{2,1,0:T(8,128)S(1)} all-to-all(f32[3,32,128]{2,1,0:T(8,128)S(1)} %broadcast_in_dim.4), channel_id=1, replica_groups=mesh['zh'=3,'zl'=4,'yl'=4,'x'=4,'yh'=2,'c'=2] {'zh'}, dimensions={0} | all-to-all | bytes 98304 | tf_op jit(solution)/shard_map/all_to_all | solution.py:272
  72.7 0.7 broadcast_in_dim.5
  73.4 11.8 %all-to-all-start.3 = ((bf16[16,32,128]{2,1,0:T(8,128)(2,1)}), bf16[16,32,128]{2,1,0:T(8,128)(2,1)S(1)}, u32[]{:S(2)}, u32[]{:S(2)}) async-start(bf16[16,32,128]{2,1,0:T(8,128)(2,1)} %broadcast_in_dim.5), calls=%async_computation.3 | async-start | bytes 262144 | tf_op jit(solution)/shard_map/all_to_all | solution.py:272
  85.2 0.8 shard_map.73
  86.0 0.0 copy-start
  86.0 1.6 %copy-done = bf16[1,4,2,4,4,64,64]{6,5,4,3,2,1,0:T(8,128)(2,1)S(1)} copy-done((bf16[1,4,2,4,4,64,64]{6,5,4,3,2,1,0:T(8,128)(2,1)S(1)}, bf16[1,4,2,4,4,64,64]{6,5,4,3,2,1,0:T(8,128)(2,1)}, u32[]{:S(2)}) %copy-start) | copy-done | bytes 1048600
  87.6 0.8 shard_map.71.b_ref
  88.4 5.8 %all-to-all-done.3 = bf16[16,32,128]{2,1,0:T(8,128)(2,1)S(1)} async-done(((bf16[16,32,128]{2,1,0:T(8,128)(2,1)}), bf16[16,32,128]{2,1,0:T(8,128)(2,1)S(1)}, u32[]{:S(2)}, u32[]{:S(2)}) %all-to-all-start.3) | async-done | bytes 131104 | tf_op jit(solution)/shard_map/all_to_all | solution.py:272
  94.2 1.7 %shard_map.72 = bf16[16,144,128]{2,1,0:T(8,128)(2,1)S(1)} custom-call(s32[1]{0:T(128)} %bitcast.tm_ref, bf16[4,4,32,128]{3,2,1,0:T(8,128)(2,1)S(1)} %bitcast.24, bf16[4,128,2048]{2,1,0:T(8,128)(2,1)S(1)} %shard_map.71.b_ref), custom_call_target="tpu_custom_call" | custom-call | tf_op jit(solution)/shard_map/pallas_call | solution.py:248
  95.9 20.5 %all_to_all.28.r_ref = bf16[16,144,128]{2,1,0:T(8,128)(2,1)S(1)} all-to-all(bf16[16,144,128]{2,1,0:T(8,128)(2,1)S(1)} %shard_map.72), channel_id=1, replica_groups=mesh['zh'=3,'zl'=4,'yl'=4,'x'=4,'yh'=2,'c'=2] {'zl','x'}, dimensions={0} | all-to-all | bytes 1179648 | tf_op jit(solution)/shard_map/all_to_all | solution.py:272
  116.4 1.4 %shard_map.74 = (bf16[32,2,64,64]{3,2,1,0:T(8,128)(2,1)}, f32[2,4,32]{2,1,0:T(4,128)}) custom-call(bf16[16,144,128]{2,1,0:T(8,128)(2,1)S(1)} %all_to_all.28.r_ref), custom_call_target="tpu_custom_call" | custom-call | tf_op jit(solution)/shard_map/pallas_call | solution.py:248
  (6 shorter events, 0.1 us)
Async XLA Ops:
  3.1 29.7 %collective-permute-start.2 = (f32[3,24,128]{2,1,0:T(8,128)S(1)}, f32[3,24,128]{2,1,0:T(8,128)S(1)}, u32[]{:S(2)}, u32[]{:S(2)}) collective-permute-start(f32[3,24,128]{2,1,0:T(8,128)S(1)} %get-tuple-element.22), channel_id=1, source_target_pairs={{0,4},{4,0},{8,12},{12,8},{1,5},{5,1},{9,13},{13,9},{2,6},{6,2},{1... | collective-permute-start | bytes 110600 | tf_op jit(solution)/shard_map/ppermute | solution.py:312
  7.0 25.8 %collective-permute-start.3 = (f32[3,24,128]{2,1,0:T(8,128)S(1)}, f32[3,24,128]{2,1,0:T(8,128)S(1)}, u32[]{:S(2)}, u32[]{:S(2)}) collective-permute-start(f32[3,24,128]{2,1,0:T(8,128)S(1)} %get-tuple-element.23), channel_id=1, source_target_pairs={{0,12},{4,8},{8,4},{12,0},{1,13},{5,9},{9,5},{13,1},{2,14},{6,10},... | collective-permute-start | bytes 110600 | tf_op jit(solution)/shard_map/ppermute | solution.py:313
  10.7 22.1 %collective-permute-start = (f32[3,144,128]{2,1,0:T(8,128)S(1)}, f32[3,144,128]{2,1,0:T(8,128)S(1)}, u32[]{:S(2)}, u32[]{:S(2)}) collective-permute-start(f32[3,144,128]{2,1,0:T(8,128)S(1)} %get-tuple-element.20), channel_id=1, source_target_pairs={{0,16},{16,0},{32,48},{48,32},{64,80},{80,64},{96,112},{112,96},{1... | collective-permute-start | bytes 663560 | tf_op jit(solution)/shard_map/ppermute | solution.py:310
  14.0 20.5 %collective-permute-start.1 = (f32[3,144,128]{2,1,0:T(8,128)S(1)}, f32[3,144,128]{2,1,0:T(8,128)S(1)}, u32[]{:S(2)}, u32[]{:S(2)}) collective-permute-start(f32[3,144,128]{2,1,0:T(8,128)S(1)} %get-tuple-element.21), channel_id=1, source_target_pairs={{0,752},{16,32},{32,16},{48,64},{64,48},{80,96},{96,80},{112,128},... | collective-permute-start | bytes 663560 | tf_op jit(solution)/shard_map/ppermute | solution.py:311
  73.4 20.9 %all-to-all-start.3 = ((bf16[16,32,128]{2,1,0:T(8,128)(2,1)}), bf16[16,32,128]{2,1,0:T(8,128)(2,1)S(1)}, u32[]{:S(2)}, u32[]{:S(2)}) async-start(bf16[16,32,128]{2,1,0:T(8,128)(2,1)} %broadcast_in_dim.5), calls=%async_computation.3 | async-start | bytes 262144 | tf_op jit(solution)/shard_map/all_to_all | solution.py:272
  86.0 1.6 %copy-start = (bf16[1,4,2,4,4,64,64]{6,5,4,3,2,1,0:T(8,128)(2,1)S(1)}, bf16[1,4,2,4,4,64,64]{6,5,4,3,2,1,0:T(8,128)(2,1)}, u32[]{:S(2)}) copy-start(bf16[1,4,2,4,4,64,64]{6,5,4,3,2,1,0:T(8,128)(2,1)} %param.6) | copy-start | bytes 3145732

commit v7 on v6

--- a/solution.py
+++ b/solution.py
@@ -163,8 +163,9 @@
         for pp in range(2):
             block = prod[:, pp * 128 : (pp + 1) * 128]
             result = (block[:64] + roll(block[64:], 64, 1) * sign) * scale
-            out_ref[pair, pp * 2] = result[:32]
-            out_ref[pair, pp * 2 + 1] = result[32:]
+            z_at = pp * 2 + pair // 2
+            out_ref[z_at, pair % 2] = result[:32]
+            out_ref[z_at, 2 + pair % 2] = result[32:]
 
 
 def kernel_factors(p_ref, out_ref):
@@ -277,7 +278,7 @@
 
 
 def local(eigvecs, gauge_links, perambulators, momenta):
-    planes = ("zh", "zl", "yl")
+    planes = ("zh", "zu", "zd", "yu", "yd")
     pairs_a = [(i, i ^ 1) for i in range(NZ)]
     pairs_b = [(i, ((i + 1) ^ 1) - 1) for i in range(NZ)]
     pairs_b = [(i, j % NZ) for i, j in pairs_b]
@@ -286,7 +287,7 @@
     z_index = lax.axis_index(planes)
     x_index = lax.axis_index("x")
     tm_index = lax.axis_index(("yh", "c"))
-    odd = jnp.stack([lax.axis_index("yl") % 2, x_index % 2]).astype(jnp.int32)
+    odd = jnp.stack([lax.axis_index("yd"), x_index % 2]).astype(jnp.int32)
 
     field = eigvecs.reshape(6 * NEV, 1, SITES)
     links = gauge_links.reshape(54, 1, SITES)
@@ -340,11 +341,11 @@
             pltpu.VMEM((8, 4 * SITES, 256), F32),
         ],
     )
-    pieces = swap(partial.reshape(16, 32, 128), ("zl", "yl"))
+    pieces = swap(partial.reshape(16, 32, 128), ("zu", "zd", "yu", "yd"))
     part = jnp.sum(pieces, axis=0)
     part = jnp.sum(spread(part, "zh", 3), axis=0)
     part, perambulators, send = lax.optimization_barrier((part.astype(BF16), perambulators, send))
-    near = spread(part, ("yl", "yh", "c"), 16).reshape(4, 4, 32, 128)
+    near = spread(part, ("zu", "yu", "yh", "c"), 16).reshape(4, 4, 32, 128)
     factors = run(kernel_factors, shape((4, 128, 16 * 128), BF16), (perambulators.reshape(4, 2, 16, NEV, NEV),))
 
     smeared = run(kernel_output, shape((2, 3, NEV, SITES), BF16), (send,))
@@ -355,7 +356,7 @@
         scalar=True,
     )
     payload, smeared = lax.optimization_barrier((payload, smeared))
-    everything = swap(payload, ("zl", "x"))
+    everything = swap(payload, ("zd", "yd", "x"))
     elementals, correlator = run(kernel_unpack, (shape((32, 2, NEV, NEV), BF16), shape((2, 4, 32), F32)), (everything,))
     return (
         smeared.reshape(1, 2, 3, NEV, 1, SITES),
@@ -365,8 +366,8 @@
 
 
 def solution(mesh):
-    fine = Mesh(mesh.devices.reshape(3, 4, 4, 4, 2, 2), ("zh", "zl", "yl", "x", "yh", "c"))
-    space = ("zh", "zl", "yl", "x")
+    fine = Mesh(mesh.devices.reshape(3, 2, 2, 2, 2, 4, 2, 2), ("zh", "zu", "zd", "yu", "yd", "x", "yh", "c"))
+    space = ("zh", "zu", "zd", "yu", "yd", "x")
     times = ("yh", "c")
 
     return jax.shard_map(

time: 118 us -> 115 us (0.975)
  blocking collectives: 55.2 us -> 49.4 us
  waiting for transfers between devices: 7.44 us -> 9.24 us
    all_to_all x4, blocking collectives: 55.2 us -> 49.4 us  [swap(): return lax.all_to_all(value, axes, split_axis=0, concat_axis=0, tiled=True)]
    all_to_all x1, waiting for transfers between devices: 5.79 us -> 7.59 us  [swap(): return lax.all_to_all(value, axes, split_axis=0, concat_axis=0, tiled=True)]
where the time goes in v7:
time: 115 us; the launch traced here: 114 us
  blocking collectives  49.4 us (43%)
  starting transfers between devices  39.3 us (34%)
  Pallas kernels  11.5 us (10%)
  waiting for transfers between devices  9.24 us (8%)
  local copies, waits for them, and re-layouts  3.34 us (3%)
    all_to_all x4, blocking collectives, swap(): return lax.all_to_all(value, axes, split_axis=0, concat_axis=0, tiled=True)  49.4 us
    ppermute x1, starting transfers between devices, local(): recv_zb = lax.ppermute(send_zb, planes, pairs_b)  16.2 us
    all_to_all x1, starting transfers between devices, swap(): return lax.all_to_all(value, axes, split_axis=0, concat_axis=0, tiled=True)  12.2 us
    pallas_call x8, Pallas kernels, run(): pl.pallas_call(kernel, out_shape=outs, in_specs=in_specs, out_specs=jax.t...  11.5 us
    all_to_all x1, waiting for transfers between devices, swap(): return lax.all_to_all(value, axes, split_axis=0, concat_axis=0, tiled=True)  7.59 us
    ppermute x1, starting transfers between devices, local(): recv_xa = lax.ppermute(send_xa, 'x', ring_a)  3.94 us
    ppermute x1, starting transfers between devices, local(): recv_xb = lax.ppermute(send_xb, 'x', ring_b)  3.72 us
    ppermute x1, starting transfers between devices, local(): recv_za = lax.ppermute(send_za, planes, pairs_a)  3.2 us
  transfers between devices with their start and end apart: 5, of which 2 were waited for; matrix products, arithmetic and copies ran while one was open for 1% of the time, Pallas kernels for 2%

profile of v7, /device:TPU:1, one launch (start us, length us, event | category | flops | bytes accessed | tf_op | source)
XLA Modules:
  0.0 114.1 jit_solution(6695891854698074954)
XLA Ops:
  0.6 0.1 pad_add_fusion.odd_ref
  0.7 2.3 %shard_map.67 = (f32[3,144,128]{2,1,0:T(8,128)S(1)}, f32[3,144,128]{2,1,0:T(8,128)S(1)}, f32[3,144,128]{2,1,0:T(8,128)S(1)}, f32[3,24,128]{2,1,0:T(8,128)S(1)}, ...) custom-call(s32[2]{0:T(128)S(1)} %pad_add_fusion.odd_ref, f32[384,1,144]{2,1,0:T(1,128)} %bitcast.25, f32[54,1,144]{2,1,0:T(1,128)} %bitcast.29), custom_call_target="tpu_custom_call" | custom-call | tf_op jit(solution)/shard_map/pallas_call | solution.py:249
  3.1 3.9 %collective-permute-start.2 = (f32[3,24,128]{2,1,0:T(8,128)S(1)}, f32[3,24,128]{2,1,0:T(8,128)S(1)}, u32[]{:S(2)}, u32[]{:S(2)}) collective-permute-start(f32[3,24,128]{2,1,0:T(8,128)S(1)} %get-tuple-element.22), channel_id=1, source_target_pairs={{0,4},{4,0},{8,12},{12,8},{1,5},{5,1},{9,13},{13,9},{2,6},{6,2},{1... | collective-permute-start | bytes 110600 | tf_op jit(solution)/shard_map/ppermute | solution.py:313
  7.0 3.7 %collective-permute-start.3 = (f32[3,24,128]{2,1,0:T(8,128)S(1)}, f32[3,24,128]{2,1,0:T(8,128)S(1)}, u32[]{:S(2)}, u32[]{:S(2)}) collective-permute-start(f32[3,24,128]{2,1,0:T(8,128)S(1)} %get-tuple-element.23), channel_id=1, source_target_pairs={{0,12},{4,8},{8,4},{12,0},{1,13},{5,9},{9,5},{13,1},{2,14},{6,10},... | collective-permute-start | bytes 110600 | tf_op jit(solution)/shard_map/ppermute | solution.py:314
  10.7 3.2 %collective-permute-start = (f32[3,144,128]{2,1,0:T(8,128)S(1)}, f32[3,144,128]{2,1,0:T(8,128)S(1)}, u32[]{:S(2)}, u32[]{:S(2)}) collective-permute-start(f32[3,144,128]{2,1,0:T(8,128)S(1)} %get-tuple-element.20), channel_id=1, source_target_pairs={{0,16},{16,0},{32,48},{48,32},{64,80},{80,64},{96,112},{112,96},{1... | collective-permute-start | bytes 663560 | tf_op jit(solution)/shard_map/ppermute | solution.py:311
  13.9 16.2 %collective-permute-start.1 = (f32[3,144,128]{2,1,0:T(8,128)S(1)}, f32[3,144,128]{2,1,0:T(8,128)S(1)}, u32[]{:S(2)}, u32[]{:S(2)}) collective-permute-start(f32[3,144,128]{2,1,0:T(8,128)S(1)} %get-tuple-element.21), channel_id=1, source_target_pairs={{0,752},{16,32},{32,16},{48,64},{64,48},{80,96},{96,80},{112,128},... | collective-permute-start | bytes 663560 | tf_op jit(solution)/shard_map/ppermute | solution.py:312
  30.2 0.8 reshape.65
  31.0 0.1 copy.15
  31.1 0.2 slice_reduce_fusion.1
  31.3 0.2 fusion.16
  31.5 0.2 fusion.12
  31.7 1.1 shard_map.68.acc_ref
  32.8 0.0 collective-permute-done.2.xa_ref
  32.8 0.0 collective-permute-done.3.xb_ref
  32.8 0.0 collective-permute-done.za_ref
  32.8 1.6 %collective-permute-done.1.zb_ref = f32[3,144,128]{2,1,0:T(8,128)S(1)} collective-permute-done((f32[3,144,128]{2,1,0:T(8,128)S(1)}, f32[3,144,128]{2,1,0:T(8,128)S(1)}, u32[]{:S(2)}, u32[]{:S(2)}) %collective-permute-start.1) | collective-permute-done | bytes 221216 | tf_op jit(solution)/shard_map/ppermute | solution.py:312
  34.4 1.2 %shard_map.69.s_ref = bf16[4,3,144,128]{3,2,1,0:T(8,128)(2,1)S(1)} custom-call(s32[2]{0:T(128)S(1)} %pad_add_fusion.odd_ref, f32[3,144,128]{2,1,0:T(8,128)S(1)} %shard_map.68.acc_ref, f32[144,54]{1,0:T(8,128)S(1)} %get-tuple-element.19.cols_ref, f32[3,144,128]{2,1,0:T(8,128)S(1)} %collective-permute-done.za_ref, ...), custom_call_target="tpu_custom_call" | custom-call | tf_op jit(solution)/shard_map/pallas_call | solution.py:249
  35.6 8.9 %all_to_all.25.refs_0_ = bf16[4,3,144,128]{3,2,1,0:T(8,128)(2,1)S(1)} all-to-all(bf16[4,3,144,128]{3,2,1,0:T(8,128)(2,1)S(1)} %shard_map.69.s_ref), channel_id=1, replica_groups=mesh['zh'=3,'zu'=2,'zd'=2,'yu'=2,'yd'=2,'x'=4,'yh'=2,'c'=2] {'x'}, dimensions={0} | all-to-all | bytes 884736 | tf_op jit(solution)/shard_map/all_to_all | solution.py:273
  44.5 2.3 %shard_map.70 = f32[4,4,32,128]{3,2,1,0:T(8,128)S(1)} custom-call(bf16[4,3,144,128]{3,2,1,0:T(8,128)(2,1)S(1)} %all_to_all.25.refs_0_, f32[16,576]{1,0:T(8,128)S(1)} %pad_maximum_fusion.refs_1_), custom_call_target="tpu_custom_call" | custom-call | tf_op jit(solution)/shard_map/pallas_call | solution.py:249
  46.8 11.1 %all_to_all.26 = f32[16,32,128]{2,1,0:T(8,128)S(1)} all-to-all(f32[16,32,128]{2,1,0:T(8,128)S(1)} %bitcast.23), channel_id=1, replica_groups=mesh['zh'=3,'zu'=2,'zd'=2,'yu'=2,'yd'=2,'x'=4,'yh'=2,'c'=2] {'zu','zd','..., dimensions={0} | all-to-all | bytes 524288 | tf_op jit(solution)/shard_map/all_to_all | solution.py:273
  57.9 14.8 %all_to_all.27 = f32[3,32,128]{2,1,0:T(8,128)S(1)} all-to-all(f32[3,32,128]{2,1,0:T(8,128)S(1)} %broadcast_in_dim.4), channel_id=1, replica_groups=mesh['zh'=3,'zu'=2,'zd'=2,'yu'=2,'yd'=2,'x'=4,'yh'=2,'c'=2] {'zh'}, dimensions={0} | all-to-all | bytes 98304 | tf_op jit(solution)/shard_map/all_to_all | solution.py:273
  72.7 0.7 broadcast_in_dim.5
  73.4 12.2 %all-to-all-start.3 = ((bf16[16,32,128]{2,1,0:T(8,128)(2,1)}), bf16[16,32,128]{2,1,0:T(8,128)(2,1)S(1)}, u32[]{:S(2)}, u32[]{:S(2)}) async-start(bf16[16,32,128]{2,1,0:T(8,128)(2,1)} %broadcast_in_dim.5), calls=%async_computation.3 | async-start | bytes 262144 | tf_op jit(solution)/shard_map/all_to_all | solution.py:273
  85.6 0.8 shard_map.73
  86.4 0.0 copy-start
  86.4 1.6 %copy-done = bf16[1,4,2,4,4,64,64]{6,5,4,3,2,1,0:T(8,128)(2,1)S(1)} copy-done((bf16[1,4,2,4,4,64,64]{6,5,4,3,2,1,0:T(8,128)(2,1)S(1)}, bf16[1,4,2,4,4,64,64]{6,5,4,3,2,1,0:T(8,128)(2,1)}, u32[]{:S(2)}) %copy-start) | copy-done | bytes 1048600
  88.0 0.8 shard_map.71.b_ref
  88.9 7.6 %all-to-all-done.3 = bf16[16,32,128]{2,1,0:T(8,128)(2,1)S(1)} async-done(((bf16[16,32,128]{2,1,0:T(8,128)(2,1)}), bf16[16,32,128]{2,1,0:T(8,128)(2,1)S(1)}, u32[]{:S(2)}, u32[]{:S(2)}) %all-to-all-start.3) | async-done | bytes 131104 | tf_op jit(solution)/shard_map/all_to_all | solution.py:273
  96.4 1.7 %shard_map.72 = bf16[16,144,128]{2,1,0:T(8,128)(2,1)S(1)} custom-call(s32[1]{0:T(128)} %bitcast.tm_ref, bf16[4,4,32,128]{3,2,1,0:T(8,128)(2,1)S(1)} %bitcast.24, bf16[4,128,2048]{2,1,0:T(8,128)(2,1)S(1)} %shard_map.71.b_ref), custom_call_target="tpu_custom_call" | custom-call | tf_op jit(solution)/shard_map/pallas_call | solution.py:249
  98.1 14.6 %all_to_all.28.r_ref = bf16[16,144,128]{2,1,0:T(8,128)(2,1)S(1)} all-to-all(bf16[16,144,128]{2,1,0:T(8,128)(2,1)S(1)} %shard_map.72), channel_id=1, replica_groups=mesh['zh'=3,'zu'=2,'zd'=2,'yu'=2,'yd'=2,'x'=4,'yh'=2,'c'=2] {'zd','yd','x'}, dimensions={0} | all-to-all | bytes 1179648 | tf_op jit(solution)/shard_map/all_to_all | solution.py:273
  112.8 1.4 %shard_map.74 = (bf16[32,2,64,64]{3,2,1,0:T(8,128)(2,1)}, f32[2,4,32]{2,1,0:T(4,128)}) custom-call(bf16[16,144,128]{2,1,0:T(8,128)(2,1)S(1)} %all_to_all.28.r_ref), custom_call_target="tpu_custom_call" | custom-call | tf_op jit(solution)/shard_map/pallas_call | solution.py:249
  (6 shorter events, 0.1 us)
Async XLA Ops:
  3.1 29.7 %collective-permute-start.2 = (f32[3,24,128]{2,1,0:T(8,128)S(1)}, f32[3,24,128]{2,1,0:T(8,128)S(1)}, u32[]{:S(2)}, u32[]{:S(2)}) collective-permute-start(f32[3,24,128]{2,1,0:T(8,128)S(1)} %get-tuple-element.22), channel_id=1, source_target_pairs={{0,4},{4,0},{8,12},{12,8},{1,5},{5,1},{9,13},{13,9},{2,6},{6,2},{1... | collective-permute-start | bytes 110600 | tf_op jit(solution)/shard_map/ppermute | solution.py:313
  7.0 25.8 %collective-permute-start.3 = (f32[3,24,128]{2,1,0:T(8,128)S(1)}, f32[3,24,128]{2,1,0:T(8,128)S(1)}, u32[]{:S(2)}, u32[]{:S(2)}) collective-permute-start(f32[3,24,128]{2,1,0:T(8,128)S(1)} %get-tuple-element.23), channel_id=1, source_target_pairs={{0,12},{4,8},{8,4},{12,0},{1,13},{5,9},{9,5},{13,1},{2,14},{6,10},... | collective-permute-start | bytes 110600 | tf_op jit(solution)/shard_map/ppermute | solution.py:314
  10.7 22.1 %collective-permute-start = (f32[3,144,128]{2,1,0:T(8,128)S(1)}, f32[3,144,128]{2,1,0:T(8,128)S(1)}, u32[]{:S(2)}, u32[]{:S(2)}) collective-permute-start(f32[3,144,128]{2,1,0:T(8,128)S(1)} %get-tuple-element.20), channel_id=1, source_target_pairs={{0,16},{16,0},{32,48},{48,32},{64,80},{80,64},{96,112},{112,96},{1... | collective-permute-start | bytes 663560 | tf_op jit(solution)/shard_map/ppermute | solution.py:311
  13.9 20.5 %collective-permute-start.1 = (f32[3,144,128]{2,1,0:T(8,128)S(1)}, f32[3,144,128]{2,1,0:T(8,128)S(1)}, u32[]{:S(2)}, u32[]{:S(2)}) collective-permute-start(f32[3,144,128]{2,1,0:T(8,128)S(1)} %get-tuple-element.21), channel_id=1, source_target_pairs={{0,752},{16,32},{32,16},{48,64},{64,48},{80,96},{96,80},{112,128},... | collective-permute-start | bytes 663560 | tf_op jit(solution)/shard_map/ppermute | solution.py:312
  73.4 23.1 %all-to-all-start.3 = ((bf16[16,32,128]{2,1,0:T(8,128)(2,1)}), bf16[16,32,128]{2,1,0:T(8,128)(2,1)S(1)}, u32[]{:S(2)}, u32[]{:S(2)}) async-start(bf16[16,32,128]{2,1,0:T(8,128)(2,1)} %broadcast_in_dim.5), calls=%async_computation.3 | async-start | bytes 262144 | tf_op jit(solution)/shard_map/all_to_all | solution.py:273
  86.4 1.6 %copy-start = (bf16[1,4,2,4,4,64,64]{6,5,4,3,2,1,0:T(8,128)(2,1)S(1)}, bf16[1,4,2,4,4,64,64]{6,5,4,3,2,1,0:T(8,128)(2,1)}, u32[]{:S(2)}) copy-start(bf16[1,4,2,4,4,64,64]{6,5,4,3,2,1,0:T(8,128)(2,1)} %param.6) | copy-start | bytes 3145732

commit v8 on v7

--- a/solution.py
+++ b/solution.py
@@ -163,9 +163,8 @@
         for pp in range(2):
             block = prod[:, pp * 128 : (pp + 1) * 128]
             result = (block[:64] + roll(block[64:], 64, 1) * sign) * scale
-            z_at = pp * 2 + pair // 2
-            out_ref[z_at, pair % 2] = result[:32]
-            out_ref[z_at, 2 + pair % 2] = result[32:]
+            out_ref[pp * 2, pair] = result[:32]
+            out_ref[pp * 2 + 1, pair] = result[32:]
 
 
 def kernel_factors(p_ref, out_ref):
@@ -256,11 +255,13 @@
     )(*args)
 
 
-def phases(momenta, z_index):
+def phases(momenta, z_base, y_base):
     site = jnp.arange(4 * SITES, dtype=jnp.int32)
+    block = site // SITES
+    row = site % SITES // LX
     turn_x = momenta[:, 0, None] * (site % LX)[None] % LX
-    turn_y = momenta[:, 1, None] * (site // LX)[None] % LX
-    turn_z = momenta[:, 2, None] * z_index % NZ
+    turn_y = momenta[:, 1, None] * (y_base + row)[None] % LX
+    turn_z = momenta[:, 2, None] * (z_base + block // 2 * 4 + block % 2)[None] % NZ
     angles = (
         2.0
         * math.pi
@@ -284,7 +285,8 @@
     pairs_b = [(i, j % NZ) for i, j in pairs_b]
     ring_a = [(i, i ^ 1) for i in range(4)]
     ring_b = [(i, (((i + 1) ^ 1) - 1) % 4) for i in range(4)]
-    z_index = lax.axis_index(planes)
+    octet = lax.axis_index(("zd", "yd"))
+    z_base = lax.axis_index("zh") * 16 + lax.axis_index("zu") * 8 + lax.axis_index("yu") * 2
     x_index = lax.axis_index("x")
     tm_index = lax.axis_index(("yh", "c"))
     odd = jnp.stack([lax.axis_index("yd"), x_index % 2]).astype(jnp.int32)
@@ -320,10 +322,10 @@
         (odd, inner, cols, recv_za, recv_zb, recv_xa, recv_xb),
         scalar=True,
     )
-    mine = lax.dynamic_index_in_dim(momenta.reshape(4, 4, 2, 3), x_index, 1, keepdims=False).reshape(8, 3)
-    phase = phases(mine, z_index)
+    mine = lax.dynamic_index_in_dim(momenta.reshape(4, 8, 3), octet, 0, keepdims=False)
+    phase = phases(mine, z_base, x_index * (SITES // LX))
     send, phase = lax.optimization_barrier((send, phase))
-    shared = swap(send, "x")
+    shared = swap(send, ("zd", "yd"))
     scale = 1.0 / math.sqrt(3.0 * NZ * LX * LX)
 
     def contract(*refs):
@@ -341,7 +343,7 @@
             pltpu.VMEM((8, 4 * SITES, 256), F32),
         ],
     )
-    pieces = swap(partial.reshape(16, 32, 128), ("zu", "zd", "yu", "yd"))
+    pieces = swap(partial.reshape(16, 32, 128), ("zu", "yu", "x"))
     part = jnp.sum(pieces, axis=0)
     part = jnp.sum(spread(part, "zh", 3), axis=0)
     part, perambulators, send = lax.optimization_barrier((part.astype(BF16), perambulators, send))

time: 115 us -> 115 us (level)
  blocking collectives: 49.4 us -> 50.8 us
    all_to_all x4, blocking collectives: 49.4 us -> 50.8 us  [swap(): return lax.all_to_all(value, axes, split_axis=0, concat_axis=0, tiled=True)]
where the time goes in v8:
time: 115 us; the launch traced here: 114 us
  blocking collectives  50.8 us (44%)
  starting transfers between devices  38.2 us (33%)
  Pallas kernels  11.5 us (10%)
  waiting for transfers between devices  9.41 us (8%)
  local copies, waits for them, and re-layouts  3.05 us (3%)
    all_to_all x4, blocking collectives, swap(): return lax.all_to_all(value, axes, split_axis=0, concat_axis=0, tiled=True)  50.8 us
    ppermute x1, starting transfers between devices, local(): recv_zb = lax.ppermute(send_zb, planes, pairs_b)  16.2 us
    pallas_call x8, Pallas kernels, run(): pl.pallas_call(kernel, out_shape=outs, in_specs=in_specs, out_specs=jax.t...  11.5 us
    all_to_all x1, starting transfers between devices, swap(): return lax.all_to_all(value, axes, split_axis=0, concat_axis=0, tiled=True)  11.1 us
    all_to_all x1, waiting for transfers between devices, swap(): return lax.all_to_all(value, axes, split_axis=0, concat_axis=0, tiled=True)  7.3 us
    ppermute x1, starting transfers between devices, local(): recv_xa = lax.ppermute(send_xa, 'x', ring_a)  3.94 us
    ppermute x1, starting transfers between devices, local(): recv_xb = lax.ppermute(send_xb, 'x', ring_b)  3.72 us
    ppermute x1, starting transfers between devices, local(): recv_za = lax.ppermute(send_za, planes, pairs_a)  3.2 us
  transfers between devices with their start and end apart: 5, of which 2 were waited for; matrix products, arithmetic and copies ran while one was open for 1% of the time, Pallas kernels for 2%

profile of v8, /device:TPU:1, one launch (start us, length us, event | category | flops | bytes accessed | tf_op | source)
XLA Modules:
  0.0 114.1 jit_solution(10957906138021239463)
XLA Ops:
  0.6 0.1 pad_add_fusion.odd_ref
  0.7 2.3 %shard_map.67 = (f32[3,144,128]{2,1,0:T(8,128)S(1)}, f32[3,144,128]{2,1,0:T(8,128)S(1)}, f32[3,144,128]{2,1,0:T(8,128)S(1)}, f32[3,24,128]{2,1,0:T(8,128)S(1)}, ...) custom-call(s32[2]{0:T(128)S(1)} %pad_add_fusion.odd_ref, f32[384,1,144]{2,1,0:T(1,128)} %bitcast.33, f32[54,1,144]{2,1,0:T(1,128)} %bitcast.35), custom_call_target="tpu_custom_call" | custom-call | tf_op jit(solution)/shard_map/pallas_call | solution.py:248
  3.1 3.9 %collective-permute-start.2 = (f32[3,24,128]{2,1,0:T(8,128)S(1)}, f32[3,24,128]{2,1,0:T(8,128)S(1)}, u32[]{:S(2)}, u32[]{:S(2)}) collective-permute-start(f32[3,24,128]{2,1,0:T(8,128)S(1)} %get-tuple-element.22), channel_id=1, source_target_pairs={{0,4},{4,0},{8,12},{12,8},{1,5},{5,1},{9,13},{13,9},{2,6},{6,2},{1... | collective-permute-start | bytes 110600 | tf_op jit(solution)/shard_map/ppermute | solution.py:315
  7.0 3.7 %collective-permute-start.3 = (f32[3,24,128]{2,1,0:T(8,128)S(1)}, f32[3,24,128]{2,1,0:T(8,128)S(1)}, u32[]{:S(2)}, u32[]{:S(2)}) collective-permute-start(f32[3,24,128]{2,1,0:T(8,128)S(1)} %get-tuple-element.23), channel_id=1, source_target_pairs={{0,12},{4,8},{8,4},{12,0},{1,13},{5,9},{9,5},{13,1},{2,14},{6,10},... | collective-permute-start | bytes 110600 | tf_op jit(solution)/shard_map/ppermute | solution.py:316
  10.7 3.2 %collective-permute-start = (f32[3,144,128]{2,1,0:T(8,128)S(1)}, f32[3,144,128]{2,1,0:T(8,128)S(1)}, u32[]{:S(2)}, u32[]{:S(2)}) collective-permute-start(f32[3,144,128]{2,1,0:T(8,128)S(1)} %get-tuple-element.20), channel_id=1, source_target_pairs={{0,16},{16,0},{32,48},{48,32},{64,80},{80,64},{96,112},{112,96},{1... | collective-permute-start | bytes 663560 | tf_op jit(solution)/shard_map/ppermute | solution.py:313
  13.9 16.2 %collective-permute-start.1 = (f32[3,144,128]{2,1,0:T(8,128)S(1)}, f32[3,144,128]{2,1,0:T(8,128)S(1)}, u32[]{:S(2)}, u32[]{:S(2)}) collective-permute-start(f32[3,144,128]{2,1,0:T(8,128)S(1)} %get-tuple-element.21), channel_id=1, source_target_pairs={{0,752},{16,32},{32,16},{48,64},{64,48},{80,96},{96,80},{112,128},... | collective-permute-start | bytes 663560 | tf_op jit(solution)/shard_map/ppermute | solution.py:314
  30.2 0.8 reshape.108
  31.0 0.2 fusion.17
  31.2 1.1 shard_map.68.acc_ref
  32.3 0.0 collective-permute-done.2.xa_ref
  32.3 0.0 collective-permute-done.3.xb_ref
  32.3 0.0 collective-permute-done.za_ref
  32.3 2.1 %collective-permute-done.1.zb_ref = f32[3,144,128]{2,1,0:T(8,128)S(1)} collective-permute-done((f32[3,144,128]{2,1,0:T(8,128)S(1)}, f32[3,144,128]{2,1,0:T(8,128)S(1)}, u32[]{:S(2)}, u32[]{:S(2)}) %collective-permute-start.1) | collective-permute-done | bytes 221216 | tf_op jit(solution)/shard_map/ppermute | solution.py:314
  34.4 1.2 %shard_map.69.s_ref = bf16[4,3,144,128]{3,2,1,0:T(8,128)(2,1)S(1)} custom-call(s32[2]{0:T(128)S(1)} %pad_add_fusion.odd_ref, f32[3,144,128]{2,1,0:T(8,128)S(1)} %shard_map.68.acc_ref, f32[144,54]{1,0:T(8,128)S(1)} %get-tuple-element.19.cols_ref, f32[3,144,128]{2,1,0:T(8,128)S(1)} %collective-permute-done.za_ref, ...), custom_call_target="tpu_custom_call" | custom-call | tf_op jit(solution)/shard_map/pallas_call | solution.py:248
  35.6 8.1 %all_to_all.25.refs_0_ = bf16[4,3,144,128]{3,2,1,0:T(8,128)(2,1)S(1)} all-to-all(bf16[4,3,144,128]{3,2,1,0:T(8,128)(2,1)S(1)} %shard_map.69.s_ref), channel_id=1, replica_groups=mesh['zh'=3,'zu'=2,'zd'=2,'yu'=2,'yd'=2,'x'=4,'yh'=2,'c'=2] {'zd','yd'}, dimensions={0} | all-to-all | bytes 884736 | tf_op jit(solution)/shard_map/all_to_all | solution.py:274
  43.8 2.3 %shard_map.70 = f32[4,4,32,128]{3,2,1,0:T(8,128)S(1)} custom-call(bf16[4,3,144,128]{3,2,1,0:T(8,128)(2,1)S(1)} %all_to_all.25.refs_0_, f32[16,576]{1,0:T(8,128)S(1)} %pad_maximum_fusion.refs_1_), custom_call_target="tpu_custom_call" | custom-call | tf_op jit(solution)/shard_map/pallas_call | solution.py:248
  46.0 13.6 %all_to_all.26 = f32[16,32,128]{2,1,0:T(8,128)S(1)} all-to-all(f32[16,32,128]{2,1,0:T(8,128)S(1)} %bitcast.31), channel_id=1, replica_groups=mesh['zh'=3,'zu'=2,'zd'=2,'yu'=2,'yd'=2,'x'=4,'yh'=2,'c'=2] {'zu','yu','x'}, dimensions={0} | all-to-all | bytes 524288 | tf_op jit(solution)/shard_map/all_to_all | solution.py:274
  59.7 15.4 %all_to_all.27 = f32[3,32,128]{2,1,0:T(8,128)S(1)} all-to-all(f32[3,32,128]{2,1,0:T(8,128)S(1)} %broadcast_in_dim.4), channel_id=1, replica_groups=mesh['zh'=3,'zu'=2,'zd'=2,'yu'=2,'yd'=2,'x'=4,'yh'=2,'c'=2] {'zh'}, dimensions={0} | all-to-all | bytes 98304 | tf_op jit(solution)/shard_map/all_to_all | solution.py:274
  75.1 0.7 broadcast_in_dim.5
  75.7 11.1 %all-to-all-start.3 = ((bf16[16,32,128]{2,1,0:T(8,128)(2,1)}), bf16[16,32,128]{2,1,0:T(8,128)(2,1)S(1)}, u32[]{:S(2)}, u32[]{:S(2)}) async-start(bf16[16,32,128]{2,1,0:T(8,128)(2,1)} %broadcast_in_dim.5), calls=%async_computation.3 | async-start | bytes 262144 | tf_op jit(solution)/shard_map/all_to_all | solution.py:274
  86.9 0.8 shard_map.73
  87.7 0.0 copy-start
  87.7 1.6 %copy-done = bf16[1,4,2,4,4,64,64]{6,5,4,3,2,1,0:T(8,128)(2,1)S(1)} copy-done((bf16[1,4,2,4,4,64,64]{6,5,4,3,2,1,0:T(8,128)(2,1)S(1)}, bf16[1,4,2,4,4,64,64]{6,5,4,3,2,1,0:T(8,128)(2,1)}, u32[]{:S(2)}) %copy-start) | copy-done | bytes 1048600
  89.3 0.8 shard_map.71.b_ref
  90.1 7.3 %all-to-all-done.3 = bf16[16,32,128]{2,1,0:T(8,128)(2,1)S(1)} async-done(((bf16[16,32,128]{2,1,0:T(8,128)(2,1)}), bf16[16,32,128]{2,1,0:T(8,128)(2,1)S(1)}, u32[]{:S(2)}, u32[]{:S(2)}) %all-to-all-start.3) | async-done | bytes 131104 | tf_op jit(solution)/shard_map/all_to_all | solution.py:274
  97.4 1.7 %shard_map.72 = bf16[16,144,128]{2,1,0:T(8,128)(2,1)S(1)} custom-call(s32[1]{0:T(128)} %bitcast.tm_ref, bf16[4,4,32,128]{3,2,1,0:T(8,128)(2,1)S(1)} %bitcast.32, bf16[4,128,2048]{2,1,0:T(8,128)(2,1)S(1)} %shard_map.71.b_ref), custom_call_target="tpu_custom_call" | custom-call | tf_op jit(solution)/shard_map/pallas_call | solution.py:248
  99.1 13.6 %all_to_all.28.r_ref = bf16[16,144,128]{2,1,0:T(8,128)(2,1)S(1)} all-to-all(bf16[16,144,128]{2,1,0:T(8,128)(2,1)S(1)} %shard_map.72), channel_id=1, replica_groups=mesh['zh'=3,'zu'=2,'zd'=2,'yu'=2,'yd'=2,'x'=4,'yh'=2,'c'=2] {'zd','yd','x'}, dimensions={0} | all-to-all | bytes 1179648 | tf_op jit(solution)/shard_map/all_to_all | solution.py:274
  112.7 1.4 %shard_map.74 = (bf16[32,2,64,64]{3,2,1,0:T(8,128)(2,1)}, f32[2,4,32]{2,1,0:T(4,128)}) custom-call(bf16[16,144,128]{2,1,0:T(8,128)(2,1)S(1)} %all_to_all.28.r_ref), custom_call_target="tpu_custom_call" | custom-call | tf_op jit(solution)/shard_map/pallas_call | solution.py:248
  (9 shorter events, 0.1 us)
Async XLA Ops:
  3.1 29.3 %collective-permute-start.2 = (f32[3,24,128]{2,1,0:T(8,128)S(1)}, f32[3,24,128]{2,1,0:T(8,128)S(1)}, u32[]{:S(2)}, u32[]{:S(2)}) collective-permute-start(f32[3,24,128]{2,1,0:T(8,128)S(1)} %get-tuple-element.22), channel_id=1, source_target_pairs={{0,4},{4,0},{8,12},{12,8},{1,5},{5,1},{9,13},{13,9},{2,6},{6,2},{1... | collective-permute-start | bytes 110600 | tf_op jit(solution)/shard_map/ppermute | solution.py:315
  7.0 25.3 %collective-permute-start.3 = (f32[3,24,128]{2,1,0:T(8,128)S(1)}, f32[3,24,128]{2,1,0:T(8,128)S(1)}, u32[]{:S(2)}, u32[]{:S(2)}) collective-permute-start(f32[3,24,128]{2,1,0:T(8,128)S(1)} %get-tuple-element.23), channel_id=1, source_target_pairs={{0,12},{4,8},{8,4},{12,0},{1,13},{5,9},{9,5},{13,1},{2,14},{6,10},... | collective-permute-start | bytes 110600 | tf_op jit(solution)/shard_map/ppermute | solution.py:316
  10.7 21.6 %collective-permute-start = (f32[3,144,128]{2,1,0:T(8,128)S(1)}, f32[3,144,128]{2,1,0:T(8,128)S(1)}, u32[]{:S(2)}, u32[]{:S(2)}) collective-permute-start(f32[3,144,128]{2,1,0:T(8,128)S(1)} %get-tuple-element.20), channel_id=1, source_target_pairs={{0,16},{16,0},{32,48},{48,32},{64,80},{80,64},{96,112},{112,96},{1... | collective-permute-start | bytes 663560 | tf_op jit(solution)/shard_map/ppermute | solution.py:313
  13.9 20.5 %collective-permute-start.1 = (f32[3,144,128]{2,1,0:T(8,128)S(1)}, f32[3,144,128]{2,1,0:T(8,128)S(1)}, u32[]{:S(2)}, u32[]{:S(2)}) collective-permute-start(f32[3,144,128]{2,1,0:T(8,128)S(1)} %get-tuple-element.21), channel_id=1, source_target_pairs={{0,752},{16,32},{32,16},{48,64},{64,48},{80,96},{96,80},{112,128},... | collective-permute-start | bytes 663560 | tf_op jit(solution)/shard_map/ppermute | solution.py:314
  75.7 21.7 %all-to-all-start.3 = ((bf16[16,32,128]{2,1,0:T(8,128)(2,1)}), bf16[16,32,128]{2,1,0:T(8,128)(2,1)S(1)}, u32[]{:S(2)}, u32[]{:S(2)}) async-start(bf16[16,32,128]{2,1,0:T(8,128)(2,1)} %broadcast_in_dim.5), calls=%async_computation.3 | async-start | bytes 262144 | tf_op jit(solution)/shard_map/all_to_all | solution.py:274
  87.7 1.6 %copy-start = (bf16[1,4,2,4,4,64,64]{6,5,4,3,2,1,0:T(8,128)(2,1)S(1)}, bf16[1,4,2,4,4,64,64]{6,5,4,3,2,1,0:T(8,128)(2,1)}, u32[]{:S(2)}) copy-start(bf16[1,4,2,4,4,64,64]{6,5,4,3,2,1,0:T(8,128)(2,1)} %param.6) | copy-start | bytes 3145732

commit v9 on v7

--- a/solution.py
+++ b/solution.py
@@ -343,8 +343,14 @@
     )
     pieces = swap(partial.reshape(16, 32, 128), ("zu", "zd", "yu", "yd"))
     part = jnp.sum(pieces, axis=0)
-    part = jnp.sum(spread(part, "zh", 3), axis=0)
-    part, perambulators, send = lax.optimization_barrier((part.astype(BF16), perambulators, send))
+    part, perambulators, send = lax.optimization_barrier((part, perambulators, send))
+    prev = lax.ppermute(part, "zh", [(0, 1), (1, 2), (2, 0)])
+    following = lax.ppermute(part, "zh", [(1, 0), (2, 1), (0, 2)])
+    third = lax.axis_index("zh")
+    term0 = jnp.where(third == 0, part, jnp.where(third == 1, prev, following))
+    term1 = jnp.where(third == 1, part, jnp.where(third == 2, prev, following))
+    term2 = jnp.where(third == 2, part, jnp.where(third == 0, prev, following))
+    part = ((term0 + term1) + term2).astype(BF16)
     near = spread(part, ("zu", "yu", "yh", "c"), 16).reshape(4, 4, 32, 128)
     factors = run(kernel_factors, shape((4, 128, 16 * 128), BF16), (perambulators.reshape(4, 2, 16, NEV, NEV),))
 

time: 115 us -> 117 us (1.017)
  blocking collectives: 49.4 us -> 34.6 us
  starting transfers between devices: 39.3 us -> 50.1 us
  waiting for transfers between devices: 9.24 us -> 15.8 us
    all_to_all x4 -> x3, blocking collectives: 49.4 us -> 34.6 us  [swap(): return lax.all_to_all(value, axes, split_axis=0, concat_axis=0, tiled=True)]
    ppermute x0 -> x2, starting transfers between devices: none -> 10.9 us  [the longest x1 8.93 us: local(): following = lax.ppermute(part, 'zh', [(1, 0), (2, 1), (0, 2)])]
    ppermute x0 -> x2, waiting for transfers between devices: none -> 6.52 us  [the longest x1 6.52 us: local(): prev = lax.ppermute(part, 'zh', [(0, 1), (1, 2), (2, 0)])]
  transfers between devices with their start and end apart: 5 -> 7, of which waited for: 2 -> 3; matrix products, arithmetic and copies ran while one was open for 1% -> 1% of each run, Pallas kernels for 2% -> 2%
where the time goes in v9:
time: 117 us
  starting transfers between devices  50.1 us (43%)
  blocking collectives  34.6 us (30%)
  waiting for transfers between devices  15.8 us (14%)
  Pallas kernels  11.5 us (10%)
  local copies, waits for them, and re-layouts  3.34 us (3%)
    all_to_all x3, blocking collectives, swap(): return lax.all_to_all(value, axes, split_axis=0, concat_axis=0, tiled=True)  34.6 us
    ppermute x1, starting transfers between devices, local(): recv_zb = lax.ppermute(send_zb, planes, pairs_b)  16.2 us
    all_to_all x1, starting transfers between devices, swap(): return lax.all_to_all(value, axes, split_axis=0, concat_axis=0, tiled=True)  12.2 us
    pallas_call x8, Pallas kernels, run(): pl.pallas_call(kernel, out_shape=outs, in_specs=in_specs, out_specs=jax.t...  11.5 us
    ppermute x1, starting transfers between devices, local(): following = lax.ppermute(part, 'zh', [(1, 0), (2, 1), (0, 2)])  8.93 us
    all_to_all x1, waiting for transfers between devices, swap(): return lax.all_to_all(value, axes, split_axis=0, concat_axis=0, tiled=True)  7.59 us
    ppermute x1, waiting for transfers between devices, local(): prev = lax.ppermute(part, 'zh', [(0, 1), (1, 2), (2, 0)])  6.52 us
    ppermute x1, starting transfers between devices, local(): recv_xa = lax.ppermute(send_xa, 'x', ring_a)  3.94 us
  transfers between devices with their start and end apart: 7, of which 3 were waited for; matrix products, arithmetic and copies ran while one was open for 1% of the time, Pallas kernels for 2%

profile of v9, /device:TPU:1, one launch (start us, length us, event | category | flops | bytes accessed | tf_op | source)
XLA Modules:
  0.0 116.6 jit_solution(12419756057642667033)
XLA Ops:
  0.6 0.1 pad_add_fusion.odd_ref
  0.7 2.3 %shard_map.67 = (f32[3,144,128]{2,1,0:T(8,128)S(1)}, f32[3,144,128]{2,1,0:T(8,128)S(1)}, f32[3,144,128]{2,1,0:T(8,128)S(1)}, f32[3,24,128]{2,1,0:T(8,128)S(1)}, ...) custom-call(s32[2]{0:T(128)S(1)} %pad_add_fusion.odd_ref, f32[384,1,144]{2,1,0:T(1,128)} %bitcast.25, f32[54,1,144]{2,1,0:T(1,128)} %bitcast.29), custom_call_target="tpu_custom_call" | custom-call | tf_op jit(solution)/shard_map/pallas_call | solution.py:249
  3.1 3.9 %collective-permute-start.2 = (f32[3,24,128]{2,1,0:T(8,128)S(1)}, f32[3,24,128]{2,1,0:T(8,128)S(1)}, u32[]{:S(2)}, u32[]{:S(2)}) collective-permute-start(f32[3,24,128]{2,1,0:T(8,128)S(1)} %get-tuple-element.22), channel_id=1, source_target_pairs={{0,4},{4,0},{8,12},{12,8},{1,5},{5,1},{9,13},{13,9},{2,6},{6,2},{1... | collective-permute-start | bytes 110600 | tf_op jit(solution)/shard_map/ppermute | solution.py:313
  7.0 3.7 %collective-permute-start.3 = (f32[3,24,128]{2,1,0:T(8,128)S(1)}, f32[3,24,128]{2,1,0:T(8,128)S(1)}, u32[]{:S(2)}, u32[]{:S(2)}) collective-permute-start(f32[3,24,128]{2,1,0:T(8,128)S(1)} %get-tuple-element.23), channel_id=1, source_target_pairs={{0,12},{4,8},{8,4},{12,0},{1,13},{5,9},{9,5},{13,1},{2,14},{6,10},... | collective-permute-start | bytes 110600 | tf_op jit(solution)/shard_map/ppermute | solution.py:314
  10.7 3.2 %collective-permute-start = (f32[3,144,128]{2,1,0:T(8,128)S(1)}, f32[3,144,128]{2,1,0:T(8,128)S(1)}, u32[]{:S(2)}, u32[]{:S(2)}) collective-permute-start(f32[3,144,128]{2,1,0:T(8,128)S(1)} %get-tuple-element.20), channel_id=1, source_target_pairs={{0,16},{16,0},{32,48},{48,32},{64,80},{80,64},{96,112},{112,96},{1... | collective-permute-start | bytes 663560 | tf_op jit(solution)/shard_map/ppermute | solution.py:311
  13.9 16.2 %collective-permute-start.1 = (f32[3,144,128]{2,1,0:T(8,128)S(1)}, f32[3,144,128]{2,1,0:T(8,128)S(1)}, u32[]{:S(2)}, u32[]{:S(2)}) collective-permute-start(f32[3,144,128]{2,1,0:T(8,128)S(1)} %get-tuple-element.21), channel_id=1, source_target_pairs={{0,752},{16,32},{32,16},{48,64},{64,48},{80,96},{96,80},{112,128},... | collective-permute-start | bytes 663560 | tf_op jit(solution)/shard_map/ppermute | solution.py:312
  30.2 0.8 reshape.64
  31.0 0.1 copy.11
  31.1 0.2 slice_reduce_fusion.1
  31.3 0.2 fusion.16
  31.5 0.2 fusion.12
  31.7 1.1 shard_map.68.acc_ref
  32.8 0.0 collective-permute-done.2.xa_ref
  32.8 0.0 collective-permute-done.3.xb_ref
  32.8 0.0 collective-permute-done.za_ref
  32.8 1.6 %collective-permute-done.1.zb_ref = f32[3,144,128]{2,1,0:T(8,128)S(1)} collective-permute-done((f32[3,144,128]{2,1,0:T(8,128)S(1)}, f32[3,144,128]{2,1,0:T(8,128)S(1)}, u32[]{:S(2)}, u32[]{:S(2)}) %collective-permute-start.1) | collective-permute-done | bytes 221216 | tf_op jit(solution)/shard_map/ppermute | solution.py:312
  34.4 1.2 %shard_map.69.s_ref = bf16[4,3,144,128]{3,2,1,0:T(8,128)(2,1)S(1)} custom-call(s32[2]{0:T(128)S(1)} %pad_add_fusion.odd_ref, f32[3,144,128]{2,1,0:T(8,128)S(1)} %shard_map.68.acc_ref, f32[144,54]{1,0:T(8,128)S(1)} %get-tuple-element.19.cols_ref, f32[3,144,128]{2,1,0:T(8,128)S(1)} %collective-permute-done.za_ref, ...), custom_call_target="tpu_custom_call" | custom-call | tf_op jit(solution)/shard_map/pallas_call | solution.py:249
  35.6 8.9 %all_to_all.20.refs_0_ = bf16[4,3,144,128]{3,2,1,0:T(8,128)(2,1)S(1)} all-to-all(bf16[4,3,144,128]{3,2,1,0:T(8,128)(2,1)S(1)} %shard_map.69.s_ref), channel_id=1, replica_groups=mesh['zh'=3,'zu'=2,'zd'=2,'yu'=2,'yd'=2,'x'=4,'yh'=2,'c'=2] {'x'}, dimensions={0} | all-to-all | bytes 884736 | tf_op jit(solution)/shard_map/all_to_all | solution.py:273
  44.5 2.3 %shard_map.70 = f32[4,4,32,128]{3,2,1,0:T(8,128)S(1)} custom-call(bf16[4,3,144,128]{3,2,1,0:T(8,128)(2,1)S(1)} %all_to_all.20.refs_0_, f32[16,576]{1,0:T(8,128)S(1)} %pad_maximum_fusion.refs_1_), custom_call_target="tpu_custom_call" | custom-call | tf_op jit(solution)/shard_map/pallas_call | solution.py:249
  46.8 11.1 %all_to_all.21 = f32[16,32,128]{2,1,0:T(8,128)S(1)} all-to-all(f32[16,32,128]{2,1,0:T(8,128)S(1)} %bitcast.23), channel_id=1, replica_groups=mesh['zh'=3,'zu'=2,'zd'=2,'yu'=2,'yd'=2,'x'=4,'yh'=2,'c'=2] {'zu','zd','..., dimensions={0} | all-to-all | bytes 524288 | tf_op jit(solution)/shard_map/all_to_all | solution.py:273
  57.8 8.9 %collective-permute-start.5 = (f32[32,128]{1,0:T(8,128)S(1)}, f32[32,128]{1,0:T(8,128)S(1)}, u32[]{:S(2)}, u32[]{:S(2)}) collective-permute-start(f32[32,128]{1,0:T(8,128)S(1)} %reduce_sum.9), channel_id=1, source_target_pairs={{256,0},{512,256},{0,512},{257,1},{513,257},{1,513},{258,2},{514,2... | collective-permute-start | bytes 49160 | tf_op jit(solution)/shard_map/ppermute | solution.py:348
  66.8 1.9 %collective-permute-start.4 = (f32[32,128]{1,0:T(8,128)S(1)}, f32[32,128]{1,0:T(8,128)S(1)}, u32[]{:S(2)}, u32[]{:S(2)}) collective-permute-start(f32[32,128]{1,0:T(8,128)S(1)} %reduce_sum.9), channel_id=1, source_target_pairs={{0,256},{256,512},{512,0},{1,257},{257,513},{513,1},{2,258},{258,5... | collective-permute-start | bytes 49160 | tf_op jit(solution)/shard_map/ppermute | solution.py:347
  68.7 0.0 collective-permute-done.5
  68.7 6.5 %collective-permute-done.4 = f32[32,128]{1,0:T(8,128)S(1)} collective-permute-done((f32[32,128]{1,0:T(8,128)S(1)}, f32[32,128]{1,0:T(8,128)S(1)}, u32[]{:S(2)}, u32[]{:S(2)}) %collective-permute-start.4) | collective-permute-done | bytes 16416 | tf_op jit(solution)/shard_map/ppermute | solution.py:347
  75.3 0.7 broadcast_in_dim.2
  75.9 12.2 %all-to-all-start.2 = ((bf16[16,32,128]{2,1,0:T(8,128)(2,1)}), bf16[16,32,128]{2,1,0:T(8,128)(2,1)S(1)}, u32[]{:S(2)}, u32[]{:S(2)}) async-start(bf16[16,32,128]{2,1,0:T(8,128)(2,1)} %broadcast_in_dim.2), calls=%async_computation.2 | async-start | bytes 262144 | tf_op jit(solution)/shard_map/all_to_all | solution.py:273
  88.1 0.8 shard_map.73
  88.9 0.0 copy-start
  88.9 1.6 %copy-done = bf16[1,4,2,4,4,64,64]{6,5,4,3,2,1,0:T(8,128)(2,1)S(1)} copy-done((bf16[1,4,2,4,4,64,64]{6,5,4,3,2,1,0:T(8,128)(2,1)S(1)}, bf16[1,4,2,4,4,64,64]{6,5,4,3,2,1,0:T(8,128)(2,1)}, u32[]{:S(2)}) %copy-start) | copy-done | bytes 1048600
  90.5 0.8 shard_map.71.b_ref
  91.4 7.6 %all-to-all-done.2 = bf16[16,32,128]{2,1,0:T(8,128)(2,1)S(1)} async-done(((bf16[16,32,128]{2,1,0:T(8,128)(2,1)}), bf16[16,32,128]{2,1,0:T(8,128)(2,1)S(1)}, u32[]{:S(2)}, u32[]{:S(2)}) %all-to-all-start.2) | async-done | bytes 131104 | tf_op jit(solution)/shard_map/all_to_all | solution.py:273
  99.0 1.7 %shard_map.72 = bf16[16,144,128]{2,1,0:T(8,128)(2,1)S(1)} custom-call(s32[1]{0:T(128)} %bitcast.tm_ref, bf16[4,4,32,128]{3,2,1,0:T(8,128)(2,1)S(1)} %bitcast.24, bf16[4,128,2048]{2,1,0:T(8,128)(2,1)S(1)} %shard_map.71.b_ref), custom_call_target="tpu_custom_call" | custom-call | tf_op jit(solution)/shard_map/pallas_call | solution.py:249
  100.6 14.6 %all_to_all.22.r_ref = bf16[16,144,128]{2,1,0:T(8,128)(2,1)S(1)} all-to-all(bf16[16,144,128]{2,1,0:T(8,128)(2,1)S(1)} %shard_map.72), channel_id=1, replica_groups=mesh['zh'=3,'zu'=2,'zd'=2,'yu'=2,'yd'=2,'x'=4,'yh'=2,'c'=2] {'zd','yd','x'}, dimensions={0} | all-to-all | bytes 1179648 | tf_op jit(solution)/shard_map/all_to_all | solution.py:273
  115.3 1.4 %shard_map.74 = (bf16[32,2,64,64]{3,2,1,0:T(8,128)(2,1)}, f32[2,4,32]{2,1,0:T(4,128)}) custom-call(bf16[16,144,128]{2,1,0:T(8,128)(2,1)S(1)} %all_to_all.22.r_ref), custom_call_target="tpu_custom_call" | custom-call | tf_op jit(solution)/shard_map/pallas_call | solution.py:249
  (5 shorter events, 0.1 us)
Async XLA Ops:
  3.1 29.7 %collective-permute-start.2 = (f32[3,24,128]{2,1,0:T(8,128)S(1)}, f32[3,24,128]{2,1,0:T(8,128)S(1)}, u32[]{:S(2)}, u32[]{:S(2)}) collective-permute-start(f32[3,24,128]{2,1,0:T(8,128)S(1)} %get-tuple-element.22), channel_id=1, source_target_pairs={{0,4},{4,0},{8,12},{12,8},{1,5},{5,1},{9,13},{13,9},{2,6},{6,2},{1... | collective-permute-start | bytes 110600 | tf_op jit(solution)/shard_map/ppermute | solution.py:313
  7.0 25.8 %collective-permute-start.3 = (f32[3,24,128]{2,1,0:T(8,128)S(1)}, f32[3,24,128]{2,1,0:T(8,128)S(1)}, u32[]{:S(2)}, u32[]{:S(2)}) collective-permute-start(f32[3,24,128]{2,1,0:T(8,128)S(1)} %get-tuple-element.23), channel_id=1, source_target_pairs={{0,12},{4,8},{8,4},{12,0},{1,13},{5,9},{9,5},{13,1},{2,14},{6,10},... | collective-permute-start | bytes 110600 | tf_op jit(solution)/shard_map/ppermute | solution.py:314
  10.7 22.1 %collective-permute-start = (f32[3,144,128]{2,1,0:T(8,128)S(1)}, f32[3,144,128]{2,1,0:T(8,128)S(1)}, u32[]{:S(2)}, u32[]{:S(2)}) collective-permute-start(f32[3,144,128]{2,1,0:T(8,128)S(1)} %get-tuple-element.20), channel_id=1, source_target_pairs={{0,16},{16,0},{32,48},{48,32},{64,80},{80,64},{96,112},{112,96},{1... | collective-permute-start | bytes 663560 | tf_op jit(solution)/shard_map/ppermute | solution.py:311
  13.9 20.5 %collective-permute-start.1 = (f32[3,144,128]{2,1,0:T(8,128)S(1)}, f32[3,144,128]{2,1,0:T(8,128)S(1)}, u32[]{:S(2)}, u32[]{:S(2)}) collective-permute-start(f32[3,144,128]{2,1,0:T(8,128)S(1)} %get-tuple-element.21), channel_id=1, source_target_pairs={{0,752},{16,32},{32,16},{48,64},{64,48},{80,96},{96,80},{112,128},... | collective-permute-start | bytes 663560 | tf_op jit(solution)/shard_map/ppermute | solution.py:312
  57.8 10.9 %collective-permute-start.5 = (f32[32,128]{1,0:T(8,128)S(1)}, f32[32,128]{1,0:T(8,128)S(1)}, u32[]{:S(2)}, u32[]{:S(2)}) collective-permute-start(f32[32,128]{1,0:T(8,128)S(1)} %reduce_sum.9), channel_id=1, source_target_pairs={{256,0},{512,256},{0,512},{257,1},{513,257},{1,513},{258,2},{514,2... | collective-permute-start | bytes 49160 | tf_op jit(solution)/shard_map/ppermute | solution.py:348
  66.8 8.5 %collective-permute-start.4 = (f32[32,128]{1,0:T(8,128)S(1)}, f32[32,128]{1,0:T(8,128)S(1)}, u32[]{:S(2)}, u32[]{:S(2)}) collective-permute-start(f32[32,128]{1,0:T(8,128)S(1)} %reduce_sum.9), channel_id=1, source_target_pairs={{0,256},{256,512},{512,0},{1,257},{257,513},{513,1},{2,258},{258,5... | collective-permute-start | bytes 49160 | tf_op jit(solution)/shard_map/ppermute | solution.py:347
  75.9 23.0 %all-to-all-start.2 = ((bf16[16,32,128]{2,1,0:T(8,128)(2,1)}), bf16[16,32,128]{2,1,0:T(8,128)(2,1)S(1)}, u32[]{:S(2)}, u32[]{:S(2)}) async-start(bf16[16,32,128]{2,1,0:T(8,128)(2,1)} %broadcast_in_dim.2), calls=%async_computation.2 | async-start | bytes 262144 | tf_op jit(solution)/shard_map/all_to_all | solution.py:273
  88.9 1.6 %copy-start = (bf16[1,4,2,4,4,64,64]{6,5,4,3,2,1,0:T(8,128)(2,1)S(1)}, bf16[1,4,2,4,4,64,64]{6,5,4,3,2,1,0:T(8,128)(2,1)}, u32[]{:S(2)}) copy-start(bf16[1,4,2,4,4,64,64]{6,5,4,3,2,1,0:T(8,128)(2,1)} %param.6) | copy-start | bytes 3145732
